TPU v7x, 32 devices: a whole 2x2x4 slice. The times are simulated.
32 devices in a mesh: path: 2 (over x), trade: 16 (over z, y, core).
Axes of the slice: x: 2, y: 2, z: 4, core: 2. Of those that a mesh axis runs over, the one named last changes fastest.
Arguments:
- factor_paths: bfloat16 [2048, 2, 128], P('trade', None, 'path'), may hold values from -6 to 6
- tenor_basis: bfloat16 [32, 16], replicated, may hold values from -1 to 1
- trade_blocks: int32 [2, 24576], P(None, 'trade'), may hold values from 0 to 63
- trade_set: int32 [24576], P('trade'), may hold values from 0 to 255
- trade_type: int32 [24576], P('trade'), may hold values from 0 to 1
- notional: float32 [24576], P('trade'), may hold values from -3 to 3
- strike: float32 [24576], P('trade'), may hold values from -2 to 2
- vol_level: float32 [24576], P('trade'), may hold values from 0.1 to 0.5
- cash_weights: float32 [16, 24576], P(None, 'trade'), may hold values from 0.02 to 0.12
- set_threshold: float32 [256], P('trade'), may hold values from 0.2 to 2
- date_weight: float32 [256, 2], P('trade'), may hold values from 0.2 to 1
Outputs:
- netting_cva: float32 [256], P('trade')
- factor_cotangent: float32 [2048, 2, 128], P('trade', None, 'path')
All inputs are finite; a program needn't handle non-finite values.
Results may differ from a plain program's by a relative error of at most 0.0091.
Values may be sent and summed in bfloat16 or wider, within the bound.
No kernel may reach another device: no remote copies, remote signals or barrier semaphores. Data moves between devices by JAX's collectives and lax.ppermute only.
A program may use at most 64 MiB of HBM per device.

v0:
```python
import jax
import jax.numpy as jnp
from jax import lax
from jax.sharding import PartitionSpec as P


def price(curves, fwd_block, disc_block, weights, notional, strike, vol_level, trade_kind):
    fwd_curve = jnp.take(curves, fwd_block, axis=0).astype(jnp.float32)
    discount = jnp.exp(-0.5 * jnp.take(curves, disc_block, axis=0).astype(jnp.float32))
    spread = jnp.transpose(weights)[:, :, None]
    forward = jnp.sum(spread * fwd_curve, axis=1)
    annuity = jnp.sum(spread * discount, axis=1)
    moneyness = forward - strike[:, None]
    scaled = moneyness / vol_level[:, None]
    option = trade_kind[:, None] == 1
    payoff = jnp.where(option, vol_level[:, None] * jax.nn.softplus(scaled), moneyness)
    trade_value = notional[:, None] * annuity * payoff
    return (trade_value, (discount, spread, annuity, payoff, scaled, option))


def adjoint_terms(saved_state, cotangent, notional):
    discount, spread, annuity, payoff, scaled, option = saved_state
    forward_cot = (
        cotangent * notional[:, None] * annuity * jnp.where(option, jax.nn.sigmoid(scaled), 1.0)
    )
    annuity_cot = cotangent * notional[:, None] * payoff
    from_forward = spread * forward_cot[:, None, :]
    from_discount = -0.5 * spread * discount * annuity_cot[:, None, :]
    return (from_forward, from_discount)


def shards(
    factor_paths,
    tenor_basis,
    trade_blocks,
    trade_set,
    trade_type,
    notional,
    strike,
    vol_level,
    cash_weights,
    set_threshold,
    date_weight,
):
    factor_rows, date_count, local_paths = factor_paths.shape
    block_size, tenor_count = tenor_basis.shape
    row_count = date_count * local_paths
    traders = lax.axis_size("trade")
    all_factors = factor_rows * traders
    block_count = all_factors // block_size
    local_sets = set_threshold.shape[0]
    local_trades = trade_set.shape[0]
    group_size = 128
    group_count = local_trades // group_size
    basis_wide = tenor_basis.astype(jnp.float32)
    factor_stack = factor_paths.reshape(factor_rows, row_count)
    pieces = factor_stack.reshape(factor_stack.shape[0] // block_size, block_size, row_count)
    own_curves = jnp.einsum(
        "jm,bjr->bmr", tenor_basis, pieces, preferred_element_type=jnp.float32
    ).astype(jnp.bfloat16)
    curves = lax.all_gather(own_curves, "trade", axis=0, tiled=True)
    trade_items = (
        trade_blocks[0].reshape(group_count, group_size),
        trade_blocks[1].reshape(group_count, group_size),
        trade_type.reshape(group_count, group_size),
        notional.reshape(group_count, group_size),
        strike.reshape(group_count, group_size),
        vol_level.reshape(group_count, group_size),
        jnp.transpose(cash_weights.reshape(tenor_count, group_count, group_size), (1, 0, 2)),
    )

    def forward_group(trade_item):
        fwd_block, disc_block, trade_kind, notional_part, strike_part, vol_part, weights = (
            trade_item
        )
        trade_value, saved_state = price(
            curves, fwd_block, disc_block, weights, notional_part, strike_part, vol_part, trade_kind
        )
        return trade_value.astype(jnp.bfloat16)

    values = lax.map(forward_group, trade_items).reshape(local_trades, row_count)
    labels = jnp.arange(lax.axis_size("trade") * local_sets, dtype=jnp.int32)
    onehot = (labels[:, None] == trade_set[None, :]).astype(jnp.bfloat16)
    set_value = lax.psum_scatter(
        jnp.dot(onehot, values, preferred_element_type=jnp.float32),
        "trade",
        scatter_dimension=0,
        tiled=True,
    )
    excess = set_value - set_threshold[:, None]
    exposure = jax.nn.softplus(excess).reshape(local_sets, date_count, local_paths)
    path_total = lax.psum(jnp.sum(exposure, axis=2), "path")
    all_paths = local_paths * lax.axis_size("path")
    netting_cva = jnp.sum(date_weight * path_total, axis=1) / all_paths
    set_cot = (
        (
            date_weight[:, :, None]
            * jax.nn.sigmoid(excess).reshape(local_sets, date_count, local_paths)
        )
        .reshape(local_sets, row_count)
        .astype(jnp.bfloat16)
    )
    shard_piece = lax.all_gather(set_cot, "trade", axis=0, tiled=True)
    labels = jnp.arange(shard_piece.shape[0], dtype=jnp.int32)
    onehot = (trade_set[:, None] == labels[None, :]).astype(jnp.bfloat16)
    trade_cot = jnp.dot(onehot, shard_piece, preferred_element_type=jnp.float32)
    block_ids = jnp.arange(block_count, dtype=jnp.int32)

    def backward_group(running, trade_item):
        (
            fwd_block,
            disc_block,
            trade_kind,
            notional_part,
            strike_part,
            vol_part,
            weights,
            cotangent,
        ) = trade_item
        trade_value, saved_state = price(
            curves, fwd_block, disc_block, weights, notional_part, strike_part, vol_part, trade_kind
        )
        from_forward, from_discount = adjoint_terms(saved_state, cotangent, notional_part)
        onehot = jnp.concatenate(
            [block_ids[:, None] == fwd_block[None, :], block_ids[:, None] == disc_block[None, :]],
            axis=1,
        ).astype(jnp.bfloat16)
        term_stack = jnp.concatenate([from_forward, from_discount], axis=0).reshape(
            2 * group_size, tenor_count * row_count
        )
        high_part = lax.optimization_barrier(term_stack.astype(jnp.bfloat16))
        low_part = (term_stack - high_part.astype(jnp.float32)).astype(jnp.bfloat16)
        added = jnp.dot(onehot, high_part, preferred_element_type=jnp.float32) + jnp.dot(
            onehot, low_part, preferred_element_type=jnp.float32
        )
        return (running + added.reshape(block_count, tenor_count, row_count), None)

    curve_cot, _ = lax.scan(
        backward_group,
        jnp.zeros((block_count, tenor_count, row_count), jnp.float32),
        trade_items + (trade_cot.reshape(group_count, group_size, row_count),),
    )
    own_cot = lax.psum_scatter(curve_cot, "trade", scatter_dimension=0, tiled=True)
    factor_cot = jnp.einsum(
        "jm,bmr->bjr", basis_wide, own_cot, precision=lax.Precision.HIGHEST
    ).reshape(factor_rows, row_count)
    return (netting_cva, factor_cot.reshape(factor_rows, date_count, local_paths))


def solution(mesh):
    return jax.shard_map(
        shards,
        mesh=mesh,
        in_specs=(
            P("trade", None, "path"),
            P(),
            P(None, "trade"),
            P("trade"),
            P("trade"),
            P("trade"),
            P("trade"),
            P("trade"),
            P(None, "trade"),
            P("trade"),
            P("trade", None),
        ),
        out_specs=(P("trade"), P("trade", None, "path")),
        check_vma=False,
    )
```

profile of v0, /device:TPU:0, one launch (start us, length us, event | category | flops | bytes accessed | tf_op | source)
XLA Modules:
  0.0 332.4 jit_solution(18374408877770693666)
XLA Ops:
  10.1 23.8 %all_gather.6 = bf16[64,16,128]{2,1,0:T(8,128)(2,1)S(1)} all-gather(bf16[4,16,128]{2,1,0:T(8,128)(2,1)S(1)} %fusion.28), channel_id=1, replica_groups=mesh['path'=2,'trade'=16] {'trade'}, dimensions={0}, use_global_device_ids=true | all-gather | bytes 278528 | tf_op jit(solution)/shard_map/all_gather | solution.py:61
  33.9 58.0 %while.22 = (s32[]{:T(128)}, bf16[12,128,128]{2,1,0:T(8,128)(2,1)S(1)}, f32[12,128]{1,0:T(8,128)}, f32[12,16,128]{2,1,0:T(8,128)S(1)}, s32[12,128]{1,0:T(8,128)S...) while((s32[]{:T(128)}, ...), condition=%wide.region_3.5_spmd, body=%wide.region_0.4_spmd.sunk | while | flops 2543234 | bytes 3500301 | solution.py:81
  37.7 1.0 multiply_reduce_fusion.7
  42.5 1.0 multiply_reduce_fusion.7
  92.0 1.0 fusion.26
  93.3 52.8 %reduce-scatter.3.cloned.1.call-done = f32[16,128]{1,0:T(8,128)} async-done(((f32[256,128]{1,0:T(8,128)}), f32[16,128]{1,0:T(8,128)}) %reduce-scatter.3.cloned.1.call-update) | async-done | bytes 8208 | tf_op jit(solution)/shard_map/reduce_scatter | solution.py:84
  146.9 19.6 %all_gather.7 = bf16[256,128]{1,0:T(8,128)(2,1)S(1)} all-gather(bf16[16,128]{1,0:T(8,128)(2,1)S(1)} %get-tuple-element.304), channel_id=1, replica_groups=mesh['path'=2,'trade'=16] {'trade'}, dimensions={0}, use_global_device_ids=true | all-gather | bytes 69632 | tf_op jit(solution)/shard_map/all_gather | solution.py:103
  166.5 1.0 fusion.27
  167.4 101.9 %while.23 = (s32[]{:T(128)}, f32[64,16,128]{2,1,0:T(8,128)S(1)}, s32[12,128]{1,0:T(8,128)S(1)}, s32[12,128]{1,0:T(8,128)S(1)}, f32[12,16,128]{2,1,0:T(8,128)S(1)...) while((s32[]{:T(128)}, f32[64,16,128]{2,1,0:T(8,128)S(1)}, ...), condition=%wide.region_11.13_spmd.clone.clone, body=%wide.region_8.12_spmd.clone.clone.sunk | while | flops 140958080 | bytes 22238244 | solution.py:138
  171.3 1.0 multiply_reduce_fusion.8
  179.8 1.0 multiply_reduce_fusion.8
  188.3 1.0 multiply_reduce_fusion.8
  196.8 1.0 multiply_reduce_fusion.8
  205.3 1.0 multiply_reduce_fusion.8
  213.7 1.0 multiply_reduce_fusion.8
  222.2 1.0 multiply_reduce_fusion.8
  230.7 1.0 multiply_reduce_fusion.8
  239.2 1.0 multiply_reduce_fusion.8
  247.7 1.0 multiply_reduce_fusion.8
  256.2 1.0 multiply_reduce_fusion.8
  264.7 1.0 multiply_reduce_fusion.8
  270.3 5.0 %psum.7 = f32[16,2]{1,0:T(8,128)S(1)} all-reduce(f32[16,2]{1,0:T(8,128)S(1)} %reduce_sum.58), channel_id=1, replica_groups=mesh['path'=2,'trade'=16] {'path'}, use_global_device_ids=true, to_apply=%region_6.8 | all-reduce | flops 32 | bytes 256 | tf_op jit(solution)/shard_map/psum | solution.py:92
  275.9 47.8 %reduce-scatter.5.cloned.1.call-done = f32[4,16,128]{2,1,0:T(8,128)} async-done(((f32[64,16,128]{2,1,0:T(8,128)}), f32[4,16,128]{2,1,0:T(8,128)}) %reduce-scatter.5.cloned.1.call-update) | async-done | bytes 32784 | tf_op jit(solution)/shard_map/reduce_scatter | solution.py:143
  323.7 1.0 convolution_bitcast_fusion
  (462 shorter events, 150.2 us)
Async XLA Ops:
  7.2 2.8 copy-start
  7.2 138.9 %reduce-scatter.3.cloned.1.call-start = ((), (), s32[]{:S(2)}) async-start(), calls=%async_computation.2 | async-start | bytes 139264 | tf_op jit(solution)/shard_map/reduce_scatter | solution.py:84
  33.9 58.0 %copy-start.2 = (s32[1536]{0:T(1024)S(1)}, s32[1536]{0:T(1024)}, u32[]{:S(2)}) copy-start(s32[1536]{0:T(1024)} %param.20) | copy-start | bytes 18436
  33.9 59.1 %copy-start.3 = (f32[16,2]{0,1:T(2,128)S(1)}, f32[16,2]{0,1:T(2,128)}, u32[]{:S(2)}) copy-start(f32[16,2]{0,1:T(2,128)} %param.27) | copy-start | bytes 388
  33.9 112.1 %copy-start.4 = (f32[16]{0:T(128)S(1)}, f32[16]{0:T(128)}, u32[]{:S(2)}) copy-start(f32[16]{0:T(128)} %param.26) | copy-start | bytes 196
  93.0 230.7 %reduce-scatter.5.cloned.1.call-start = ((), (), s32[]{:S(2)}) async-start(), calls=%async_computation.3 | async-start | bytes 557056 | tf_op jit(solution)/shard_map/reduce_scatter | solution.py:143
  269.3 0.8 copy-start.1
Sparse Core Ops, SparseCore 0:
  93.1 52.9 reduce-scatter.2
  270.2 53.4 reduce-scatter.4
where the time goes:
time: 336 us; the launch traced here: 332 us
  waiting for transfers between devices  101 us (30%)
  local copies, waits for them, and re-layouts  88 us (26%)
  other arithmetic  62.2 us (19%)
  blocking collectives  48.4 us (14%)
  matrix products  16.4 us (5%)
  between operations  14.2 us (4%)
    reduce_scatter x1, waiting for transfers between devices, shards(): lax.psum_scatter(jnp.dot(onehot, values, preferred_element_type=jnp.float...  52.8 us
    reduce_scatter x1, waiting for transfers between devices, shards(): lax.psum_scatter(curve_cot, 'trade', scatter_dimension=0, tiled=True)  47.8 us
    all_gather x1, blocking collectives, shards(): curves = lax.all_gather(own_curves, 'trade', axis=0, tiled=True)  23.8 us
    reduce_sum x24, other arithmetic, price(): annuity = jnp.sum(spread * discount, axis=1)  23.3 us
    all_gather x1, blocking collectives, shards(): shard_piece = lax.all_gather(set_cot, 'trade', axis=0, tiled=True)  19.6 us
    gather x24, local copies, waits for them, and re-layouts, price(): jnp.take(curves, disc_block, axis=0).astype(jnp.float32)  16.9 us
    gather x24, local copies, waits for them, and re-layouts, price(): fwd_curve = jnp.take(curves, fwd_block, axis=0).astype(jnp.float32)  16.9 us
    dynamic_slice x24, local copies, waits for them, and re-layouts, shards(): lax.map(forward_group, trade_items).reshape(local_trades, row_count)  16.9 us
  transfers between devices with their start and end apart: 2, of which 2 were waited for; matrix products, arithmetic and copies ran while one was open for 0% of the time, Pallas kernels for 0%

commit v1 on v0

v1 whole, which is shorter than its diff:
```python
import functools

import jax
import jax.numpy as jnp
from jax import lax
from jax.experimental import pallas as pl
from jax.experimental.pallas import tpu as pltpu
from jax.sharding import PartitionSpec as P

F32 = jnp.float32
BF16 = jnp.bfloat16
NT = (((1,), (1,)), ((), ()))
TN = (((0,), (0,)), ((), ()))
TILE = 512


def log1p_unit(e):
    return jnp.where(e < 1e-4, (1.0 - 0.5 * e) * e, jnp.log(1.0 + e))


def fill_weighted_onehot(out, ids, weights, blocks):
    tenors = weights.shape[0]
    ids = jnp.broadcast_to(ids, weights.shape)
    zero = jnp.zeros_like(weights)
    for b in range(blocks):
        out[b * tenors : (b + 1) * tenors, :] = jnp.where(ids == b, weights, zero).astype(BF16)


def fill_onehot(out, ids):
    sets, trades = out.shape
    step = 16
    row = lax.broadcasted_iota(jnp.int32, (step, trades), 0)
    ids = jnp.broadcast_to(ids, (step, trades))
    for n in range(0, sets, step):
        out[n : n + step, :] = jnp.where(ids == row + n, 1.0, 0.0).astype(BF16)


def forward_kernel(
    curves, blocks_ref, set_ref, kind_ref, notional_ref, strike_ref, vol_ref, weights_ref,
    sets_out, fwd_scale, ann_scale, w_fwd, w_disc, onehot,
):
    i = pl.program_id(0)
    rows = curves.shape[1]
    tile = weights_ref.shape[1]
    tenors = weights_ref.shape[0]
    blocks = curves.shape[0] // tenors
    weights = weights_ref[...]
    fill_weighted_onehot(w_fwd, blocks_ref[0:1, :], weights, blocks)
    fill_weighted_onehot(w_disc, blocks_ref[1:2, :], weights, blocks)
    fill_onehot(onehot, set_ref[...])
    curve = curves[...]
    discount = jnp.exp(-0.5 * curve.astype(F32)).astype(BF16)
    forward = lax.dot_general(curve, w_fwd[...], TN, preferred_element_type=F32)
    annuity = lax.dot_general(discount, w_disc[...], TN, preferred_element_type=F32)
    vol = vol_ref[...]
    notional = notional_ref[...]
    option = jnp.broadcast_to(kind_ref[...] == 1, (rows, tile))
    moneyness = forward - strike_ref[...]
    scaled = moneyness * (1.0 / vol)
    e = jnp.exp(-jnp.abs(scaled))
    softplus = jnp.maximum(scaled, 0.0) + log1p_unit(e)
    sigmoid = jnp.where(scaled >= 0.0, 1.0, e) / (1.0 + e)
    payoff = jnp.where(option, vol * softplus, moneyness)
    slope = jnp.where(option, sigmoid, 1.0)
    scaled_annuity = notional * annuity
    value = (scaled_annuity * payoff).astype(BF16)
    fwd_scale[...] = scaled_annuity * slope
    ann_scale[...] = notional * payoff
    added = lax.dot_general(onehot[...], value, NT, preferred_element_type=F32)

    @pl.when(i == 0)
    def _():
        sets_out[...] = added

    @pl.when(i > 0)
    def _():
        sets_out[...] += added


def backward_kernel(
    curves, cots, fwd_scale, ann_scale, w_fwd, w_disc, onehot, out, from_fwd, from_disc
):
    i = pl.program_id(0)
    trade_cot = lax.dot_general(cots[...], onehot[...], TN, preferred_element_type=F32)
    fwd_cot = (trade_cot * fwd_scale[...]).astype(BF16)
    ann_cot = (trade_cot * ann_scale[...]).astype(BF16)
    a = lax.dot_general(w_fwd[...], fwd_cot, NT, preferred_element_type=F32)
    b = lax.dot_general(w_disc[...], ann_cot, NT, preferred_element_type=F32)

    @pl.when(i == 0)
    def _():
        from_fwd[...] = a
        from_disc[...] = b

    @pl.when(i > 0)
    def _():
        from_fwd[...] += a
        from_disc[...] += b

    @pl.when(i == pl.num_programs(0) - 1)
    def _():
        discount = jnp.exp(-0.5 * curves[...].astype(F32))
        out[...] = (from_fwd[...] - 0.5 * discount * from_disc[...]).astype(out.dtype)


def whole(shape):
    return pl.BlockSpec(shape, lambda i: (0,) * len(shape))


def column(height, tile):
    return pl.BlockSpec((height, tile), lambda i: (0, i))


def gather_parts(x, axis):
    n = lax.axis_size(axis)
    return lax.all_to_all(jnp.broadcast_to(x[None], (n,) + x.shape), axis, 0, 0)


def scatter_sum(x, axis):
    n = lax.axis_size(axis)
    parts = x.reshape((n, x.shape[0] // n) + x.shape[1:])
    return jnp.sum(lax.all_to_all(parts, axis, 0, 0).astype(F32), axis=0)


def sum_over(x, axis):
    n = lax.axis_size(axis)
    total = x
    for shift in range(1, n):
        total = total + lax.ppermute(x, axis, [(i, (i + shift) % n) for i in range(n)])
    return total


def shards(
    factor_paths, tenor_basis, trade_blocks, trade_set, trade_type, notional, strike,
    vol_level, cash_weights, set_threshold, date_weight,
):
    factor_rows, dates, paths = factor_paths.shape
    block_size, tenors = tenor_basis.shape
    rows = dates * paths
    traders = lax.axis_size("trade")
    blocks = factor_rows * traders // block_size
    local_sets = set_threshold.shape[0]
    sets = local_sets * traders
    trades = trade_set.shape[0]
    tile = TILE if trades % TILE == 0 else trades
    grid = (trades // tile,)

    pieces = factor_paths.reshape(factor_rows // block_size, block_size, rows)
    own_curves = jnp.einsum(
        "jm,bjr->bmr", tenor_basis, pieces, preferred_element_type=F32
    ).astype(BF16)
    curves = gather_parts(own_curves.reshape(-1, rows), "trade").reshape(blocks * tenors, rows)

    params = pltpu.CompilerParams(dimension_semantics=("arbitrary",))
    height = blocks * tenors
    partial, fwd_scale, ann_scale, w_fwd, w_disc, onehot = pl.pallas_call(
        forward_kernel,
        grid=grid,
        in_specs=[whole((height, rows)), column(2, tile)]
        + [column(1, tile)] * 5 + [column(tenors, tile)],
        out_specs=[whole((sets, rows)), column(rows, tile), column(rows, tile),
                   column(height, tile), column(height, tile), column(sets, tile)],
        out_shape=[
            jax.ShapeDtypeStruct((sets, rows), F32),
            jax.ShapeDtypeStruct((rows, trades), F32),
            jax.ShapeDtypeStruct((rows, trades), F32),
            jax.ShapeDtypeStruct((height, trades), BF16),
            jax.ShapeDtypeStruct((height, trades), BF16),
            jax.ShapeDtypeStruct((sets, trades), BF16),
        ],
        compiler_params=params,
        name="price",
    )(
        curves, trade_blocks, trade_set[None], trade_type[None], notional[None],
        strike[None], vol_level[None], cash_weights,
    )

    set_value = scatter_sum(partial, "trade")
    excess = set_value - set_threshold[:, None]
    exposure = jax.nn.softplus(excess).reshape(local_sets, dates, paths)
    path_total = sum_over(jnp.sum(exposure, axis=2), "path")
    netting_cva = jnp.sum(date_weight * path_total, axis=1) / (paths * lax.axis_size("path"))
    set_cot = (jnp.repeat(date_weight, paths, axis=1) * jax.nn.sigmoid(excess)).astype(BF16)
    cots = gather_parts(set_cot, "trade").reshape(sets, rows)

    curve_cot = pl.pallas_call(
        backward_kernel,
        grid=grid,
        in_specs=[whole((height, rows)), whole((sets, rows)), column(rows, tile),
                  column(rows, tile), column(height, tile), column(height, tile),
                  column(sets, tile)],
        out_specs=whole((height, rows)),
        out_shape=jax.ShapeDtypeStruct((height, rows), BF16),
        scratch_shapes=[pltpu.VMEM((height, rows), F32)] * 2,
        compiler_params=params,
        name="adjoint",
    )(curves, cots, fwd_scale, ann_scale, w_fwd, w_disc, onehot)

    own_cot = scatter_sum(curve_cot, "trade").reshape(-1, tenors, rows)
    factor_cot = jnp.einsum(
        "jm,bmr->bjr", tenor_basis.astype(F32), own_cot, precision=lax.Precision.HIGHEST
    )
    return netting_cva, factor_cot.reshape(factor_rows, dates, paths)


def solution(mesh):
    return jax.shard_map(
        shards,
        mesh=mesh,
        in_specs=(
            P("trade", None, "path"), P(), P(None, "trade"), P("trade"), P("trade"),
            P("trade"), P("trade"), P("trade"), P(None, "trade"), P("trade"),
            P("trade", None),
        ),
        out_specs=(P("trade"), P("trade", None, "path")),
        check_vma=False,
    )
```

time: 336 us -> 71.5 us (0.21)
  waiting for transfers between devices: 101 us -> 18 us
  local copies, waits for them, and re-layouts: 88 us -> 10.8 us
  other arithmetic: 62.2 us -> 1.62 us
  blocking collectives: 48.4 us -> 10.2 us
  matrix products: 16.4 us -> 0.34 us
  starting transfers between devices: 0.08 us -> 16 us
  between operations: 14.2 us -> 0.72 us
  Pallas kernels: 0 us -> 13.1 us
    reduce_scatter x2 -> x0, waiting for transfers between devices: 101 us -> none  [the longest x1 52.8 us: shards(): lax.psum_scatter(jnp.dot(onehot, values, preferred_element_type=jnp.float...]
    all_gather x2 -> x0, blocking collectives: 43.4 us -> none  [the longest x1 23.8 us: shards(): curves = lax.all_gather(own_curves, 'trade', axis=0, tiled=True)]
    gather x48 -> x0, local copies, waits for them, and re-layouts: 33.8 us -> none  [the longest x24 16.9 us: price(): jnp.take(curves, disc_block, axis=0).astype(jnp.float32)]
    reduce_sum x26 -> x4, other arithmetic: 23.5 us -> 0.36 us  [the longest x1 0.19 us: shards(): path_total = sum_over(jnp.sum(exposure, axis=2), 'path')]
    eq x48 -> x0, other arithmetic: 16.9 us -> none  [the longest x24 16.7 us: price(): option = trade_kind[:, None] == 1]
    dynamic_slice x24 -> x0, local copies, waits for them, and re-layouts: 16.9 us -> none  [shards(): lax.map(forward_group, trade_items).reshape(local_trades, row_count)]
    dot_general x28 -> x2, matrix products: 16.4 us -> 0.34 us  [the longest x1 0.22 us: shards(): jnp.einsum('jm,bmr->bjr', tenor_basis.astype(F32), own_cot, precision=lax...]
    all_to_all x0 -> x3, waiting for transfers between devices: none -> 15.8 us  [the longest x2 12.3 us: scatter_sum(): return jnp.sum(lax.all_to_all(parts, axis, 0, 0).astype(F32), axis=0)]
  transfers between devices with their start and end apart: 2 -> 4, of which waited for: 2 -> 4; matrix products, arithmetic and copies ran while one was open for 0% -> 12% of each run, Pallas kernels for 0% -> 0%
where the time goes in v1:
time: 71.5 us; the launch traced here: 70.7 us
  waiting for transfers between devices  18 us (25%)
  starting transfers between devices  16 us (22%)
  Pallas kernels  13.1 us (18%)
  local copies, waits for them, and re-layouts  10.8 us (15%)
  blocking collectives  10.2 us (14%)
  other arithmetic  1.62 us (2%)
  between operations  0.72 us (1%)
    all_to_all x2, waiting for transfers between devices, scatter_sum(): return jnp.sum(lax.all_to_all(parts, axis, 0, 0).astype(F32), axis=0)  12.3 us
    all_to_all x1, blocking collectives, gather_parts(): return lax.all_to_all(jnp.broadcast_to(x[None], (n,) + x.shape), axis, 0, 0)  10.2 us
    all_to_all x1, starting transfers between devices, gather_parts(): return lax.all_to_all(jnp.broadcast_to(x[None], (n,) + x.shape), axis, 0, 0)  7.41 us
    all_to_all x2, starting transfers between devices, scatter_sum(): return jnp.sum(lax.all_to_all(parts, axis, 0, 0).astype(F32), axis=0)  7.05 us
    pallas_call x1, Pallas kernels, shards(): pl.pallas_call(backward_kernel, grid=grid, in_specs=[whole((height, rows)...  6.84 us
    pallas_call x1, Pallas kernels, shards(): pl.pallas_call(forward_kernel, grid=grid, in_specs=[whole((height, rows))...  6.25 us
    all_to_all x1, waiting for transfers between devices, gather_parts(): return lax.all_to_all(jnp.broadcast_to(x[None], (n,) + x.shape), axis, 0, 0)  3.54 us
    unnamed x9, local copies, waits for them, and re-layouts  3.07 us
  transfers between devices with their start and end apart: 4, of which 4 were waited for; matrix products, arithmetic and copies ran while one was open for 12% of the time, Pallas kernels for 0%

profile of v1, /device:TPU:0, one launch (start us, length us, event | category | flops | bytes accessed | tf_op | source)
XLA Modules:
  0.0 70.7 jit_solution(687115451077560255)
XLA Ops:
  0.6 0.9 %copy.19 = bf16[128,2,64]{2,1,0:T(2,128)(2,1)S(1)} copy(bf16[128,2,64]{0,2,1:T(8,128)(2,1)} %param.11) | data formatting | bytes 65536 | tf_op args[0]
  1.8 0.7 %broadcast_in_dim.33 = bf16[16,64,128]{2,1,0:T(8,128)(2,1)} broadcast(bf16[64,128]{1,0:T(8,128)(2,1)S(1)} %bitcast.23), dimensions={1,2} | broadcast | bytes 278528 | tf_op jit(solution)/shard_map/broadcast_in_dim | solution.py:116
  2.5 7.4 %all-to-all-start = ((bf16[16,64,128]{2,1,0:T(8,128)(2,1)}), bf16[16,64,128]{2,1,0:T(8,128)(2,1)S(1)}, u32[]{:S(2)}, u32[]{:S(2)}) async-start(bf16[16,64,128]{2,1,0:T(8,128)(2,1)} %broadcast_in_dim.33), calls=%async_computation | async-start | bytes 524288 | tf_op jit(solution)/shard_map/all_to_all | solution.py:116
  9.9 1.3 %broadcast_in_dim.34.set_ref = s32[1,1536]{1,0:T(1,128)} reshape(s32[1536]{0:T(1024)} %param.14) | data formatting | bytes 12288 | tf_op jit(solution)/shard_map/broadcast_in_dim | solution.py:174
  11.2 1.3 %broadcast_in_dim.35.kind_ref = s32[1,1536]{1,0:T(1,128)} reshape(s32[1536]{0:T(1024)} %param.15) | data formatting | bytes 12288 | tf_op jit(solution)/shard_map/broadcast_in_dim | solution.py:174
  12.5 1.3 %broadcast_in_dim.36.notional_ref = f32[1,1536]{1,0:T(1,128)} reshape(f32[1536]{0:T(1024)} %param.16) | data formatting | bytes 12288 | tf_op jit(solution)/shard_map/broadcast_in_dim | solution.py:174
  13.8 1.3 %broadcast_in_dim.37.strike_ref = f32[1,1536]{1,0:T(1,128)} reshape(f32[1536]{0:T(1024)} %param.17) | data formatting | bytes 12288 | tf_op jit(solution)/shard_map/broadcast_in_dim | solution.py:175
  15.1 1.3 %broadcast_in_dim.38.vol_ref = f32[1,1536]{1,0:T(1,128)} reshape(f32[1536]{0:T(1024)} %param.18) | data formatting | bytes 12288 | tf_op jit(solution)/shard_map/broadcast_in_dim | solution.py:175
  16.4 3.5 %all-to-all-done = bf16[16,64,128]{2,1,0:T(8,128)(2,1)S(1)} async-done(((bf16[16,64,128]{2,1,0:T(8,128)(2,1)}), bf16[16,64,128]{2,1,0:T(8,128)(2,1)S(1)}, u32[]{:S(2)}, u32[]{:S(2)}) %all-to-all-start) | async-done | bytes 262176 | tf_op jit(solution)/shard_map/all_to_all | solution.py:116
  19.9 0.7 copy-done.1
  20.6 6.2 %price.1 = (f32[256,128]{1,0:T(8,128)}, f32[128,1536]{1,0:T(8,128)}, f32[128,1536]{1,0:T(8,128)}, bf16[1024,1536]{1,0:T(8,128)(2,1)}, bf16[1024,1536]{1,0:T(8,128)(2,1)}, /*index=5*/bf16[256,1536]{1,0:T(8,128)(2,1)}) custom-call(bf16[1024,128]{1,0:T(8,128)(2,1)} %bitcast.17, s32[2,1536]{1,0:T(2,128)} %blocks_ref.1, s32[1,1536]{1,0:T(1,128)} %broadcast_in_dim.34.set_ref, ...), custom_call_target="tpu_custom_call" | custom-call | tf_op jit(solution)/shard_map/price/pallas_call | solution.py:156
  26.9 3.5 %all-to-all-start.1 = ((f32[16,16,128]{2,1,0:T(8,128)}), f32[16,16,128]{2,1,0:T(8,128)S(1)}, u32[]{:S(2)}, u32[]{:S(2)}) async-start(f32[16,16,128]{2,1,0:T(8,128)} %bitcast.22), calls=%async_computation.1 | async-start | bytes 262144 | tf_op jit(solution)/shard_map/all_to_all | solution.py:122
  30.4 0.8 %copy.20 = f32[16,2]{1,0:T(8,128)S(1)} copy(f32[16,2]{0,1:T(2,128)} %param.21) | data formatting | bytes 256 | tf_op args[10]
  31.3 7.0 %all-to-all-done.1 = f32[16,16,128]{2,1,0:T(8,128)S(1)} async-done(((f32[16,16,128]{2,1,0:T(8,128)}), f32[16,16,128]{2,1,0:T(8,128)S(1)}, u32[]{:S(2)}, u32[]{:S(2)}) %all-to-all-start.1) | async-done | bytes 131104 | tf_op jit(solution)/shard_map/all_to_all | solution.py:122
  38.3 0.7 %multiply_convert_fusion = bf16[16,128]{1,0:T(8,128)(2,1)S(1)} fusion(f32[16,128]{1,0:T(8,128)S(1)} %reshape.62, f32[16,128]{1,0:T(8,128)S(1)} %reduce_sum.38, f32[16]{0:T(128)} %param.20), kind=kLoop, calls=%fused_computation.5 | loop fusion | flops 12288 | bytes 20544 | tf_op jit(solution)/shard_map/convert_element_type | solution.py:183
  39.1 10.2 %all_to_all.20 = bf16[16,16,128]{2,1,0:T(8,128)(2,1)} all-to-all(bf16[16,16,128]{2,1,0:T(8,128)(2,1)S(1)} %broadcast_in_dim.40), channel_id=1, replica_groups=mesh['path'=2,'trade'=16] {'trade'}, dimensions={0} | all-to-all | bytes 131072 | tf_op jit(solution)/shard_map/all_to_all | solution.py:116
  49.2 6.8 %adjoint.1 = bf16[1024,128]{1,0:T(8,128)(2,1)} custom-call(bf16[1024,128]{1,0:T(8,128)(2,1)} %bitcast.18, bf16[256,128]{1,0:T(8,128)(2,1)} %bitcast.20, f32[128,1536]{1,0:T(8,128)} %get-tuple-element.9.fwd_scale, f32[128,1536]{1,0:T(8,128)} %get-tuple-element.10.ann_scale, bf16[1024,1536]{1,0:T(8,128)(2,1)} %get-tuple-element.11.w_fwd, ...), custom_call_target="tpu_custom_call" | custom-call | tf_op jit(solution)/shard_map/adjoint/pallas_call | solution.py:186
  56.1 3.5 %all-to-all-start.3 = ((bf16[16,64,128]{2,1,0:T(8,128)(2,1)}), bf16[16,64,128]{2,1,0:T(8,128)(2,1)S(1)}, u32[]{:S(2)}, u32[]{:S(2)}) async-start(bf16[16,64,128]{2,1,0:T(8,128)(2,1)} %bitcast.19), calls=%async_computation.3 | async-start | bytes 524288 | tf_op jit(solution)/shard_map/all_to_all | solution.py:122
  59.9 1.6 %collective-permute-start = (f32[16,2]{1,0:T(8,128)S(1)}, f32[16,2]{1,0:T(8,128)S(1)}, u32[]{:S(2)}, u32[]{:S(2)}) collective-permute-start(f32[16,2]{1,0:T(8,128)S(1)} %fusion), channel_id=1, source_target_pairs={{0,16},{16,0},{1,17},{17,1},{2,18},{18,2},{3,19},{19,3},{4,20},{20... | collective-permute-start | bytes 392 | tf_op jit(solution)/shard_map/ppermute | solution.py:129
  61.5 2.2 %collective-permute-done = f32[16,2]{1,0:T(8,128)S(1)} collective-permute-done((f32[16,2]{1,0:T(8,128)S(1)}, f32[16,2]{1,0:T(8,128)S(1)}, u32[]{:S(2)}, u32[]{:S(2)}) %collective-permute-start) | collective-permute-done | bytes 160 | tf_op jit(solution)/shard_map/ppermute | solution.py:129
  63.7 0.5 broadcast_multiply_fusion
  64.2 5.4 %all-to-all-done.3 = bf16[16,64,128]{2,1,0:T(8,128)(2,1)S(1)} async-done(((bf16[16,64,128]{2,1,0:T(8,128)(2,1)}), bf16[16,64,128]{2,1,0:T(8,128)(2,1)S(1)}, u32[]{:S(2)}, u32[]{:S(2)}) %all-to-all-start.3) | async-done | bytes 262176 | tf_op jit(solution)/shard_map/all_to_all | solution.py:122
  69.6 0.2 convolution_bitcast_fusion
  70.0 0.7 %copy.22 = f32[128,2,64]{0,2,1:T(8,128)} copy(f32[128,2,64]{2,1,0:T(2,128)S(1)} %reshape.66) | data formatting | bytes 131072
  (16 shorter events, 1.0 us)
Async XLA Ops:
  0.6 1.0 %copy-start = (bf16[32,16]{0,1:T(8,128)(2,1)S(1)}, bf16[32,16]{0,1:T(8,128)(2,1)}, u32[]{:S(2)}) copy-start(bf16[32,16]{0,1:T(8,128)(2,1)} %param.12) | copy-start | bytes 3076
  2.5 17.4 %all-to-all-start = ((bf16[16,64,128]{2,1,0:T(8,128)(2,1)}), bf16[16,64,128]{2,1,0:T(8,128)(2,1)S(1)}, u32[]{:S(2)}, u32[]{:S(2)}) async-start(bf16[16,64,128]{2,1,0:T(8,128)(2,1)} %broadcast_in_dim.33), calls=%async_computation | async-start | bytes 524288 | tf_op jit(solution)/shard_map/all_to_all | solution.py:116
  19.9 0.7 copy-start.1
  26.9 11.4 %all-to-all-start.1 = ((f32[16,16,128]{2,1,0:T(8,128)}), f32[16,16,128]{2,1,0:T(8,128)S(1)}, u32[]{:S(2)}, u32[]{:S(2)}) async-start(f32[16,16,128]{2,1,0:T(8,128)} %bitcast.22), calls=%async_computation.1 | async-start | bytes 262144 | tf_op jit(solution)/shard_map/all_to_all | solution.py:122
  49.2 10.5 %copy-start.2 = (f32[16]{0:T(128)S(1)}, f32[16]{0:T(128)}, u32[]{:S(2)}) copy-start(f32[16]{0:T(128)} %param.20) | copy-start | bytes 196
  56.1 13.5 %all-to-all-start.3 = ((bf16[16,64,128]{2,1,0:T(8,128)(2,1)}), bf16[16,64,128]{2,1,0:T(8,128)(2,1)S(1)}, u32[]{:S(2)}, u32[]{:S(2)}) async-start(bf16[16,64,128]{2,1,0:T(8,128)(2,1)} %bitcast.19), calls=%async_computation.3 | async-start | bytes 524288 | tf_op jit(solution)/shard_map/all_to_all | solution.py:122
  59.9 3.7 %collective-permute-start = (f32[16,2]{1,0:T(8,128)S(1)}, f32[16,2]{1,0:T(8,128)S(1)}, u32[]{:S(2)}, u32[]{:S(2)}) collective-permute-start(f32[16,2]{1,0:T(8,128)S(1)} %fusion), channel_id=1, source_target_pairs={{0,16},{16,0},{1,17},{17,1},{2,18},{18,2},{3,19},{19,3},{4,20},{20... | collective-permute-start | bytes 392 | tf_op jit(solution)/shard_map/ppermute | solution.py:129

commit v2 on v1

v2 whole, which is shorter than its diff:
```python
import functools
import math

import jax
import jax.numpy as jnp
from jax import lax
from jax.experimental import pallas as pl
from jax.experimental.pallas import tpu as pltpu
from jax.sharding import PartitionSpec as P

F32 = jnp.float32
BF16 = jnp.bfloat16
NT = (((1,), (1,)), ((), ()))
TN = (((0,), (0,)), ((), ()))
LANES = 128
TILE = 512
VMEM = pl.BlockSpec(memory_space=pltpu.VMEM)


def log1p_unit(e):
    return jnp.where(e < 1e-4, (1.0 - 0.5 * e) * e, jnp.log(1.0 + e))


def split_bf16(x):
    high = x.astype(BF16)
    return high, (x - high.astype(F32)).astype(BF16)


def iota(shape, dim):
    return lax.broadcasted_iota(jnp.int32, shape, dim)


def block_basis(basis_t, factors, height):
    tenors, size = basis_t.shape
    down = (iota((factors, size), 0) % size == iota((factors, size), 1)).astype(BF16)
    across = (iota((tenors, height), 1) % tenors == iota((tenors, height), 0)).astype(BF16)
    spread = lax.dot_general(down, basis_t, NT, preferred_element_type=F32).astype(BF16)
    tiled = jnp.dot(spread, across, preferred_element_type=F32)
    same = iota((factors, height), 0) // size == iota((factors, height), 1) // tenors
    return jnp.where(same, tiled, 0.0).astype(BF16)


def pair_order(ids, local, devices):
    shift = int(math.log2(local))
    core = lax.rem(lax.axis_index("trade"), 2)
    owner = jnp.right_shift(ids, shift)
    side = jnp.bitwise_xor(jnp.bitwise_and(owner, 1), core)
    place = side * (devices // 2) + jnp.right_shift(owner, 1)
    return place * local + jnp.bitwise_and(ids, local - 1)


def curve_kernel(factors_ref, basis_ref, weight_ref, out):
    copies = out.shape[0]
    rows, factors = factors_ref.shape
    tenors, size = basis_ref.shape
    height = factors // size * tenors
    basis = block_basis(basis_ref[...], factors, height)
    curves = lax.dot_general(
        basis, factors_ref[...], (((0,), (1,)), ((), ())), preferred_element_type=F32
    ).astype(BF16)
    dates, sets = weight_ref.shape
    high, low = split_bf16(weight_ref[...])
    span = rows // dates
    lane = iota((dates, rows), 1)
    owner = (lane // span == iota((dates, rows), 0)).astype(BF16)
    first = (lane % span < span // 2).astype(BF16)
    weights = lax.dot_general(high, owner * first, TN, preferred_element_type=F32)
    weights += lax.dot_general(low, owner * (1.0 - first), TN, preferred_element_type=F32)
    for k in range(copies):
        out[k, :height, :] = curves
        out[k, height:, :] = weights.astype(BF16)


def prep_kernel(devices, blocks_ref, set_ref, weights_ref, w_fwd, w_disc, onehot):
    tenors, trades = weights_ref.shape
    height = w_fwd.shape[0]
    blocks = height // tenors
    sets = onehot.shape[0]
    zero = jnp.zeros((tenors, LANES), F32)
    row = iota((16, LANES), 0)
    set_rows = pair_order(set_ref[...], sets // devices, devices)
    block_rows = pair_order(blocks_ref[...], blocks // devices, devices)
    for t in range(0, trades, LANES):
        lanes = slice(t, t + LANES)
        weights = weights_ref[:, lanes]
        for k, out in enumerate((w_fwd, w_disc)):
            ids = jnp.broadcast_to(block_rows[k : k + 1, lanes], (tenors, LANES))
            for b in range(blocks):
                out[b * tenors : (b + 1) * tenors, lanes] = jnp.where(
                    ids == b, weights, zero
                ).astype(BF16)
        ids = jnp.broadcast_to(set_rows[t // LANES : t // LANES + 1, :], (16, LANES))
        for n in range(0, sets, 16):
            onehot[n : n + 16, lanes] = jnp.where(ids == row + n, 1.0, 0.0).astype(BF16)


def joined_curves(mine, partner, height):
    parts = [ref[k, :height, :] for ref in (mine, partner) for k in range(ref.shape[0])]
    return jnp.concatenate(parts, axis=0)


def param_row(ref, start, tile):
    return jnp.concatenate(
        [ref[j : j + 1, :] for j in range(start // LANES, (start + tile) // LANES)], axis=1
    )


def price_kernel(
    height, mine, partner, w_fwd, w_disc, onehot, kind_ref, notional_ref, strike_ref, vol_ref,
    threshold_ref, keep, send, fwd_scale, ann_scale,
):
    rows = mine.shape[2]
    trades = w_fwd.shape[1]
    half = keep.shape[0]
    tile = TILE if trades % TILE == 0 else trades
    curve = joined_curves(mine, partner, height)
    discount = jnp.exp(-0.5 * curve.astype(F32)).astype(BF16)
    total = jnp.zeros((2 * half, rows), F32)
    for t in range(0, trades, tile):
        lanes = slice(t, t + tile)
        forward = lax.dot_general(curve, w_fwd[:, lanes], TN, preferred_element_type=F32)
        annuity = lax.dot_general(discount, w_disc[:, lanes], TN, preferred_element_type=F32)
        vol = param_row(vol_ref, t, tile)
        notional = param_row(notional_ref, t, tile)
        option = jnp.broadcast_to(param_row(kind_ref, t, tile) == 1, (rows, tile))
        moneyness = forward - param_row(strike_ref, t, tile)
        scaled = moneyness * (1.0 / vol)
        e = jnp.exp(-jnp.abs(scaled))
        softplus = jnp.maximum(scaled, 0.0) + log1p_unit(e)
        sigmoid = jnp.where(scaled >= 0.0, 1.0, e) / (1.0 + e)
        payoff = jnp.where(option, vol * softplus, moneyness)
        slope = jnp.where(option, sigmoid, 1.0)
        scaled_annuity = notional * annuity
        value = (scaled_annuity * payoff).astype(BF16)
        fwd_scale[:, lanes] = scaled_annuity * slope
        ann_scale[:, lanes] = notional * payoff
        total += lax.dot_general(onehot[:, lanes], value, NT, preferred_element_type=F32)
    keep[...] = total[:half]
    send[...] = total[half:].astype(BF16)
    sets = threshold_ref.shape[1]
    chip = lax.axis_index("trade") // 2
    own = pl.ds(pl.multiple_of(chip * sets, sets), sets)
    square = iota((sets, sets), 0) == iota((sets, sets), 1)
    column = jnp.sum(jnp.where(square, threshold_ref[...], 0.0), axis=1, keepdims=True)
    keep[own, :] = keep[own, :] - column


def sets_kernel(height, mine, *refs):
    parts, (cots, own_out, excess_ref) = refs[:-3], refs[-3:]
    chips, padded, rows = mine.shape
    sets = padded - height
    excess = parts[0][...].astype(F32)
    for part in parts[1:]:
        excess += part[...].astype(F32)
    excess_ref[...] = excess
    split = jnp.concatenate([mine[k, height:, :] for k in range(chips)], axis=0).astype(F32)
    quarter = rows // 4
    lane = iota(split.shape, 1)
    other = jnp.where(
        lane % (2 * quarter) < quarter,
        pltpu.roll(split, rows - quarter, 1),
        pltpu.roll(split, quarter, 1),
    )
    e = jnp.exp(-jnp.abs(excess))
    sigmoid = jnp.where(excess >= 0.0, 1.0, e) / (1.0 + e)
    cots[...] = ((split + other) * sigmoid).astype(BF16)
    chip = lax.axis_index("trade") // 2
    own_out[...] = excess_ref[pl.ds(pl.multiple_of(chip * sets, sets), sets), :]


def adjoint_kernel(
    height, mine, partner, cots_mine, cots_partner, fwd_scale, ann_scale, w_fwd, w_disc, onehot,
    keep, send,
):
    half = keep.shape[0]
    rows, trades = fwd_scale.shape
    tile = TILE if trades % TILE == 0 else trades
    cots = jnp.concatenate([cots_mine[...], cots_partner[...]], axis=0)
    from_fwd = jnp.zeros((2 * half, rows), F32)
    from_disc = jnp.zeros((2 * half, rows), F32)
    for t in range(0, trades, tile):
        lanes = slice(t, t + tile)
        trade_cot = lax.dot_general(cots, onehot[:, lanes], TN, preferred_element_type=F32)
        fwd_cot = (trade_cot * fwd_scale[:, lanes]).astype(BF16)
        ann_cot = (trade_cot * ann_scale[:, lanes]).astype(BF16)
        from_fwd += lax.dot_general(w_fwd[:, lanes], fwd_cot, NT, preferred_element_type=F32)
        from_disc += lax.dot_general(w_disc[:, lanes], ann_cot, NT, preferred_element_type=F32)
    discount = jnp.exp(-0.5 * joined_curves(mine, partner, height).astype(F32))
    total = from_fwd - 0.5 * discount * from_disc
    keep[...] = total[:half]
    send[...] = total[half:].astype(BF16)


def factor_kernel(parts, basis_ref, out):
    total = parts[0].astype(F32)
    for k in range(1, parts.shape[0]):
        total += parts[k].astype(F32)
    basis = block_basis(basis_ref[...], out.shape[1], total.shape[0])
    dims = (((0,), (1,)), ((), ()))
    high, low = split_bf16(total)
    out[...] = lax.dot_general(high, basis, dims, preferred_element_type=F32) + lax.dot_general(
        low, basis, dims, preferred_element_type=F32
    )


def call(kernel, name, out_shape, scratch=(), flops=1_000_000, moved=1_000_000):
    def run(*args):
        return pl.pallas_call(
            kernel,
            in_specs=[VMEM] * len(args),
            out_specs=jax.tree.map(lambda _: VMEM, out_shape),
            out_shape=out_shape,
            scratch_shapes=scratch,
            cost_estimate=pl.CostEstimate(flops=flops, bytes_accessed=moved, transcendentals=0),
            compiler_params=pltpu.CompilerParams(vmem_limit_bytes=24 * 2**20),
            name=name,
        )(*args)

    return run


def swap(x, mask):
    n = lax.axis_size("trade")
    return lax.ppermute(x, "trade", [(i, i ^ mask) for i in range(n)])


def chip_exchange(x):
    n = lax.axis_size("trade")
    groups = [[2 * k + core for k in range(n // 2)] for core in range(2)]
    return lax.all_to_all(x, "trade", 0, 0, axis_index_groups=groups)


def sum_over(x, axis):
    n = lax.axis_size(axis)
    total = x
    for shift in range(1, n):
        total = total + lax.ppermute(x, axis, [(i, (i + shift) % n) for i in range(n)])
    return total


def shards(
    factor_paths, tenor_basis, trade_blocks, trade_set, trade_type, notional, strike,
    vol_level, cash_weights, set_threshold, date_weight,
):
    factor_rows, dates, paths = factor_paths.shape
    block_size, tenors = tenor_basis.shape
    rows = dates * paths
    devices = lax.axis_size("trade")
    chips = devices // 2
    local_blocks = factor_rows // block_size
    height = local_blocks * tenors
    local_sets = set_threshold.shape[0]
    half_sets = local_sets * chips
    half_rows = height * chips
    trades = trade_set.shape[0]
    shape = jax.ShapeDtypeStruct

    factors = jnp.transpose(factor_paths, (1, 2, 0)).reshape(rows, factor_rows)
    basis_t = jnp.transpose(tenor_basis)
    payload = call(curve_kernel, "curves", shape((chips, height + local_sets, rows), BF16))(
        factors, basis_t, jnp.transpose(date_weight)
    )
    mine = chip_exchange(payload)
    partner = swap(mine, 1)

    w_fwd, w_disc, onehot = call(
        functools.partial(prep_kernel, devices), "prep",
        [shape((2 * half_rows, trades), BF16)] * 2 + [shape((2 * half_sets, trades), BF16)],
        flops=400_000_000, moved=8_000_000,
    )(trade_blocks, trade_set.reshape(-1, LANES), cash_weights)
    keep, send, fwd_scale, ann_scale = call(
        functools.partial(price_kernel, height), "price",
        [shape((half_sets, rows), F32), shape((half_sets, rows), BF16),
         shape((rows, trades), F32), shape((rows, trades), F32)],
    )(
        mine, partner, w_fwd, w_disc, onehot, trade_type.reshape(-1, LANES),
        notional.reshape(-1, LANES), strike.reshape(-1, LANES), vol_level.reshape(-1, LANES),
        set_threshold[None],
    )

    total = (keep + swap(send, 1).astype(F32)).astype(BF16)
    bits = [1 << k for k in range(1, int(math.log2(devices)))]
    steps = [bits[:1]] if len(bits) % 2 else []
    steps += [bits[k : k + 2] for k in range(len(bits) % 2, len(bits), 2)]
    for step in steps:
        masks = step if len(step) == 1 else [step[0], step[1], step[0] + step[1]]
        parts = [total] + [swap(total, mask) for mask in masks]
        if step is not steps[-1]:
            total = functools.reduce(jnp.add, [p.astype(F32) for p in parts]).astype(BF16)
    cots_mine, excess = call(
        functools.partial(sets_kernel, height), "sets",
        [shape((half_sets, rows), BF16), shape((local_sets, rows), F32)],
        [pltpu.VMEM((half_sets, rows), F32)],
    )(mine, *parts)
    cots_partner = swap(cots_mine, 1)

    keep, send = call(
        functools.partial(adjoint_kernel, height), "adjoint",
        [shape((half_rows, rows), F32), shape((half_rows, rows), BF16)],
    )(mine, partner, cots_mine, cots_partner, fwd_scale, ann_scale, w_fwd, w_disc, onehot)
    pair = (keep + swap(send, 1).astype(F32)).astype(BF16)
    arrived = chip_exchange(pair.reshape(chips, height, rows))
    factor_cot = call(factor_kernel, "factors", shape((rows, factor_rows), F32))(arrived, basis_t)
    factor_cot = jnp.transpose(factor_cot.reshape(dates, paths, factor_rows), (2, 0, 1))

    exposure = jax.nn.softplus(excess).reshape(local_sets, dates, paths)
    weighted = jnp.sum(date_weight * jnp.sum(exposure, axis=2), axis=1)
    netting_cva = sum_over(weighted, "path") / (paths * lax.axis_size("path"))
    return netting_cva, factor_cot


def solution(mesh):
    return jax.shard_map(
        shards,
        mesh=mesh,
        in_specs=(
            P("trade", None, "path"), P(), P(None, "trade"), P("trade"), P("trade"),
            P("trade"), P("trade"), P("trade"), P(None, "trade"), P("trade"),
            P("trade", None),
        ),
        out_specs=(P("trade"), P("trade", None, "path")),
        check_vma=False,
    )
```

time: 71.5 us -> 67.1 us (0.938)
  waiting for transfers between devices: 18 us -> 11.9 us
  local copies, waits for them, and re-layouts: 10.8 us -> 16.5 us
  Pallas kernels: 13.1 us -> 7.51 us
  blocking collectives: 10.2 us -> 14.7 us
  starting transfers between devices: 16 us -> 11.7 us
  other arithmetic: 1.62 us -> 3.09 us
    all_to_all x3 -> x1, waiting for transfers between devices: 15.8 us -> 2.39 us  [chip_exchange(): return lax.all_to_all(x, 'trade', 0, 0, axis_index_groups=groups)]
    unnamed x9 -> x45, local copies, waits for them, and re-layouts: 3.07 us -> 16.4 us
    all_to_all x3 -> x1, starting transfers between devices: 14.5 us -> 3.97 us  [chip_exchange(): return lax.all_to_all(x, 'trade', 0, 0, axis_index_groups=groups)]
    ppermute x0 -> x8, waiting for transfers between devices: none -> 7.47 us  [swap(): return lax.ppermute(x, 'trade', [(i, i ^ mask) for i in range(n)])]
    broadcast_in_dim x8 -> x0, local copies, waits for them, and re-layouts: 7.31 us -> none  [the longest x1 1.3 us: shards(): trade_set[None]]
    ppermute x0 -> x8, starting transfers between devices: none -> 6.17 us  [swap(): return lax.ppermute(x, 'trade', [(i, i ^ mask) for i in range(n)])]
    pallas_call x2 -> x6, Pallas kernels: 13.1 us -> 7.51 us  [run(): pl.pallas_call(kernel, in_specs=[VMEM] * len(args), out_specs=jax.tree.ma...]
    all_to_all x1, blocking collectives: 10.2 us -> 14.7 us  [chip_exchange(): return lax.all_to_all(x, 'trade', 0, 0, axis_index_groups=groups)]
  transfers between devices with their start and end apart: 4 -> 10, of which waited for: 4 -> 9; matrix products, arithmetic and copies ran while one was open for 12% -> 3% of each run, Pallas kernels for 0% -> 2%
where the time goes in v2:
time: 67.1 us; the launch traced here: 66.1 us
  local copies, waits for them, and re-layouts  16.5 us (25%)
  blocking collectives  14.7 us (22%)
  waiting for transfers between devices  11.9 us (18%)
  starting transfers between devices  11.7 us (17%)
  Pallas kernels  7.51 us (11%)
  other arithmetic  3.09 us (5%)
  between operations  0.78 us (1%)
    unnamed x45, local copies, waits for them, and re-layouts  16.4 us
    all_to_all x1, blocking collectives, chip_exchange(): return lax.all_to_all(x, 'trade', 0, 0, axis_index_groups=groups)  14.7 us
    pallas_call x6, Pallas kernels, run(): pl.pallas_call(kernel, in_specs=[VMEM] * len(args), out_specs=jax.tree.ma...  7.51 us
    ppermute x8, waiting for transfers between devices, swap(): return lax.ppermute(x, 'trade', [(i, i ^ mask) for i in range(n)])  7.47 us
    ppermute x8, starting transfers between devices, swap(): return lax.ppermute(x, 'trade', [(i, i ^ mask) for i in range(n)])  6.17 us
    all_to_all x1, starting transfers between devices, chip_exchange(): return lax.all_to_all(x, 'trade', 0, 0, axis_index_groups=groups)  3.97 us
    all_to_all x1, waiting for transfers between devices, chip_exchange(): return lax.all_to_all(x, 'trade', 0, 0, axis_index_groups=groups)  2.39 us
    ppermute x1, waiting for transfers between devices, sum_over(): lax.ppermute(x, axis, [(i, (i + shift) % n) for i in range(n)])  2.08 us
  transfers between devices with their start and end apart: 10, of which 9 were waited for; matrix products, arithmetic and copies ran while one was open for 3% of the time, Pallas kernels for 2%

profile of v2, /device:TPU:0, one launch (start us, length us, event | category | flops | bytes accessed | tf_op | source)
XLA Modules:
  0.0 66.1 jit_solution(6444065860064179819)
XLA Ops:
  3.2 14.7 %all_to_all.10.mine = bf16[8,80,128]{2,1,0:T(8,128)(2,1)S(1)} all-to-all(bf16[8,80,128]{2,1,0:T(8,128)(2,1)S(1)} %curves.1), channel_id=1, replica_groups={{0,2,4,6,8,10,12,14},{1,3,5,7,9,11,13,15},{16,18,20,22,24,26,28,30},{17..., dimensions={0} | all-to-all | bytes 327680 | tf_op jit(solution)/shard_map/all_to_all | solution.py:230
  17.9 0.9 %copy-done.19 = f32[16,1536]{1,0:T(8,128)S(1)} copy-done((f32[16,1536]{1,0:T(8,128)S(1)}, f32[16,1536]{1,0:T(8,128)}, u32[]{:S(2)}) %copy-start.19) | copy-done | bytes 98328
  20.1 1.4 %prep.1 = (bf16[1024,1536]{1,0:T(8,128)(2,1)S(1)}, bf16[1024,1536]{1,0:T(8,128)(2,1)S(1)}, bf16[256,1536]{1,0:T(8,128)(2,1)S(1)}) custom-call(s32[2,1536]{1,0:T(2,128)S(1)} %copy-done.20, s32[12,128]{1,0:T(8,128)S(1)} %bitcast.24, f32[16,1536]{1,0:T(8,128)S(1)} %copy-done.19), custom_call_target="tpu_custom_call" | custom-call | flops 400000000 | bytes 8000000 | tf_op jit(solution)/shard_map/prep/pallas_call | solution.py:208
  25.1 1.7 %price.1 = (f32[128,128]{1,0:T(8,128)S(1)}, bf16[128,128]{1,0:T(8,128)(2,1)S(1)}, f32[128,1536]{1,0:T(8,128)S(1)}, f32[128,1536]{1,0:T(8,128)S(1)}) custom-call(bf16[8,80,128]{2,1,0:T(8,128)(2,1)S(1)} %all_to_all.10.mine, bf16[8,80,128]{2,1,0:T(8,128)(2,1)S(1)} %collective-permute-done.partner, bf16[1024,1536]{1,0:T(8,128)(2,1)S(1)} %get-tuple-element.13.w_fwd, ...), custom_call_target="tpu_custom_call" | custom-call | flops 1000000 | bytes 1000000 | tf_op jit(solution)/shard_map/price/pallas_call | solution.py:208
  26.9 0.9 %copy-done.4 = f32[128,1536]{1,0:T(8,128)} copy-done((f32[128,1536]{1,0:T(8,128)}, f32[128,1536]{1,0:T(8,128)S(1)}, u32[]{:S(2)}) %copy-start.4) | copy-done | bytes 786456
  27.7 0.9 %copy-done.6 = f32[128,1536]{1,0:T(8,128)} copy-done((f32[128,1536]{1,0:T(8,128)}, f32[128,1536]{1,0:T(8,128)S(1)}, u32[]{:S(2)}) %copy-start.6) | copy-done | bytes 786456
  29.2 0.9 %collective-permute-done.1 = bf16[128,128]{1,0:T(8,128)(2,1)S(1)} collective-permute-done((bf16[128,128]{1,0:T(8,128)(2,1)S(1)}, bf16[128,128]{1,0:T(8,128)(2,1)S(1)}, u32[]{:S(2)}, u32[]{:S(2)}) %collective-permute-start.1) | collective-permute-done | bytes 32800 | tf_op jit(solution)/shard_map/ppermute | solution.py:224
  30.0 1.0 %collective-permute-start.2 = (bf16[128,128]{1,0:T(8,128)(2,1)S(1)}, bf16[128,128]{1,0:T(8,128)(2,1)S(1)}, u32[]{:S(2)}, u32[]{:S(2)}) collective-permute-start(bf16[128,128]{1,0:T(8,128)(2,1)S(1)} %add_convert_fusion.2), channel_id=1, source_target_pairs={{0,2},{1,3},{2,0},{3,1},{4,6},{5,7},{6,4},{7,5},{8,10},{9,11},{10,... | collective-permute-start | bytes 98312 | tf_op jit(solution)/shard_map/ppermute | solution.py:224
  31.0 3.0 %collective-permute-done.2 = bf16[128,128]{1,0:T(8,128)(2,1)S(1)} collective-permute-done((bf16[128,128]{1,0:T(8,128)(2,1)S(1)}, bf16[128,128]{1,0:T(8,128)(2,1)S(1)}, u32[]{:S(2)}, u32[]{:S(2)}) %collective-permute-start.2) | collective-permute-done | bytes 32800 | tf_op jit(solution)/shard_map/ppermute | solution.py:224
  34.7 1.1 %collective-permute-start.4 = (bf16[128,128]{1,0:T(8,128)(2,1)S(1)}, bf16[128,128]{1,0:T(8,128)(2,1)S(1)}, u32[]{:S(2)}, u32[]{:S(2)}) collective-permute-start(bf16[128,128]{1,0:T(8,128)(2,1)S(1)} %add_convert_fusion.1.refs_0_), channel_id=1, source_target_pairs={{0,8},{1,9},{2,10},{3,11},{4,12},{5,13},{6,14},{7,15},{8,0},{9,1},... | collective-permute-start | bytes 98312 | tf_op jit(solution)/shard_map/ppermute | solution.py:224
  35.8 2.7 %collective-permute-start.3 = (bf16[128,128]{1,0:T(8,128)(2,1)S(1)}, bf16[128,128]{1,0:T(8,128)(2,1)S(1)}, u32[]{:S(2)}, u32[]{:S(2)}) collective-permute-start(bf16[128,128]{1,0:T(8,128)(2,1)S(1)} %add_convert_fusion.1.refs_0_), channel_id=1, source_target_pairs={{0,4},{1,5},{2,6},{3,7},{4,0},{5,1},{6,2},{7,3},{8,12},{9,13},{10,... | collective-permute-start | bytes 98312 | tf_op jit(solution)/shard_map/ppermute | solution.py:224
  38.5 1.4 %collective-permute-done.5.refs_3_ = bf16[128,128]{1,0:T(8,128)(2,1)S(1)} collective-permute-done((bf16[128,128]{1,0:T(8,128)(2,1)S(1)}, bf16[128,128]{1,0:T(8,128)(2,1)S(1)}, u32[]{:S(2)}, u32[]{:S(2)}) %collective-permute-start.5) | collective-permute-done | bytes 32800 | tf_op jit(solution)/shard_map/ppermute | solution.py:224
  41.7 1.9 %copy-done.1 = bf16[1024,1536]{1,0:T(8,128)(2,1)S(1)} copy-done((bf16[1024,1536]{1,0:T(8,128)(2,1)S(1)}, bf16[1024,1536]{1,0:T(8,128)(2,1)}, u32[]{:S(2)}) %copy-start.1) | copy-done | bytes 3145752
  43.6 1.1 %copy-done.3 = bf16[256,1536]{1,0:T(8,128)(2,1)S(1)} copy-done((bf16[256,1536]{1,0:T(8,128)(2,1)S(1)}, bf16[256,1536]{1,0:T(8,128)(2,1)}, u32[]{:S(2)}) %copy-start.3) | copy-done | bytes 786456
  44.8 1.1 %copy-done.5 = f32[128,1536]{1,0:T(8,128)S(1)} copy-done((f32[128,1536]{1,0:T(8,128)S(1)}, f32[128,1536]{1,0:T(8,128)}, u32[]{:S(2)}) %copy-start.5) | copy-done | bytes 786456
  45.9 1.1 %copy-done.7 = f32[128,1536]{1,0:T(8,128)S(1)} copy-done((f32[128,1536]{1,0:T(8,128)S(1)}, f32[128,1536]{1,0:T(8,128)}, u32[]{:S(2)}) %copy-start.7) | copy-done | bytes 786456
  47.0 2.8 %adjoint.1 = (f32[512,128]{1,0:T(8,128)S(1)}, bf16[512,128]{1,0:T(8,128)(2,1)}) custom-call(bf16[8,80,128]{2,1,0:T(8,128)(2,1)S(1)} %all_to_all.10.mine, bf16[8,80,128]{2,1,0:T(8,128)(2,1)S(1)} %collective-permute-done.partner, bf16[128,128]{1,0:T(8,128)(2,1)S(1)} %get-tuple-element.19.cots_mine, bf16[128,128]{1,0:T(8,128)(2,1)S(1)} %collective-permute-done.7.cots_partner, ...), custom_call_target="tpu_custom_call" | custom-call | flops 1000000 | bytes 1000000 | tf_op jit(solution)/shard_map/adjoint/pallas_call | solution.py:208
  50.9 1.2 %collective-permute-done.8 = bf16[512,128]{1,0:T(8,128)(2,1)S(1)} collective-permute-done((bf16[512,128]{1,0:T(8,128)(2,1)}, bf16[512,128]{1,0:T(8,128)(2,1)S(1)}, u32[]{:S(2)}, u32[]{:S(2)}) %collective-permute-start.8) | collective-permute-done | bytes 131104 | tf_op jit(solution)/shard_map/ppermute | solution.py:224
  52.1 1.6 %add_convert_fusion = bf16[512,128]{1,0:T(8,128)(2,1)} fusion(f32[512,128]{1,0:T(8,128)} %copy-done.8, bf16[512,128]{1,0:T(8,128)(2,1)S(1)} %collective-permute-done.8), kind=kLoop, calls=%fused_computation | loop fusion | flops 196608 | bytes 524288 | tf_op jit(solution)/shard_map/convert_element_type | solution.py:301
  53.8 4.0 %all-to-all-start.1 = ((bf16[8,64,128]{2,1,0:T(8,128)(2,1)}), bf16[8,64,128]{2,1,0:T(8,128)(2,1)S(1)}, u32[]{:S(2)}, u32[]{:S(2)}) async-start(bf16[8,64,128]{2,1,0:T(8,128)(2,1)} %bitcast.10), calls=%async_computation.1 | async-start | bytes 262144 | tf_op jit(solution)/shard_map/all_to_all | solution.py:230
  58.6 1.5 %collective-permute-start.6 = (f32[16]{0:T(128)S(1)}, f32[16]{0:T(128)S(1)}, u32[]{:S(2)}, u32[]{:S(2)}) collective-permute-start(f32[16]{0:T(128)S(1)} %multiply_reduce_fusion), channel_id=1, source_target_pairs={{0,16},{16,0},{1,17},{17,1},{2,18},{18,2},{3,19},{19,3},{4,20},{20... | collective-permute-start | bytes 200 | tf_op jit(solution)/shard_map/ppermute | solution.py:237
  60.1 2.1 %collective-permute-done.6 = f32[16]{0:T(128)S(1)} collective-permute-done((f32[16]{0:T(128)S(1)}, f32[16]{0:T(128)S(1)}, u32[]{:S(2)}, u32[]{:S(2)}) %collective-permute-start.6) | collective-permute-done | bytes 96 | tf_op jit(solution)/shard_map/ppermute | solution.py:237
  62.7 2.4 %all-to-all-done.1.parts = bf16[8,64,128]{2,1,0:T(8,128)(2,1)S(1)} async-done(((bf16[8,64,128]{2,1,0:T(8,128)(2,1)}), bf16[8,64,128]{2,1,0:T(8,128)(2,1)S(1)}, u32[]{:S(2)}, u32[]{:S(2)}) %all-to-all-start.1) | async-done | bytes 131104 | tf_op jit(solution)/shard_map/all_to_all | solution.py:230
  65.1 1.0 %factors.1 = f32[128,128]{1,0:T(8,128)} custom-call(bf16[8,64,128]{2,1,0:T(8,128)(2,1)S(1)} %all-to-all-done.1.parts, bf16[16,32]{1,0:T(8,128)(2,1)S(1)} %bitcast.17), custom_call_target="tpu_custom_call" | custom-call | flops 1000000 | bytes 1000000 | tf_op jit(solution)/shard_map/factors/pallas_call | solution.py:208
  (56 shorter events, 12.9 us)
Async XLA Ops:
  0.6 0.8 %copy-start.9 = (bf16[128,2,64]{0,2,1:T(8,128)(2,1)S(1)}, bf16[128,2,64]{0,2,1:T(8,128)(2,1)}, u32[]{:S(2)}) copy-start(bf16[128,2,64]{0,2,1:T(8,128)(2,1)} %param.11) | copy-start | bytes 98308
  17.8 3.7 %collective-permute-start = (bf16[8,80,128]{2,1,0:T(8,128)(2,1)S(1)}, bf16[8,80,128]{2,1,0:T(8,128)(2,1)S(1)}, u32[]{:S(2)}, u32[]{:S(2)}) collective-permute-start(bf16[8,80,128]{2,1,0:T(8,128)(2,1)S(1)} %all_to_all.10.mine), channel_id=1, source_target_pairs={{0,1},{1,0},{2,3},{3,2},{4,5},{5,4},{6,7},{7,6},{8,9},{9,8},{10,11... | collective-permute-start | bytes 491528 | tf_op jit(solution)/shard_map/ppermute | solution.py:224
  17.9 0.9 %copy-start.19 = (f32[16,1536]{1,0:T(8,128)S(1)}, f32[16,1536]{1,0:T(8,128)}, u32[]{:S(2)}) copy-start(f32[16,1536]{1,0:T(8,128)} %weights_ref.1) | copy-start | bytes 294916
  21.6 5.3 %copy-start = (bf16[1024,1536]{1,0:T(8,128)(2,1)}, bf16[1024,1536]{1,0:T(8,128)(2,1)S(1)}, u32[]{:S(2)}) copy-start(bf16[1024,1536]{1,0:T(8,128)(2,1)S(1)} %get-tuple-element.14.w_disc) | copy-start | bytes 9437188
  21.6 5.3 %copy-start.2 = (bf16[256,1536]{1,0:T(8,128)(2,1)}, bf16[256,1536]{1,0:T(8,128)(2,1)S(1)}, u32[]{:S(2)}) copy-start(bf16[256,1536]{1,0:T(8,128)(2,1)S(1)} %get-tuple-element.15.onehot) | copy-start | bytes 2359300
  21.6 0.7 %copy-start.12 = (s32[1536]{0:T(1024)S(1)}, s32[1536]{0:T(1024)}, u32[]{:S(2)}) copy-start(s32[1536]{0:T(1024)} %param.15) | copy-start | bytes 18436
  22.3 0.7 %copy-start.13 = (f32[1536]{0:T(1024)S(1)}, f32[1536]{0:T(1024)}, u32[]{:S(2)}) copy-start(f32[1536]{0:T(1024)} %param.16) | copy-start | bytes 18436
  25.1 15.4 %copy-start.17 = (f32[16,2]{0,1:T(2,128)S(1)}, f32[16,2]{0,1:T(2,128)}, u32[]{:S(2)}) copy-start(f32[16,2]{0,1:T(2,128)} %param.21) | copy-start | bytes 388
  26.9 0.9 %copy-start.4 = (f32[128,1536]{1,0:T(8,128)}, f32[128,1536]{1,0:T(8,128)S(1)}, u32[]{:S(2)}) copy-start(f32[128,1536]{1,0:T(8,128)S(1)} %get-tuple-element.20.fwd_scale) | copy-start | bytes 2359300
  27.7 0.9 %copy-start.6 = (f32[128,1536]{1,0:T(8,128)}, f32[128,1536]{1,0:T(8,128)S(1)}, u32[]{:S(2)}) copy-start(f32[128,1536]{1,0:T(8,128)S(1)} %get-tuple-element.21.ann_scale) | copy-start | bytes 2359300
  28.6 1.4 %collective-permute-start.1 = (bf16[128,128]{1,0:T(8,128)(2,1)S(1)}, bf16[128,128]{1,0:T(8,128)(2,1)S(1)}, u32[]{:S(2)}, u32[]{:S(2)}) collective-permute-start(bf16[128,128]{1,0:T(8,128)(2,1)S(1)} %get-tuple-element.17), channel_id=1, source_target_pairs={{0,1},{1,0},{2,3},{3,2},{4,5},{5,4},{6,7},{7,6},{8,9},{9,8},{10,11... | collective-permute-start | bytes 98312 | tf_op jit(solution)/shard_map/ppermute | solution.py:224
  30.0 4.0 %collective-permute-start.2 = (bf16[128,128]{1,0:T(8,128)(2,1)S(1)}, bf16[128,128]{1,0:T(8,128)(2,1)S(1)}, u32[]{:S(2)}, u32[]{:S(2)}) collective-permute-start(bf16[128,128]{1,0:T(8,128)(2,1)S(1)} %add_convert_fusion.2), channel_id=1, source_target_pairs={{0,2},{1,3},{2,0},{3,1},{4,6},{5,7},{6,4},{7,5},{8,10},{9,11},{10,... | collective-permute-start | bytes 98312 | tf_op jit(solution)/shard_map/ppermute | solution.py:224
  34.0 5.9 %collective-permute-start.5 = (bf16[128,128]{1,0:T(8,128)(2,1)S(1)}, bf16[128,128]{1,0:T(8,128)(2,1)S(1)}, u32[]{:S(2)}, u32[]{:S(2)}) collective-permute-start(bf16[128,128]{1,0:T(8,128)(2,1)S(1)} %add_convert_fusion.1.refs_0_), channel_id=1, source_target_pairs={{0,12},{1,13},{2,14},{3,15},{4,8},{5,9},{6,10},{7,11},{8,4},{9,5},... | collective-permute-start | bytes 98312 | tf_op jit(solution)/shard_map/ppermute | solution.py:224
  34.7 5.5 %collective-permute-start.4 = (bf16[128,128]{1,0:T(8,128)(2,1)S(1)}, bf16[128,128]{1,0:T(8,128)(2,1)S(1)}, u32[]{:S(2)}, u32[]{:S(2)}) collective-permute-start(bf16[128,128]{1,0:T(8,128)(2,1)S(1)} %add_convert_fusion.1.refs_0_), channel_id=1, source_target_pairs={{0,8},{1,9},{2,10},{3,11},{4,12},{5,13},{6,14},{7,15},{8,0},{9,1},... | collective-permute-start | bytes 98312 | tf_op jit(solution)/shard_map/ppermute | solution.py:224
  35.8 4.6 %collective-permute-start.3 = (bf16[128,128]{1,0:T(8,128)(2,1)S(1)}, bf16[128,128]{1,0:T(8,128)(2,1)S(1)}, u32[]{:S(2)}, u32[]{:S(2)}) collective-permute-start(bf16[128,128]{1,0:T(8,128)(2,1)S(1)} %add_convert_fusion.1.refs_0_), channel_id=1, source_target_pairs={{0,4},{1,5},{2,6},{3,7},{4,0},{5,1},{6,2},{7,3},{8,12},{9,13},{10,... | collective-permute-start | bytes 98312 | tf_op jit(solution)/shard_map/ppermute | solution.py:224
  40.5 1.3 %collective-permute-start.7 = (bf16[128,128]{1,0:T(8,128)(2,1)S(1)}, bf16[128,128]{1,0:T(8,128)(2,1)S(1)}, u32[]{:S(2)}, u32[]{:S(2)}) collective-permute-start(bf16[128,128]{1,0:T(8,128)(2,1)S(1)} %get-tuple-element.19.cots_mine), channel_id=1, source_target_pairs={{0,1},{1,0},{2,3},{3,2},{4,5},{5,4},{6,7},{7,6},{8,9},{9,8},{10,11... | collective-permute-start | bytes 98312 | tf_op jit(solution)/shard_map/ppermute | solution.py:224
  41.7 1.9 %copy-start.1 = (bf16[1024,1536]{1,0:T(8,128)(2,1)S(1)}, bf16[1024,1536]{1,0:T(8,128)(2,1)}, u32[]{:S(2)}) copy-start(bf16[1024,1536]{1,0:T(8,128)(2,1)} %copy-done) | copy-start | bytes 9437188
  43.6 1.1 %copy-start.3 = (bf16[256,1536]{1,0:T(8,128)(2,1)S(1)}, bf16[256,1536]{1,0:T(8,128)(2,1)}, u32[]{:S(2)}) copy-start(bf16[256,1536]{1,0:T(8,128)(2,1)} %copy-done.2) | copy-start | bytes 2359300
  44.8 1.1 %copy-start.5 = (f32[128,1536]{1,0:T(8,128)S(1)}, f32[128,1536]{1,0:T(8,128)}, u32[]{:S(2)}) copy-start(f32[128,1536]{1,0:T(8,128)} %copy-done.4) | copy-start | bytes 2359300
  45.9 1.1 %copy-start.7 = (f32[128,1536]{1,0:T(8,128)S(1)}, f32[128,1536]{1,0:T(8,128)}, u32[]{:S(2)}) copy-start(f32[128,1536]{1,0:T(8,128)} %copy-done.6) | copy-start | bytes 2359300
  47.0 18.1 %copy-start.11 = (bf16[32,16]{0,1:T(8,128)(2,1)S(1)}, bf16[32,16]{0,1:T(8,128)(2,1)}, u32[]{:S(2)}) copy-start(bf16[32,16]{0,1:T(8,128)(2,1)} %param.12) | copy-start | bytes 3076
  50.6 1.6 %collective-permute-start.8 = (bf16[512,128]{1,0:T(8,128)(2,1)}, bf16[512,128]{1,0:T(8,128)(2,1)S(1)}, u32[]{:S(2)}, u32[]{:S(2)}) collective-permute-start(bf16[512,128]{1,0:T(8,128)(2,1)} %get-tuple-element.23), channel_id=1, source_target_pairs={{0,1},{1,0},{2,3},{3,2},{4,5},{5,4},{6,7},{7,6},{8,9},{9,8},{10,11... | collective-permute-start | bytes 393224 | tf_op jit(solution)/shard_map/ppermute | solution.py:224
  53.8 11.3 %all-to-all-start.1 = ((bf16[8,64,128]{2,1,0:T(8,128)(2,1)}), bf16[8,64,128]{2,1,0:T(8,128)(2,1)S(1)}, u32[]{:S(2)}, u32[]{:S(2)}) async-start(bf16[8,64,128]{2,1,0:T(8,128)(2,1)} %bitcast.10), calls=%async_computation.1 | async-start | bytes 262144 | tf_op jit(solution)/shard_map/all_to_all | solution.py:230
  58.6 3.6 %collective-permute-start.6 = (f32[16]{0:T(128)S(1)}, f32[16]{0:T(128)S(1)}, u32[]{:S(2)}, u32[]{:S(2)}) collective-permute-start(f32[16]{0:T(128)S(1)} %multiply_reduce_fusion), channel_id=1, source_target_pairs={{0,16},{16,0},{1,17},{17,1},{2,18},{18,2},{3,19},{19,3},{4,20},{20... | collective-permute-start | bytes 200 | tf_op jit(solution)/shard_map/ppermute | solution.py:237
  (8 other events, 5.5 us)

commit v3 on v2

v3 whole, which is shorter than its diff:
```python
import functools
import math

import jax
import jax.numpy as jnp
from jax import lax
from jax.experimental import pallas as pl
from jax.experimental.pallas import tpu as pltpu
from jax.sharding import PartitionSpec as P

F32 = jnp.float32
BF16 = jnp.bfloat16
NT = (((1,), (1,)), ((), ()))
TN = (((0,), (0,)), ((), ()))
LANES = 128
TILE = 512
VMEM = pl.BlockSpec(memory_space=pltpu.VMEM)
HBM = pl.BlockSpec(memory_space=pltpu.HBM)
VMEM_LIMIT = 8 * 2**20


def log1p_unit(e):
    return jnp.where(e < 1e-4, (1.0 - 0.5 * e) * e, jnp.log(1.0 + e))


def split_bf16(x):
    high = x.astype(BF16)
    return high, (x - high.astype(F32)).astype(BF16)


def iota(shape, dim):
    return lax.broadcasted_iota(jnp.int32, shape, dim)


def block_basis(basis_t, factors, height):
    tenors, size = basis_t.shape
    down = (iota((factors, size), 0) % size == iota((factors, size), 1)).astype(BF16)
    across = (iota((tenors, height), 1) % tenors == iota((tenors, height), 0)).astype(BF16)
    spread = lax.dot_general(down, basis_t, NT, preferred_element_type=F32).astype(BF16)
    tiled = jnp.dot(spread, across, preferred_element_type=F32)
    same = iota((factors, height), 0) // size == iota((factors, height), 1) // tenors
    return jnp.where(same, tiled, 0.0).astype(BF16)


def bits_of(n):
    return int(math.log2(n))


def pair_order(ids, local, devices):
    core = lax.rem(lax.axis_index("trade"), 2)
    owner = jnp.right_shift(ids, bits_of(local))
    side = jnp.bitwise_xor(jnp.bitwise_and(owner, 1), core)
    place = side * (devices // 2) + jnp.right_shift(owner, 1)
    return place * local + jnp.bitwise_and(ids, local - 1)


def cube_place(owner, devices):
    distance = jnp.bitwise_xor(owner, lax.axis_index("trade"))
    bits = bits_of(devices)
    place = jnp.zeros_like(distance)
    for k in range(bits):
        bit = jnp.bitwise_and(jnp.right_shift(distance, k), 1)
        place = jnp.bitwise_or(place, jnp.left_shift(bit, bits - 1 - k))
    return place


def cube_order(ids, local, devices):
    place = cube_place(jnp.right_shift(ids, bits_of(local)), devices)
    return place * local + jnp.bitwise_and(ids, local - 1)


def fetch(pairs, sems):
    copies = [pltpu.make_async_copy(src, dst, sems.at[k]) for k, (src, dst) in enumerate(pairs)]
    for copy in copies:
        copy.start()
    for copy in copies:
        copy.wait()


def curve_kernel(
    factors_hbm, basis_hbm, weight_hbm, out, basis_out, weight_ref, factors_ref, basis_ref, sems
):
    fetch(
        [(factors_hbm, factors_ref), (basis_hbm, basis_ref), (weight_hbm, weight_ref)], sems
    )
    rows, factors = factors_ref.shape
    tenors, size = basis_ref.shape
    height = factors // size * tenors
    basis = block_basis(basis_ref[...], factors, height)
    basis_out[...] = basis
    out[:height, :] = lax.dot_general(
        basis, factors_ref[...], (((0,), (1,)), ((), ())), preferred_element_type=F32
    ).astype(BF16)
    dates = weight_ref.shape[0]
    high, low = split_bf16(weight_ref[...])
    span = rows // dates
    lane = iota((dates, rows), 1)
    owner = (lane // span == iota((dates, rows), 0)).astype(BF16)
    first = (lane % span < span // 2).astype(BF16)
    weights = lax.dot_general(high, owner * first, TN, preferred_element_type=F32)
    weights += lax.dot_general(low, owner * (1.0 - first), TN, preferred_element_type=F32)
    out[height:, :] = weights.astype(BF16)


def prep_kernel(devices, *refs):
    sources, rest = refs[:8], refs[8:]
    w_fwd, w_disc, onehot = rest[:3]
    params, (blocks_ref, set_ref, weights_ref, sems) = rest[3:8], rest[8:]
    fetch(list(zip(sources, (blocks_ref, set_ref, weights_ref) + tuple(params))), sems)
    tenors, trades = weights_ref.shape
    height = w_fwd.shape[0]
    blocks = height // tenors
    sets = onehot.shape[0]
    zero = jnp.zeros((tenors, LANES), F32)
    row = iota((16, LANES), 0)
    set_rows = pair_order(set_ref[...], sets // devices, devices)
    block_rows = cube_order(blocks_ref[...], blocks // devices, devices)
    for t in range(0, trades, LANES):
        lanes = slice(t, t + LANES)
        weights = weights_ref[:, lanes]
        for k, out in enumerate((w_fwd, w_disc)):
            ids = jnp.broadcast_to(block_rows[k : k + 1, lanes], (tenors, LANES))
            for b in range(blocks):
                out[b * tenors : (b + 1) * tenors, lanes] = jnp.where(
                    ids == b, weights, zero
                ).astype(BF16)
        ids = jnp.broadcast_to(set_rows[t // LANES : t // LANES + 1, :], (16, LANES))
        for n in range(0, sets, 16):
            onehot[n : n + 16, lanes] = jnp.where(ids == row + n, 1.0, 0.0).astype(BF16)


def joined_curves(ref, height, padded):
    parts = [ref[k : k + height, :] for k in range(0, ref.shape[0], padded)]
    return jnp.concatenate(parts, axis=0)


def param_row(ref, start, tile):
    return jnp.concatenate(
        [ref[j : j + 1, :] for j in range(start // LANES, (start + tile) // LANES)], axis=1
    )


def price_kernel(
    height, padded, gathered, w_fwd, w_disc, onehot, kind_ref, notional_ref, strike_ref, vol_ref,
    threshold_ref, keep, send, fwd_scale, ann_scale,
):
    rows = gathered.shape[1]
    trades = w_fwd.shape[1]
    half = keep.shape[0]
    tile = TILE if trades % TILE == 0 else trades
    curve = joined_curves(gathered, height, padded)
    discount = jnp.exp(-0.5 * curve.astype(F32)).astype(BF16)
    total = jnp.zeros((2 * half, rows), F32)
    for t in range(0, trades, tile):
        lanes = slice(t, t + tile)
        forward = lax.dot_general(curve, w_fwd[:, lanes], TN, preferred_element_type=F32)
        annuity = lax.dot_general(discount, w_disc[:, lanes], TN, preferred_element_type=F32)
        vol = param_row(vol_ref, t, tile)
        notional = param_row(notional_ref, t, tile)
        option = jnp.broadcast_to(param_row(kind_ref, t, tile) == 1, (rows, tile))
        moneyness = forward - param_row(strike_ref, t, tile)
        scaled = moneyness * (1.0 / vol)
        e = jnp.exp(-jnp.abs(scaled))
        softplus = jnp.maximum(scaled, 0.0) + log1p_unit(e)
        sigmoid = jnp.where(scaled >= 0.0, 1.0, e) / (1.0 + e)
        payoff = jnp.where(option, vol * softplus, moneyness)
        slope = jnp.where(option, sigmoid, 1.0)
        scaled_annuity = notional * annuity
        value = (scaled_annuity * payoff).astype(BF16)
        fwd_scale[:, lanes] = scaled_annuity * slope
        ann_scale[:, lanes] = notional * payoff
        total += lax.dot_general(onehot[:, lanes], value, NT, preferred_element_type=F32)
    keep[...] = total[:half]
    send[...] = total[half:].astype(BF16)
    sets = threshold_ref.shape[1]
    chip = lax.axis_index("trade") // 2
    own = pl.ds(pl.multiple_of(chip * sets, sets), sets)
    square = iota((sets, sets), 0) == iota((sets, sets), 1)
    column = jnp.sum(jnp.where(square, threshold_ref[...], 0.0), axis=1, keepdims=True)
    keep[own, :] = keep[own, :] - column


def sets_kernel(height, gathered, weight_ref, *refs):
    parts, (cots, cva, excess_ref) = refs[:-3], refs[-3:]
    dates, sets = weight_ref.shape
    padded = height + sets
    rows = gathered.shape[1]
    devices = gathered.shape[0] // padded
    me = lax.axis_index("trade")
    excess = parts[0][...].astype(F32)
    for part in parts[1:]:
        excess += part[...].astype(F32)
    excess_ref[...] = excess
    chunks = []
    for k in range(devices // 2):
        place = cube_place(2 * k + lax.rem(me, 2), devices)
        start = pl.multiple_of(place * padded + height, math.gcd(padded, height))
        chunks.append(gathered[pl.ds(start, sets), :])
    split = jnp.concatenate(chunks, axis=0).astype(F32)
    span = rows // dates
    lane = iota(split.shape, 1)
    other = jnp.where(
        lane % span < span // 2,
        pltpu.roll(split, rows - span // 2, 1),
        pltpu.roll(split, span // 2, 1),
    )
    e = jnp.exp(-jnp.abs(excess))
    sigmoid = jnp.where(excess >= 0.0, 1.0, e) / (1.0 + e)
    cots[...] = ((split + other) * sigmoid).astype(BF16)
    chip = me // 2
    own = excess_ref[pl.ds(pl.multiple_of(chip * sets, sets), sets), :]
    exposure = jnp.maximum(own, 0.0) + log1p_unit(jnp.exp(-jnp.abs(own)))
    square = iota((sets, sets), 0) == iota((sets, sets), 1)
    date = iota((sets, rows), 1) // span
    total = jnp.zeros((sets, 1), F32)
    for d in range(dates):
        weight = jnp.where(square, weight_ref[d : d + 1, :], 0.0)
        weight = jnp.sum(weight, axis=1, keepdims=True)
        total += weight * jnp.sum(jnp.where(date == d, exposure, 0.0), axis=1, keepdims=True)
    cva[...] = jnp.sum(jnp.where(square, total, 0.0), axis=0, keepdims=True)


def half_cot(height, padded, side, gathered, fwd_cots, ann_cots, w_fwd, w_disc):
    trades = w_fwd.shape[1]
    half = gathered.shape[0] // padded * height // 2
    tile = TILE if trades % TILE == 0 else trades
    band = slice(side * half, (side + 1) * half)
    from_fwd = from_disc = 0.0
    for t in range(0, trades, tile):
        lanes = slice(t, t + tile)
        from_fwd += lax.dot_general(
            w_fwd[band, lanes], fwd_cots[:, lanes], NT, preferred_element_type=F32
        )
        from_disc += lax.dot_general(
            w_disc[band, lanes], ann_cots[:, lanes], NT, preferred_element_type=F32
        )
    curve = joined_curves(gathered, height, padded)[band]
    return from_fwd - 0.5 * jnp.exp(-0.5 * curve.astype(F32)) * from_disc


def adjoint_kernel(
    height, padded, gathered, cots_mine, cots_partner, fwd_scale, ann_scale, w_fwd, w_disc,
    onehot, send, fwd_cots, ann_cots,
):
    trades = fwd_scale.shape[1]
    tile = TILE if trades % TILE == 0 else trades
    cots = jnp.concatenate([cots_mine[...], cots_partner[...]], axis=0)
    for t in range(0, trades, tile):
        lanes = slice(t, t + tile)
        trade_cot = lax.dot_general(cots, onehot[:, lanes], TN, preferred_element_type=F32)
        fwd_cots[:, lanes] = (trade_cot * fwd_scale[:, lanes]).astype(BF16)
        ann_cots[:, lanes] = (trade_cot * ann_scale[:, lanes]).astype(BF16)
    total = half_cot(height, padded, 1, gathered, fwd_cots, ann_cots, w_fwd, w_disc)
    send[...] = total.astype(BF16)


def keep_kernel(height, padded, gathered, fwd_cots, ann_cots, w_fwd, w_disc, keep):
    keep[...] = half_cot(height, padded, 0, gathered, fwd_cots, ann_cots, w_fwd, w_disc)


def fold_kernel(kept, arrived, keep, send):
    half = keep.shape[0]
    keep[...] = kept[:half, :] + arrived[:half, :].astype(F32)
    send[...] = (kept[half:, :] + arrived[half:, :].astype(F32)).astype(BF16)


def factor_kernel(kept, arrived, basis, out):
    total = kept[...] + arrived[...].astype(F32)
    dims = (((0,), (1,)), ((), ()))
    high, low = split_bf16(total)
    out[...] = lax.dot_general(high, basis[...], dims, preferred_element_type=F32)
    out[...] += lax.dot_general(low, basis[...], dims, preferred_element_type=F32)


def call(kernel, name, out_shape, scratch=(), flops=1_000_000, moved=1_000_000, space=VMEM):
    def run(*args):
        return pl.pallas_call(
            kernel,
            in_specs=[space] * len(args),
            out_specs=jax.tree.map(lambda _: VMEM, out_shape),
            out_shape=out_shape,
            scratch_shapes=scratch,
            cost_estimate=pl.CostEstimate(flops=flops, bytes_accessed=moved, transcendentals=0),
            compiler_params=pltpu.CompilerParams(vmem_limit_bytes=VMEM_LIMIT),
            name=name,
        )(*args)

    return run


def swap(x, mask):
    n = lax.axis_size("trade")
    return lax.ppermute(x, "trade", [(i, i ^ mask) for i in range(n)])


def sum_over(x, axis):
    n = lax.axis_size(axis)
    total = x
    for shift in range(1, n):
        total = total + lax.ppermute(x, axis, [(i, (i + shift) % n) for i in range(n)])
    return total


def shards(
    factor_paths, tenor_basis, trade_blocks, trade_set, trade_type, notional, strike,
    vol_level, cash_weights, set_threshold, date_weight,
):
    factor_rows, dates, paths = factor_paths.shape
    block_size, tenors = tenor_basis.shape
    rows = dates * paths
    devices = lax.axis_size("trade")
    local_blocks = factor_rows // block_size
    height = local_blocks * tenors
    local_sets = set_threshold.shape[0]
    padded = height + local_sets
    half_sets = local_sets * devices // 2
    all_rows = height * devices
    trades = trade_set.shape[0]
    shape = jax.ShapeDtypeStruct
    lane_rows = (trades // LANES, LANES)
    dma = pltpu.SemaphoreType.DMA

    factors = jnp.transpose(factor_paths, (1, 2, 0)).reshape(rows, factor_rows)
    gathered, basis, weights = call(
        curve_kernel, "curves",
        [shape((padded, rows), BF16), shape((factor_rows, height), BF16),
         shape((dates, local_sets), F32)],
        [pltpu.VMEM((rows, factor_rows), BF16), pltpu.VMEM((tenors, block_size), BF16), dma((3,))],
        space=HBM,
    )(factors, jnp.transpose(tenor_basis), jnp.transpose(date_weight))
    for k in reversed(range(bits_of(devices))):
        gathered = jnp.concatenate([gathered, swap(gathered, 1 << k)], axis=0)

    w_fwd, w_disc, onehot, *params = call(
        functools.partial(prep_kernel, devices), "prep",
        [shape((all_rows, trades), BF16)] * 2 + [shape((2 * half_sets, trades), BF16)]
        + [shape(lane_rows, jnp.int32)] + [shape(lane_rows, F32)] * 3 + [shape((1, local_sets), F32)],
        [pltpu.VMEM((2, trades), jnp.int32), pltpu.VMEM(lane_rows, jnp.int32),
         pltpu.VMEM((tenors, trades), F32), dma((8,))],
        flops=400_000_000, moved=8_000_000, space=HBM,
    )(
        trade_blocks, trade_set.reshape(lane_rows), cash_weights, trade_type.reshape(lane_rows),
        notional.reshape(lane_rows), strike.reshape(lane_rows), vol_level.reshape(lane_rows),
        set_threshold[None],
    )
    keep, send, fwd_scale, ann_scale = call(
        functools.partial(price_kernel, height, padded), "price",
        [shape((half_sets, rows), F32), shape((half_sets, rows), BF16),
         shape((rows, trades), F32), shape((rows, trades), F32)],
    )(gathered, w_fwd, w_disc, onehot, *params)

    total = (keep + swap(send, 1).astype(F32)).astype(BF16)
    bits = [1 << k for k in range(1, bits_of(devices))]
    steps = [bits[:1]] if len(bits) % 2 else []
    steps += [bits[k : k + 2] for k in range(len(bits) % 2, len(bits), 2)]
    for step in steps:
        masks = step if len(step) == 1 else [step[0], step[1], step[0] + step[1]]
        parts = [total] + [swap(total, mask) for mask in masks]
        if step is not steps[-1]:
            total = functools.reduce(jnp.add, [p.astype(F32) for p in parts]).astype(BF16)
    cots_mine, cva = call(
        functools.partial(sets_kernel, height), "sets",
        [shape((half_sets, rows), BF16), shape((1, local_sets), F32)],
        [pltpu.VMEM((half_sets, rows), F32)],
    )(gathered, weights, *parts)
    cots_partner = swap(cots_mine, 1)

    send, fwd_cots, ann_cots = call(
        functools.partial(adjoint_kernel, height, padded), "adjoint",
        [shape((all_rows // 2, rows), BF16)] + [shape((rows, trades), BF16)] * 2,
    )(gathered, cots_mine, cots_partner, fwd_scale, ann_scale, w_fwd, w_disc, onehot)
    keep = call(
        functools.partial(keep_kernel, height, padded), "keep", shape((all_rows // 2, rows), F32),
        flops=200_000_000, moved=4_000_000,
    )(gathered, fwd_cots, ann_cots, w_fwd, w_disc)
    arrived = swap(send, 1)
    for k in range(1, bits_of(devices)):
        size = all_rows >> (k + 1)
        keep, send = call(
            fold_kernel, f"fold{k}", [shape((size, rows), F32), shape((size, rows), BF16)]
        )(keep, arrived)
        arrived = swap(send, 1 << k)
    factor_cot = call(factor_kernel, "factors", shape((rows, factor_rows), F32))(
        keep, arrived, basis
    )
    factor_cot = jnp.transpose(factor_cot.reshape(dates, paths, factor_rows), (2, 0, 1))
    netting_cva = sum_over(cva[0], "path") / (paths * lax.axis_size("path"))
    return netting_cva, factor_cot


def solution(mesh):
    return jax.shard_map(
        shards,
        mesh=mesh,
        in_specs=(
            P("trade", None, "path"), P(), P(None, "trade"), P("trade"), P("trade"),
            P("trade"), P("trade"), P("trade"), P(None, "trade"), P("trade"),
            P("trade", None),
        ),
        out_specs=(P("trade"), P("trade", None, "path")),
        check_vma=False,
    )
```

time: 67.1 us -> 57.8 us (0.86)
  blocking collectives: 14.7 us -> 0 us
  waiting for transfers between devices: 11.9 us -> 21.1 us
  local copies, waits for them, and re-layouts: 16.5 us -> 7.91 us
  starting transfers between devices: 11.7 us -> 19.8 us
  other arithmetic: 3.09 us -> 0.56 us
    all_to_all x1 -> x0, blocking collectives: 14.7 us -> none  [chip_exchange(): return lax.all_to_all(x, 'trade', 0, 0, axis_index_groups=groups)]
    ppermute x8 -> x14, waiting for transfers between devices: 7.47 us -> 21.1 us  [swap(): return lax.ppermute(x, 'trade', [(i, i ^ mask) for i in range(n)])]
    ppermute x8 -> x14, starting transfers between devices: 6.17 us -> 18.3 us  [swap(): return lax.ppermute(x, 'trade', [(i, i ^ mask) for i in range(n)])]
    unnamed x45 -> x26, local copies, waits for them, and re-layouts: 16.4 us -> 7.89 us
    all_to_all x1 -> x0, starting transfers between devices: 3.97 us -> none  [chip_exchange(): return lax.all_to_all(x, 'trade', 0, 0, axis_index_groups=groups)]
    all_to_all x1 -> x0, waiting for transfers between devices: 2.39 us -> none  [chip_exchange(): return lax.all_to_all(x, 'trade', 0, 0, axis_index_groups=groups)]
    ppermute x1, waiting for transfers between devices: 2.08 us -> 0.01 us  [sum_over(): lax.ppermute(x, axis, [(i, (i + shift) % n) for i in range(n)])]
    convert_element_type x1 -> x0, other arithmetic: 1.63 us -> none  [shards(): pair = (keep + swap(send, 1).astype(F32)).astype(BF16)]
  transfers between devices with their start and end apart: 10 -> 15, of which waited for: 9 -> 12; matrix products, arithmetic and copies ran while one was open for 3% -> 1% of each run, Pallas kernels for 2% -> 5%
where the time goes in v3:
time: 57.8 us; the launch traced here: 57.2 us
  waiting for transfers between devices  21.1 us (37%)
  starting transfers between devices  19.8 us (34%)
  local copies, waits for them, and re-layouts  7.91 us (14%)
  Pallas kernels  7.12 us (12%)
  between operations  0.77 us (1%)
    ppermute x14, waiting for transfers between devices, swap(): return lax.ppermute(x, 'trade', [(i, i ^ mask) for i in range(n)])  21.1 us
    ppermute x14, starting transfers between devices, swap(): return lax.ppermute(x, 'trade', [(i, i ^ mask) for i in range(n)])  18.3 us
    unnamed x26, local copies, waits for them, and re-layouts  7.89 us
    pallas_call x10, Pallas kernels, run(): pl.pallas_call(kernel, in_specs=[space] * len(args), out_specs=jax.tree.m...  7.12 us
    ppermute x1, starting transfers between devices, sum_over(): lax.ppermute(x, axis, [(i, (i + shift) % n) for i in range(n)])  1.49 us
  transfers between devices with their start and end apart: 15, of which 12 were waited for; matrix products, arithmetic and copies ran while one was open for 1% of the time, Pallas kernels for 5%

profile of v3, /device:TPU:0, one launch (start us, length us, event | category | flops | bytes accessed | tf_op | source)
XLA Modules:
  0.0 57.2 jit_solution(6921968852160111017)
XLA Ops:
  3.2 4.1 %collective-permute-start = (bf16[80,128]{1,0:T(8,128)(2,1)S(1)}, bf16[80,128]{1,0:T(8,128)(2,1)S(1)}, u32[]{:S(2)}, u32[]{:S(2)}) collective-permute-start(bf16[80,128]{1,0:T(8,128)(2,1)S(1)} %get-tuple-element.28), channel_id=1, source_target_pairs={{0,8},{1,9},{2,10},{3,11},{4,12},{5,13},{6,14},{7,15},{8,0},{9,1},... | collective-permute-start | bytes 61448 | tf_op jit(solution)/shard_map/ppermute | solution.py:293
  7.4 1.8 %collective-permute-done = bf16[80,128]{1,0:T(8,128)(2,1)S(1)} collective-permute-done((bf16[80,128]{1,0:T(8,128)(2,1)S(1)}, bf16[80,128]{1,0:T(8,128)(2,1)S(1)}, u32[]{:S(2)}, u32[]{:S(2)}) %collective-permute-start) | collective-permute-done | bytes 20512 | tf_op jit(solution)/shard_map/ppermute | solution.py:293
  9.1 1.9 %collective-permute-start.1 = (bf16[160,128]{1,0:T(8,128)(2,1)S(1)}, bf16[160,128]{1,0:T(8,128)(2,1)S(1)}, u32[]{:S(2)}, u32[]{:S(2)}) collective-permute-start(bf16[160,128]{1,0:T(8,128)(2,1)S(1)} %pad_maximum_fusion.2), channel_id=1, source_target_pairs={{0,4},{1,5},{2,6},{3,7},{4,0},{5,1},{6,2},{7,3},{8,12},{9,13},{10,... | collective-permute-start | bytes 122888 | tf_op jit(solution)/shard_map/ppermute | solution.py:293
  16.8 1.6 %prep.1 = (bf16[1024,1536]{1,0:T(8,128)(2,1)S(1)}, bf16[1024,1536]{1,0:T(8,128)(2,1)S(1)}, bf16[256,1536]{1,0:T(8,128)(2,1)S(1)}, s32[12,128]{1,0:T(8,128)S(1)},...) custom-call(s32[2,1536]{1,0:T(2,128)S(1)} %copy-done.4, ...), custom_call_target="tpu_custom_call" | custom-call | flops 400000000 | bytes 8000000 | tf_op jit(solution)/shard_map/prep/pallas_call | solution.py:277
  18.4 1.6 %collective-permute-start.2 = (bf16[320,128]{1,0:T(8,128)(2,1)S(1)}, bf16[320,128]{1,0:T(8,128)(2,1)S(1)}, u32[]{:S(2)}, u32[]{:S(2)}) collective-permute-start(bf16[320,128]{1,0:T(8,128)(2,1)S(1)} %pad_maximum_fusion.1), channel_id=1, source_target_pairs={{0,2},{1,3},{2,0},{3,1},{4,6},{5,7},{6,4},{7,5},{8,10},{9,11},{10,... | collective-permute-start | bytes 245768 | tf_op jit(solution)/shard_map/ppermute | solution.py:293
  20.0 2.9 %collective-permute-done.2 = bf16[320,128]{1,0:T(8,128)(2,1)S(1)} collective-permute-done((bf16[320,128]{1,0:T(8,128)(2,1)S(1)}, bf16[320,128]{1,0:T(8,128)(2,1)S(1)}, u32[]{:S(2)}, u32[]{:S(2)}) %collective-permute-start.2) | collective-permute-done | bytes 81952 | tf_op jit(solution)/shard_map/ppermute | solution.py:293
  23.1 1.3 %collective-permute-done.3 = bf16[640,128]{1,0:T(8,128)(2,1)S(1)} collective-permute-done((bf16[640,128]{1,0:T(8,128)(2,1)S(1)}, bf16[640,128]{1,0:T(8,128)(2,1)S(1)}, u32[]{:S(2)}, u32[]{:S(2)}) %collective-permute-start.3) | collective-permute-done | bytes 163872 | tf_op jit(solution)/shard_map/ppermute | solution.py:293
  24.5 1.8 %price.1 = (f32[128,128]{1,0:T(8,128)S(1)}, bf16[128,128]{1,0:T(8,128)(2,1)S(1)}, f32[128,1536]{1,0:T(8,128)S(1)}, f32[128,1536]{1,0:T(8,128)S(1)}) custom-call(bf16[1280,128]{1,0:T(8,128)(2,1)S(1)} %constant_dynamic-update-slice_fusion.gathered, bf16[1024,1536]{1,0:T(8,128)(2,1)S(1)} %get-tuple-element.30.w_fwd, ...), custom_call_target="tpu_custom_call" | custom-call | flops 1000000 | bytes 1000000 | tf_op jit(solution)/shard_map/price/pallas_call | solution.py:277
  26.5 1.1 %collective-permute-done.4 = bf16[128,128]{1,0:T(8,128)(2,1)S(1)} collective-permute-done((bf16[128,128]{1,0:T(8,128)(2,1)S(1)}, bf16[128,128]{1,0:T(8,128)(2,1)S(1)}, u32[]{:S(2)}, u32[]{:S(2)}) %collective-permute-start.4) | collective-permute-done | bytes 32800 | tf_op jit(solution)/shard_map/ppermute | solution.py:293
  27.5 1.6 %collective-permute-start.5 = (bf16[128,128]{1,0:T(8,128)(2,1)S(1)}, bf16[128,128]{1,0:T(8,128)(2,1)S(1)}, u32[]{:S(2)}, u32[]{:S(2)}) collective-permute-start(bf16[128,128]{1,0:T(8,128)(2,1)S(1)} %add_convert_fusion.1), channel_id=1, source_target_pairs={{0,2},{1,3},{2,0},{3,1},{4,6},{5,7},{6,4},{7,5},{8,10},{9,11},{10,... | collective-permute-start | bytes 98312 | tf_op jit(solution)/shard_map/ppermute | solution.py:293
  29.1 2.4 %collective-permute-done.5 = bf16[128,128]{1,0:T(8,128)(2,1)S(1)} collective-permute-done((bf16[128,128]{1,0:T(8,128)(2,1)S(1)}, bf16[128,128]{1,0:T(8,128)(2,1)S(1)}, u32[]{:S(2)}, u32[]{:S(2)}) %collective-permute-start.5) | collective-permute-done | bytes 32800 | tf_op jit(solution)/shard_map/ppermute | solution.py:293
  31.5 2.5 %collective-permute-start.8 = (bf16[128,128]{1,0:T(8,128)(2,1)S(1)}, bf16[128,128]{1,0:T(8,128)(2,1)S(1)}, u32[]{:S(2)}, u32[]{:S(2)}) collective-permute-start(bf16[128,128]{1,0:T(8,128)(2,1)S(1)} %add_convert_fusion.refs_0_), channel_id=1, source_target_pairs={{0,12},{1,13},{2,14},{3,15},{4,8},{5,9},{6,10},{7,11},{8,4},{9,5},... | collective-permute-start | bytes 98312 | tf_op jit(solution)/shard_map/ppermute | solution.py:293
  34.4 1.6 %collective-permute-start.6 = (bf16[128,128]{1,0:T(8,128)(2,1)S(1)}, bf16[128,128]{1,0:T(8,128)(2,1)S(1)}, u32[]{:S(2)}, u32[]{:S(2)}) collective-permute-start(bf16[128,128]{1,0:T(8,128)(2,1)S(1)} %add_convert_fusion.refs_0_), channel_id=1, source_target_pairs={{0,4},{1,5},{2,6},{3,7},{4,0},{5,1},{6,2},{7,3},{8,12},{9,13},{10,... | collective-permute-start | bytes 98312 | tf_op jit(solution)/shard_map/ppermute | solution.py:293
  36.0 1.3 %collective-permute-done.8.refs_3_ = bf16[128,128]{1,0:T(8,128)(2,1)S(1)} collective-permute-done((bf16[128,128]{1,0:T(8,128)(2,1)S(1)}, bf16[128,128]{1,0:T(8,128)(2,1)S(1)}, u32[]{:S(2)}, u32[]{:S(2)}) %collective-permute-start.8) | collective-permute-done | bytes 32800 | tf_op jit(solution)/shard_map/ppermute | solution.py:293
  37.3 1.9 %collective-permute-done.7.refs_2_ = bf16[128,128]{1,0:T(8,128)(2,1)S(1)} collective-permute-done((bf16[128,128]{1,0:T(8,128)(2,1)S(1)}, bf16[128,128]{1,0:T(8,128)(2,1)S(1)}, u32[]{:S(2)}, u32[]{:S(2)}) %collective-permute-start.7) | collective-permute-done | bytes 32800 | tf_op jit(solution)/shard_map/ppermute | solution.py:293
  39.5 1.2 %collective-permute-done.10.cots_partner = bf16[128,128]{1,0:T(8,128)(2,1)S(1)} collective-permute-done((bf16[128,128]{1,0:T(8,128)(2,1)S(1)}, bf16[128,128]{1,0:T(8,128)(2,1)S(1)}, u32[]{:S(2)}, u32[]{:S(2)}) %collective-permute-start.10) | collective-permute-done | bytes 32800 | tf_op jit(solution)/shard_map/ppermute | solution.py:293
  40.7 1.2 %adjoint.1 = (bf16[512,128]{1,0:T(8,128)(2,1)S(1)}, bf16[128,1536]{1,0:T(8,128)(2,1)S(1)}, bf16[128,1536]{1,0:T(8,128)(2,1)S(1)}) custom-call(bf16[1280,128]{1,0:T(8,128)(2,1)S(1)} %constant_dynamic-update-slice_fusion.gathered, bf16[128,128]{1,0:T(8,128)(2,1)S(1)} %get-tuple-element.41.cots_mine, bf16[128,128]{1,0:T(8,128)(2,1)S(1)} %collective-permute-done.10.cots_partner, ...), custom_call_target="tpu_custom_call" | custom-call | flops 1000000 | bytes 1000000 | tf_op jit(solution)/shard_map/adjoint/pallas_call | solution.py:277
  42.1 1.0 %keep.1.kept = f32[512,128]{1,0:T(8,128)S(1)} custom-call(bf16[1280,128]{1,0:T(8,128)(2,1)S(1)} %constant_dynamic-update-slice_fusion.gathered, bf16[128,1536]{1,0:T(8,128)(2,1)S(1)} %get-tuple-element.44.fwd_cots, bf16[128,1536]{1,0:T(8,128)(2,1)S(1)} %get-tuple-element.45.ann_cots, bf16[1024,1536]{1,0:T(8,128)(2,1)S(1)} %get-tuple-element.30.w_fwd, ...), custom_call_target="tpu_custom_call" | custom-call | flops 200000000 | bytes 4000000 | tf_op jit(solution)/shard_map/keep/pallas_call | solution.py:277
  43.4 1.6 %collective-permute-start.12 = (bf16[256,128]{1,0:T(8,128)(2,1)S(1)}, bf16[256,128]{1,0:T(8,128)(2,1)S(1)}, u32[]{:S(2)}, u32[]{:S(2)}) collective-permute-start(bf16[256,128]{1,0:T(8,128)(2,1)S(1)} %get-tuple-element.48), channel_id=1, source_target_pairs={{0,2},{1,3},{2,0},{3,1},{4,6},{5,7},{6,4},{7,5},{8,10},{9,11},{10,... | collective-permute-start | bytes 196616 | tf_op jit(solution)/shard_map/ppermute | solution.py:293
  44.9 2.7 %collective-permute-done.12.arrived = bf16[256,128]{1,0:T(8,128)(2,1)S(1)} collective-permute-done((bf16[256,128]{1,0:T(8,128)(2,1)S(1)}, bf16[256,128]{1,0:T(8,128)(2,1)S(1)}, u32[]{:S(2)}, u32[]{:S(2)}) %collective-permute-start.12) | collective-permute-done | bytes 65568 | tf_op jit(solution)/shard_map/ppermute | solution.py:293
  48.4 1.5 %collective-permute-start.9 = (f32[16]{0:T(128)S(1)}, f32[16]{0:T(128)S(1)}, u32[]{:S(2)}, u32[]{:S(2)}) collective-permute-start(f32[16]{0:T(128)S(1)} %bitcast.25), channel_id=1, source_target_pairs={{0,16},{16,0},{1,17},{17,1},{2,18},{18,2},{3,19},{19,3},{4,20},{20... | collective-permute-start | bytes 200 | tf_op jit(solution)/shard_map/ppermute | solution.py:300
  49.9 1.8 %collective-permute-done.13.arrived = bf16[128,128]{1,0:T(8,128)(2,1)S(1)} collective-permute-done((bf16[128,128]{1,0:T(8,128)(2,1)S(1)}, bf16[128,128]{1,0:T(8,128)(2,1)S(1)}, u32[]{:S(2)}, u32[]{:S(2)}) %collective-permute-start.13) | collective-permute-done | bytes 32800 | tf_op jit(solution)/shard_map/ppermute | solution.py:293
  51.7 1.7 %collective-permute-start.14 = (bf16[64,128]{1,0:T(8,128)(2,1)S(1)}, bf16[64,128]{1,0:T(8,128)(2,1)S(1)}, u32[]{:S(2)}, u32[]{:S(2)}) collective-permute-start(bf16[64,128]{1,0:T(8,128)(2,1)S(1)} %get-tuple-element.52), channel_id=1, source_target_pairs={{0,8},{1,9},{2,10},{3,11},{4,12},{5,13},{6,14},{7,15},{8,0},{9,1},... | collective-permute-start | bytes 49160 | tf_op jit(solution)/shard_map/ppermute | solution.py:293
  54.0 2.5 %collective-permute-done.14.arrived = bf16[64,128]{1,0:T(8,128)(2,1)S(1)} collective-permute-done((bf16[64,128]{1,0:T(8,128)(2,1)S(1)}, bf16[64,128]{1,0:T(8,128)(2,1)S(1)}, u32[]{:S(2)}, u32[]{:S(2)}) %collective-permute-start.14) | collective-permute-done | bytes 16416 | tf_op jit(solution)/shard_map/ppermute | solution.py:293
  (49 shorter events, 11.8 us)
Async XLA Ops:
  0.6 0.8 %copy-start = (bf16[128,2,64]{0,2,1:T(8,128)(2,1)S(1)}, bf16[128,2,64]{0,2,1:T(8,128)(2,1)}, u32[]{:S(2)}) copy-start(bf16[128,2,64]{0,2,1:T(8,128)(2,1)} %param.11) | copy-start | bytes 98308
  1.4 0.7 %copy-start.1 = (bf16[32,16]{0,1:T(8,128)(2,1)S(1)}, bf16[32,16]{0,1:T(8,128)(2,1)}, u32[]{:S(2)}) copy-start(bf16[32,16]{0,1:T(8,128)(2,1)} %param.12) | copy-start | bytes 3076
  3.2 5.9 %collective-permute-start = (bf16[80,128]{1,0:T(8,128)(2,1)S(1)}, bf16[80,128]{1,0:T(8,128)(2,1)S(1)}, u32[]{:S(2)}, u32[]{:S(2)}) collective-permute-start(bf16[80,128]{1,0:T(8,128)(2,1)S(1)} %get-tuple-element.28), channel_id=1, source_target_pairs={{0,8},{1,9},{2,10},{3,11},{4,12},{5,13},{6,14},{7,15},{8,0},{9,1},... | collective-permute-start | bytes 61448 | tf_op jit(solution)/shard_map/ppermute | solution.py:293
  9.1 9.3 %collective-permute-start.1 = (bf16[160,128]{1,0:T(8,128)(2,1)S(1)}, bf16[160,128]{1,0:T(8,128)(2,1)S(1)}, u32[]{:S(2)}, u32[]{:S(2)}) collective-permute-start(bf16[160,128]{1,0:T(8,128)(2,1)S(1)} %pad_maximum_fusion.2), channel_id=1, source_target_pairs={{0,4},{1,5},{2,6},{3,7},{4,0},{5,1},{6,2},{7,3},{8,12},{9,13},{10,... | collective-permute-start | bytes 122888 | tf_op jit(solution)/shard_map/ppermute | solution.py:293
  11.0 0.9 %copy-start.3 = (f32[16,1536]{1,0:T(8,128)S(1)}, f32[16,1536]{1,0:T(8,128)}, u32[]{:S(2)}) copy-start(f32[16,1536]{1,0:T(8,128)} %refs_2_.1) | copy-start | bytes 294916
  11.9 0.7 %copy-start.4 = (s32[2,1536]{1,0:T(2,128)S(1)}, s32[2,1536]{1,0:T(2,128)}, u32[]{:S(2)}) copy-start(s32[2,1536]{1,0:T(2,128)} %refs_0_.1) | copy-start | bytes 36868
  12.6 0.7 %copy-start.5 = (s32[1536]{0:T(1024)S(1)}, s32[1536]{0:T(1024)}, u32[]{:S(2)}) copy-start(s32[1536]{0:T(1024)} %param.14) | copy-start | bytes 18436
  13.3 0.7 %copy-start.6 = (s32[1536]{0:T(1024)S(1)}, s32[1536]{0:T(1024)}, u32[]{:S(2)}) copy-start(s32[1536]{0:T(1024)} %param.15) | copy-start | bytes 18436
  14.0 0.7 %copy-start.7 = (f32[1536]{0:T(1024)S(1)}, f32[1536]{0:T(1024)}, u32[]{:S(2)}) copy-start(f32[1536]{0:T(1024)} %param.16) | copy-start | bytes 18436
  14.7 0.7 %copy-start.8 = (f32[1536]{0:T(1024)S(1)}, f32[1536]{0:T(1024)}, u32[]{:S(2)}) copy-start(f32[1536]{0:T(1024)} %param.17) | copy-start | bytes 18436
  15.4 0.7 %copy-start.9 = (f32[1536]{0:T(1024)S(1)}, f32[1536]{0:T(1024)}, u32[]{:S(2)}) copy-start(f32[1536]{0:T(1024)} %param.18) | copy-start | bytes 18436
  18.4 4.5 %collective-permute-start.2 = (bf16[320,128]{1,0:T(8,128)(2,1)S(1)}, bf16[320,128]{1,0:T(8,128)(2,1)S(1)}, u32[]{:S(2)}, u32[]{:S(2)}) collective-permute-start(bf16[320,128]{1,0:T(8,128)(2,1)S(1)} %pad_maximum_fusion.1), channel_id=1, source_target_pairs={{0,2},{1,3},{2,0},{3,1},{4,6},{5,7},{6,4},{7,5},{8,10},{9,11},{10,... | collective-permute-start | bytes 245768 | tf_op jit(solution)/shard_map/ppermute | solution.py:293
  23.0 1.5 %collective-permute-start.3 = (bf16[640,128]{1,0:T(8,128)(2,1)S(1)}, bf16[640,128]{1,0:T(8,128)(2,1)S(1)}, u32[]{:S(2)}, u32[]{:S(2)}) collective-permute-start(bf16[640,128]{1,0:T(8,128)(2,1)S(1)} %pad_maximum_fusion), channel_id=1, source_target_pairs={{0,1},{1,0},{2,3},{3,2},{4,5},{5,4},{6,7},{7,6},{8,9},{9,8},{10,11... | collective-permute-start | bytes 491528 | tf_op jit(solution)/shard_map/ppermute | solution.py:293
  26.2 1.3 %collective-permute-start.4 = (bf16[128,128]{1,0:T(8,128)(2,1)S(1)}, bf16[128,128]{1,0:T(8,128)(2,1)S(1)}, u32[]{:S(2)}, u32[]{:S(2)}) collective-permute-start(bf16[128,128]{1,0:T(8,128)(2,1)S(1)} %get-tuple-element.39), channel_id=1, source_target_pairs={{0,1},{1,0},{2,3},{3,2},{4,5},{5,4},{6,7},{7,6},{8,9},{9,8},{10,11... | collective-permute-start | bytes 98312 | tf_op jit(solution)/shard_map/ppermute | solution.py:293
  27.5 4.0 %collective-permute-start.5 = (bf16[128,128]{1,0:T(8,128)(2,1)S(1)}, bf16[128,128]{1,0:T(8,128)(2,1)S(1)}, u32[]{:S(2)}, u32[]{:S(2)}) collective-permute-start(bf16[128,128]{1,0:T(8,128)(2,1)S(1)} %add_convert_fusion.1), channel_id=1, source_target_pairs={{0,2},{1,3},{2,0},{3,1},{4,6},{5,7},{6,4},{7,5},{8,10},{9,11},{10,... | collective-permute-start | bytes 98312 | tf_op jit(solution)/shard_map/ppermute | solution.py:293
  31.5 5.8 %collective-permute-start.8 = (bf16[128,128]{1,0:T(8,128)(2,1)S(1)}, bf16[128,128]{1,0:T(8,128)(2,1)S(1)}, u32[]{:S(2)}, u32[]{:S(2)}) collective-permute-start(bf16[128,128]{1,0:T(8,128)(2,1)S(1)} %add_convert_fusion.refs_0_), channel_id=1, source_target_pairs={{0,12},{1,13},{2,14},{3,15},{4,8},{5,9},{6,10},{7,11},{8,4},{9,5},... | collective-permute-start | bytes 98312 | tf_op jit(solution)/shard_map/ppermute | solution.py:293
  34.1 5.2 %collective-permute-start.7 = (bf16[128,128]{1,0:T(8,128)(2,1)S(1)}, bf16[128,128]{1,0:T(8,128)(2,1)S(1)}, u32[]{:S(2)}, u32[]{:S(2)}) collective-permute-start(bf16[128,128]{1,0:T(8,128)(2,1)S(1)} %add_convert_fusion.refs_0_), channel_id=1, source_target_pairs={{0,8},{1,9},{2,10},{3,11},{4,12},{5,13},{6,14},{7,15},{8,0},{9,1},... | collective-permute-start | bytes 98312 | tf_op jit(solution)/shard_map/ppermute | solution.py:293
  34.4 4.9 %collective-permute-start.6 = (bf16[128,128]{1,0:T(8,128)(2,1)S(1)}, bf16[128,128]{1,0:T(8,128)(2,1)S(1)}, u32[]{:S(2)}, u32[]{:S(2)}) collective-permute-start(bf16[128,128]{1,0:T(8,128)(2,1)S(1)} %add_convert_fusion.refs_0_), channel_id=1, source_target_pairs={{0,4},{1,5},{2,6},{3,7},{4,0},{5,1},{6,2},{7,3},{8,12},{9,13},{10,... | collective-permute-start | bytes 98312 | tf_op jit(solution)/shard_map/ppermute | solution.py:293
  39.4 1.3 %collective-permute-start.10 = (bf16[128,128]{1,0:T(8,128)(2,1)S(1)}, bf16[128,128]{1,0:T(8,128)(2,1)S(1)}, u32[]{:S(2)}, u32[]{:S(2)}) collective-permute-start(bf16[128,128]{1,0:T(8,128)(2,1)S(1)} %get-tuple-element.41.cots_mine), channel_id=1, source_target_pairs={{0,1},{1,0},{2,3},{3,2},{4,5},{5,4},{6,7},{7,6},{8,9},{9,8},{10,11... | collective-permute-start | bytes 98312 | tf_op jit(solution)/shard_map/ppermute | solution.py:293
  41.9 1.4 %collective-permute-start.11 = (bf16[512,128]{1,0:T(8,128)(2,1)S(1)}, bf16[512,128]{1,0:T(8,128)(2,1)S(1)}, u32[]{:S(2)}, u32[]{:S(2)}) collective-permute-start(bf16[512,128]{1,0:T(8,128)(2,1)S(1)} %get-tuple-element.46), channel_id=1, source_target_pairs={{0,1},{1,0},{2,3},{3,2},{4,5},{5,4},{6,7},{7,6},{8,9},{9,8},{10,11... | collective-permute-start | bytes 393224 | tf_op jit(solution)/shard_map/ppermute | solution.py:293
  43.4 4.3 %collective-permute-start.12 = (bf16[256,128]{1,0:T(8,128)(2,1)S(1)}, bf16[256,128]{1,0:T(8,128)(2,1)S(1)}, u32[]{:S(2)}, u32[]{:S(2)}) collective-permute-start(bf16[256,128]{1,0:T(8,128)(2,1)S(1)} %get-tuple-element.48), channel_id=1, source_target_pairs={{0,2},{1,3},{2,0},{3,1},{4,6},{5,7},{6,4},{7,5},{8,10},{9,11},{10,... | collective-permute-start | bytes 196616 | tf_op jit(solution)/shard_map/ppermute | solution.py:293
  47.7 4.0 %collective-permute-start.13 = (bf16[128,128]{1,0:T(8,128)(2,1)S(1)}, bf16[128,128]{1,0:T(8,128)(2,1)S(1)}, u32[]{:S(2)}, u32[]{:S(2)}) collective-permute-start(bf16[128,128]{1,0:T(8,128)(2,1)S(1)} %get-tuple-element.50), channel_id=1, source_target_pairs={{0,4},{1,5},{2,6},{3,7},{4,0},{5,1},{6,2},{7,3},{8,12},{9,13},{10,... | collective-permute-start | bytes 98312 | tf_op jit(solution)/shard_map/ppermute | solution.py:293
  48.4 5.0 %collective-permute-start.9 = (f32[16]{0:T(128)S(1)}, f32[16]{0:T(128)S(1)}, u32[]{:S(2)}, u32[]{:S(2)}) collective-permute-start(f32[16]{0:T(128)S(1)} %bitcast.25), channel_id=1, source_target_pairs={{0,16},{16,0},{1,17},{17,1},{2,18},{18,2},{3,19},{19,3},{4,20},{20... | collective-permute-start | bytes 200 | tf_op jit(solution)/shard_map/ppermute | solution.py:300
  51.7 4.7 %collective-permute-start.14 = (bf16[64,128]{1,0:T(8,128)(2,1)S(1)}, bf16[64,128]{1,0:T(8,128)(2,1)S(1)}, u32[]{:S(2)}, u32[]{:S(2)}) collective-permute-start(bf16[64,128]{1,0:T(8,128)(2,1)S(1)} %get-tuple-element.52), channel_id=1, source_target_pairs={{0,8},{1,9},{2,10},{3,11},{4,12},{5,13},{6,14},{7,15},{8,0},{9,1},... | collective-permute-start | bytes 49160 | tf_op jit(solution)/shard_map/ppermute | solution.py:293
  (2 other events, 1.3 us)

commit v4 on v3

--- a/solution.py
+++ b/solution.py
@@ -272,8 +272,13 @@
     out[...] += lax.dot_general(low, basis[...], dims, preferred_element_type=F32)
 
 
-def call(kernel, name, out_shape, scratch=(), flops=1_000_000, moved=1_000_000, space=VMEM):
+def call(
+    kernel, name, out_shape, scratch=(), flops=1_000_000, moved=1_000_000, space=VMEM,
+    limit=VMEM_LIMIT,
+):
     def run(*args):
+        if space is HBM:
+            args = [pltpu.with_memory_space_constraint(x, pltpu.HBM) for x in args]
         return pl.pallas_call(
             kernel,
             in_specs=[space] * len(args),
@@ -281,7 +286,7 @@
             out_shape=out_shape,
             scratch_shapes=scratch,
             cost_estimate=pl.CostEstimate(flops=flops, bytes_accessed=moved, transcendentals=0),
-            compiler_params=pltpu.CompilerParams(vmem_limit_bytes=VMEM_LIMIT),
+            compiler_params=pltpu.CompilerParams(vmem_limit_bytes=limit),
             name=name,
         )(*args)
 

time: 57.8 us -> 51.9 us (0.90)
  local copies, waits for them, and re-layouts: 7.91 us -> 0.06 us
  Pallas kernels: 7.12 us -> 8.64 us
  waiting for transfers between devices: 21.1 us -> 21.9 us
    unnamed x26 -> x4, local copies, waits for them, and re-layouts: 7.89 us -> 0.04 us
    pallas_call x10, Pallas kernels: 7.12 us -> 8.64 us  [run(): pl.pallas_call(kernel, in_specs=[space] * len(args), out_specs=jax.tree.m...]
    ppermute x14, waiting for transfers between devices: 21.1 us -> 21.9 us  [swap(): return lax.ppermute(x, 'trade', [(i, i ^ mask) for i in range(n)])]
  transfers between devices with their start and end apart: 15 -> 15, of which waited for: 12 -> 12; matrix products, arithmetic and copies ran while one was open for 1% -> 1% of each run, Pallas kernels for 5% -> 7%
where the time goes in v4:
time: 51.9 us; the launch traced here: 51.7 us
  waiting for transfers between devices  21.9 us (42%)
  starting transfers between devices  19.8 us (38%)
  Pallas kernels  8.64 us (17%)
  between operations  0.76 us (1%)
  other arithmetic  0.56 us (1%)
    ppermute x14, waiting for transfers between devices, swap(): return lax.ppermute(x, 'trade', [(i, i ^ mask) for i in range(n)])  21.9 us
    ppermute x14, starting transfers between devices, swap(): return lax.ppermute(x, 'trade', [(i, i ^ mask) for i in range(n)])  18.2 us
    pallas_call x10, Pallas kernels, run(): pl.pallas_call(kernel, in_specs=[space] * len(args), out_specs=jax.tree.m...  8.64 us
    ppermute x1, starting transfers between devices, sum_over(): lax.ppermute(x, axis, [(i, (i + shift) % n) for i in range(n)])  1.55 us
  transfers between devices with their start and end apart: 15, of which 12 were waited for; matrix products, arithmetic and copies ran while one was open for 1% of the time, Pallas kernels for 7%

profile of v4, /device:TPU:0, one launch (start us, length us, event | category | flops | bytes accessed | tf_op | source)
XLA Modules:
  0.0 51.7 jit_solution(2734266091861690642)
XLA Ops:
  0.6 1.2 %curves.1 = (bf16[80,128]{1,0:T(8,128)(2,1)S(1)}, bf16[128,64]{1,0:T(8,128)(2,1)S(1)}, f32[2,16]{1,0:T(2,128)S(1)}) custom-call(bf16[128,128]{1,0:T(8,128)(2,1)} %bitcast.18, bf16[16,32]{1,0:T(8,128)(2,1)} %bitcast.19, f32[2,16]{1,0:T(2,128)} %bitcast.20), custom_call_target="tpu_custom_call" | custom-call | flops 1000000 | bytes 1000000 | tf_op jit(solution)/shard_map/curves/pallas_call | solution.py:282
  1.8 4.1 %collective-permute-start = (bf16[80,128]{1,0:T(8,128)(2,1)S(1)}, bf16[80,128]{1,0:T(8,128)(2,1)S(1)}, u32[]{:S(2)}, u32[]{:S(2)}) collective-permute-start(bf16[80,128]{1,0:T(8,128)(2,1)S(1)} %get-tuple-element.28), channel_id=1, source_target_pairs={{0,8},{1,9},{2,10},{3,11},{4,12},{5,13},{6,14},{7,15},{8,0},{9,1},... | collective-permute-start | bytes 61448 | tf_op jit(solution)/shard_map/ppermute | solution.py:298
  6.0 1.8 %collective-permute-done = bf16[80,128]{1,0:T(8,128)(2,1)S(1)} collective-permute-done((bf16[80,128]{1,0:T(8,128)(2,1)S(1)}, bf16[80,128]{1,0:T(8,128)(2,1)S(1)}, u32[]{:S(2)}, u32[]{:S(2)}) %collective-permute-start) | collective-permute-done | bytes 20512 | tf_op jit(solution)/shard_map/ppermute | solution.py:298
  7.8 1.9 %collective-permute-start.1 = (bf16[160,128]{1,0:T(8,128)(2,1)S(1)}, bf16[160,128]{1,0:T(8,128)(2,1)S(1)}, u32[]{:S(2)}, u32[]{:S(2)}) collective-permute-start(bf16[160,128]{1,0:T(8,128)(2,1)S(1)} %pad_maximum_fusion.2), channel_id=1, source_target_pairs={{0,4},{1,5},{2,6},{3,7},{4,0},{5,1},{6,2},{7,3},{8,12},{9,13},{10,... | collective-permute-start | bytes 122888 | tf_op jit(solution)/shard_map/ppermute | solution.py:298
  9.6 2.4 %prep.1 = (bf16[1024,1536]{1,0:T(8,128)(2,1)S(1)}, bf16[1024,1536]{1,0:T(8,128)(2,1)S(1)}, bf16[256,1536]{1,0:T(8,128)(2,1)S(1)}, s32[12,128]{1,0:T(8,128)S(1)},...) custom-call(s32[2,1536]{1,0:T(2,128)} %refs_0_.1, ...), custom_call_target="tpu_custom_call" | custom-call | flops 400000000 | bytes 8000000 | tf_op jit(solution)/shard_map/prep/pallas_call | solution.py:282
  12.1 1.6 %collective-permute-start.2 = (bf16[320,128]{1,0:T(8,128)(2,1)S(1)}, bf16[320,128]{1,0:T(8,128)(2,1)S(1)}, u32[]{:S(2)}, u32[]{:S(2)}) collective-permute-start(bf16[320,128]{1,0:T(8,128)(2,1)S(1)} %pad_maximum_fusion.1), channel_id=1, source_target_pairs={{0,2},{1,3},{2,0},{3,1},{4,6},{5,7},{6,4},{7,5},{8,10},{9,11},{10,... | collective-permute-start | bytes 245768 | tf_op jit(solution)/shard_map/ppermute | solution.py:298
  13.7 2.9 %collective-permute-done.2 = bf16[320,128]{1,0:T(8,128)(2,1)S(1)} collective-permute-done((bf16[320,128]{1,0:T(8,128)(2,1)S(1)}, bf16[320,128]{1,0:T(8,128)(2,1)S(1)}, u32[]{:S(2)}, u32[]{:S(2)}) %collective-permute-start.2) | collective-permute-done | bytes 81952 | tf_op jit(solution)/shard_map/ppermute | solution.py:298
  16.7 1.3 %collective-permute-done.3 = bf16[640,128]{1,0:T(8,128)(2,1)S(1)} collective-permute-done((bf16[640,128]{1,0:T(8,128)(2,1)S(1)}, bf16[640,128]{1,0:T(8,128)(2,1)S(1)}, u32[]{:S(2)}, u32[]{:S(2)}) %collective-permute-start.3) | collective-permute-done | bytes 163872 | tf_op jit(solution)/shard_map/ppermute | solution.py:298
  18.1 1.8 %price.1 = (f32[128,128]{1,0:T(8,128)S(1)}, bf16[128,128]{1,0:T(8,128)(2,1)S(1)}, f32[128,1536]{1,0:T(8,128)S(1)}, f32[128,1536]{1,0:T(8,128)S(1)}) custom-call(bf16[1280,128]{1,0:T(8,128)(2,1)S(1)} %constant_dynamic-update-slice_fusion.gathered, bf16[1024,1536]{1,0:T(8,128)(2,1)S(1)} %get-tuple-element.30.w_fwd, ...), custom_call_target="tpu_custom_call" | custom-call | flops 1000000 | bytes 1000000 | tf_op jit(solution)/shard_map/price/pallas_call | solution.py:282
  20.1 1.1 %collective-permute-done.4 = bf16[128,128]{1,0:T(8,128)(2,1)S(1)} collective-permute-done((bf16[128,128]{1,0:T(8,128)(2,1)S(1)}, bf16[128,128]{1,0:T(8,128)(2,1)S(1)}, u32[]{:S(2)}, u32[]{:S(2)}) %collective-permute-start.4) | collective-permute-done | bytes 32800 | tf_op jit(solution)/shard_map/ppermute | solution.py:298
  21.2 1.6 %collective-permute-start.5 = (bf16[128,128]{1,0:T(8,128)(2,1)S(1)}, bf16[128,128]{1,0:T(8,128)(2,1)S(1)}, u32[]{:S(2)}, u32[]{:S(2)}) collective-permute-start(bf16[128,128]{1,0:T(8,128)(2,1)S(1)} %add_convert_fusion.1), channel_id=1, source_target_pairs={{0,2},{1,3},{2,0},{3,1},{4,6},{5,7},{6,4},{7,5},{8,10},{9,11},{10,... | collective-permute-start | bytes 98312 | tf_op jit(solution)/shard_map/ppermute | solution.py:298
  22.8 2.3 %collective-permute-done.5 = bf16[128,128]{1,0:T(8,128)(2,1)S(1)} collective-permute-done((bf16[128,128]{1,0:T(8,128)(2,1)S(1)}, bf16[128,128]{1,0:T(8,128)(2,1)S(1)}, u32[]{:S(2)}, u32[]{:S(2)}) %collective-permute-start.5) | collective-permute-done | bytes 32800 | tf_op jit(solution)/shard_map/ppermute | solution.py:298
  25.2 3.7 %collective-permute-start.8 = (bf16[128,128]{1,0:T(8,128)(2,1)S(1)}, bf16[128,128]{1,0:T(8,128)(2,1)S(1)}, u32[]{:S(2)}, u32[]{:S(2)}) collective-permute-start(bf16[128,128]{1,0:T(8,128)(2,1)S(1)} %add_convert_fusion.refs_0_), channel_id=1, source_target_pairs={{0,12},{1,13},{2,14},{3,15},{4,8},{5,9},{6,10},{7,11},{8,4},{9,5},... | collective-permute-start | bytes 98312 | tf_op jit(solution)/shard_map/ppermute | solution.py:298
  29.6 1.3 %collective-permute-done.8.refs_3_ = bf16[128,128]{1,0:T(8,128)(2,1)S(1)} collective-permute-done((bf16[128,128]{1,0:T(8,128)(2,1)S(1)}, bf16[128,128]{1,0:T(8,128)(2,1)S(1)}, u32[]{:S(2)}, u32[]{:S(2)}) %collective-permute-start.8) | collective-permute-done | bytes 32800 | tf_op jit(solution)/shard_map/ppermute | solution.py:298
  31.0 2.7 %collective-permute-done.7.refs_2_ = bf16[128,128]{1,0:T(8,128)(2,1)S(1)} collective-permute-done((bf16[128,128]{1,0:T(8,128)(2,1)S(1)}, bf16[128,128]{1,0:T(8,128)(2,1)S(1)}, u32[]{:S(2)}, u32[]{:S(2)}) %collective-permute-start.7) | collective-permute-done | bytes 32800 | tf_op jit(solution)/shard_map/ppermute | solution.py:298
  33.9 1.2 %collective-permute-done.10.cots_partner = bf16[128,128]{1,0:T(8,128)(2,1)S(1)} collective-permute-done((bf16[128,128]{1,0:T(8,128)(2,1)S(1)}, bf16[128,128]{1,0:T(8,128)(2,1)S(1)}, u32[]{:S(2)}, u32[]{:S(2)}) %collective-permute-start.10) | collective-permute-done | bytes 32800 | tf_op jit(solution)/shard_map/ppermute | solution.py:298
  35.1 1.2 %adjoint.1 = (bf16[512,128]{1,0:T(8,128)(2,1)S(1)}, bf16[128,1536]{1,0:T(8,128)(2,1)S(1)}, bf16[128,1536]{1,0:T(8,128)(2,1)S(1)}) custom-call(bf16[1280,128]{1,0:T(8,128)(2,1)S(1)} %constant_dynamic-update-slice_fusion.gathered, bf16[128,128]{1,0:T(8,128)(2,1)S(1)} %get-tuple-element.41.cots_mine, bf16[128,128]{1,0:T(8,128)(2,1)S(1)} %collective-permute-done.10.cots_partner, ...), custom_call_target="tpu_custom_call" | custom-call | flops 1000000 | bytes 1000000 | tf_op jit(solution)/shard_map/adjoint/pallas_call | solution.py:282
  36.6 1.0 %keep.1.kept = f32[512,128]{1,0:T(8,128)S(1)} custom-call(bf16[1280,128]{1,0:T(8,128)(2,1)S(1)} %constant_dynamic-update-slice_fusion.gathered, bf16[128,1536]{1,0:T(8,128)(2,1)S(1)} %get-tuple-element.44.fwd_cots, bf16[128,1536]{1,0:T(8,128)(2,1)S(1)} %get-tuple-element.45.ann_cots, bf16[1024,1536]{1,0:T(8,128)(2,1)S(1)} %get-tuple-element.30.w_fwd, ...), custom_call_target="tpu_custom_call" | custom-call | flops 200000000 | bytes 4000000 | tf_op jit(solution)/shard_map/keep/pallas_call | solution.py:282
  37.8 1.6 %collective-permute-start.12 = (bf16[256,128]{1,0:T(8,128)(2,1)S(1)}, bf16[256,128]{1,0:T(8,128)(2,1)S(1)}, u32[]{:S(2)}, u32[]{:S(2)}) collective-permute-start(bf16[256,128]{1,0:T(8,128)(2,1)S(1)} %get-tuple-element.48), channel_id=1, source_target_pairs={{0,2},{1,3},{2,0},{3,1},{4,6},{5,7},{6,4},{7,5},{8,10},{9,11},{10,... | collective-permute-start | bytes 196616 | tf_op jit(solution)/shard_map/ppermute | solution.py:298
  39.4 2.7 %collective-permute-done.12.arrived = bf16[256,128]{1,0:T(8,128)(2,1)S(1)} collective-permute-done((bf16[256,128]{1,0:T(8,128)(2,1)S(1)}, bf16[256,128]{1,0:T(8,128)(2,1)S(1)}, u32[]{:S(2)}, u32[]{:S(2)}) %collective-permute-start.12) | collective-permute-done | bytes 65568 | tf_op jit(solution)/shard_map/ppermute | solution.py:298
  42.2 1.6 %collective-permute-start.9 = (f32[16]{0:T(128)S(1)}, f32[16]{0:T(128)S(1)}, u32[]{:S(2)}, u32[]{:S(2)}) collective-permute-start(f32[16]{0:T(128)S(1)} %bitcast.16), channel_id=1, source_target_pairs={{0,16},{16,0},{1,17},{17,1},{2,18},{18,2},{3,19},{19,3},{4,20},{20... | collective-permute-start | bytes 200 | tf_op jit(solution)/shard_map/ppermute | solution.py:305
  43.8 2.3 %collective-permute-done.13.arrived = bf16[128,128]{1,0:T(8,128)(2,1)S(1)} collective-permute-done((bf16[128,128]{1,0:T(8,128)(2,1)S(1)}, bf16[128,128]{1,0:T(8,128)(2,1)S(1)}, u32[]{:S(2)}, u32[]{:S(2)}) %collective-permute-start.13) | collective-permute-done | bytes 32800 | tf_op jit(solution)/shard_map/ppermute | solution.py:298
  46.1 2.3 %collective-permute-start.14 = (bf16[64,128]{1,0:T(8,128)(2,1)S(1)}, bf16[64,128]{1,0:T(8,128)(2,1)S(1)}, u32[]{:S(2)}, u32[]{:S(2)}) collective-permute-start(bf16[64,128]{1,0:T(8,128)(2,1)S(1)} %get-tuple-element.52), channel_id=1, source_target_pairs={{0,8},{1,9},{2,10},{3,11},{4,12},{5,13},{6,14},{7,15},{8,0},{9,1},... | collective-permute-start | bytes 49160 | tf_op jit(solution)/shard_map/ppermute | solution.py:298
  48.9 1.9 %collective-permute-done.14.arrived = bf16[64,128]{1,0:T(8,128)(2,1)S(1)} collective-permute-done((bf16[64,128]{1,0:T(8,128)(2,1)S(1)}, bf16[64,128]{1,0:T(8,128)(2,1)S(1)}, u32[]{:S(2)}, u32[]{:S(2)}) %collective-permute-start.14) | collective-permute-done | bytes 16416 | tf_op jit(solution)/shard_map/ppermute | solution.py:298
  (27 shorter events, 3.3 us)
Async XLA Ops:
  1.8 5.9 %collective-permute-start = (bf16[80,128]{1,0:T(8,128)(2,1)S(1)}, bf16[80,128]{1,0:T(8,128)(2,1)S(1)}, u32[]{:S(2)}, u32[]{:S(2)}) collective-permute-start(bf16[80,128]{1,0:T(8,128)(2,1)S(1)} %get-tuple-element.28), channel_id=1, source_target_pairs={{0,8},{1,9},{2,10},{3,11},{4,12},{5,13},{6,14},{7,15},{8,0},{9,1},... | collective-permute-start | bytes 61448 | tf_op jit(solution)/shard_map/ppermute | solution.py:298
  7.8 4.3 %collective-permute-start.1 = (bf16[160,128]{1,0:T(8,128)(2,1)S(1)}, bf16[160,128]{1,0:T(8,128)(2,1)S(1)}, u32[]{:S(2)}, u32[]{:S(2)}) collective-permute-start(bf16[160,128]{1,0:T(8,128)(2,1)S(1)} %pad_maximum_fusion.2), channel_id=1, source_target_pairs={{0,4},{1,5},{2,6},{3,7},{4,0},{5,1},{6,2},{7,3},{8,12},{9,13},{10,... | collective-permute-start | bytes 122888 | tf_op jit(solution)/shard_map/ppermute | solution.py:298
  12.1 4.5 %collective-permute-start.2 = (bf16[320,128]{1,0:T(8,128)(2,1)S(1)}, bf16[320,128]{1,0:T(8,128)(2,1)S(1)}, u32[]{:S(2)}, u32[]{:S(2)}) collective-permute-start(bf16[320,128]{1,0:T(8,128)(2,1)S(1)} %pad_maximum_fusion.1), channel_id=1, source_target_pairs={{0,2},{1,3},{2,0},{3,1},{4,6},{5,7},{6,4},{7,5},{8,10},{9,11},{10,... | collective-permute-start | bytes 245768 | tf_op jit(solution)/shard_map/ppermute | solution.py:298
  16.6 1.5 %collective-permute-start.3 = (bf16[640,128]{1,0:T(8,128)(2,1)S(1)}, bf16[640,128]{1,0:T(8,128)(2,1)S(1)}, u32[]{:S(2)}, u32[]{:S(2)}) collective-permute-start(bf16[640,128]{1,0:T(8,128)(2,1)S(1)} %pad_maximum_fusion), channel_id=1, source_target_pairs={{0,1},{1,0},{2,3},{3,2},{4,5},{5,4},{6,7},{7,6},{8,9},{9,8},{10,11... | collective-permute-start | bytes 491528 | tf_op jit(solution)/shard_map/ppermute | solution.py:298
  19.9 1.3 %collective-permute-start.4 = (bf16[128,128]{1,0:T(8,128)(2,1)S(1)}, bf16[128,128]{1,0:T(8,128)(2,1)S(1)}, u32[]{:S(2)}, u32[]{:S(2)}) collective-permute-start(bf16[128,128]{1,0:T(8,128)(2,1)S(1)} %get-tuple-element.39), channel_id=1, source_target_pairs={{0,1},{1,0},{2,3},{3,2},{4,5},{5,4},{6,7},{7,6},{8,9},{9,8},{10,11... | collective-permute-start | bytes 98312 | tf_op jit(solution)/shard_map/ppermute | solution.py:298
  21.2 4.0 %collective-permute-start.5 = (bf16[128,128]{1,0:T(8,128)(2,1)S(1)}, bf16[128,128]{1,0:T(8,128)(2,1)S(1)}, u32[]{:S(2)}, u32[]{:S(2)}) collective-permute-start(bf16[128,128]{1,0:T(8,128)(2,1)S(1)} %add_convert_fusion.1), channel_id=1, source_target_pairs={{0,2},{1,3},{2,0},{3,1},{4,6},{5,7},{6,4},{7,5},{8,10},{9,11},{10,... | collective-permute-start | bytes 98312 | tf_op jit(solution)/shard_map/ppermute | solution.py:298
  25.2 5.8 %collective-permute-start.8 = (bf16[128,128]{1,0:T(8,128)(2,1)S(1)}, bf16[128,128]{1,0:T(8,128)(2,1)S(1)}, u32[]{:S(2)}, u32[]{:S(2)}) collective-permute-start(bf16[128,128]{1,0:T(8,128)(2,1)S(1)} %add_convert_fusion.refs_0_), channel_id=1, source_target_pairs={{0,12},{1,13},{2,14},{3,15},{4,8},{5,9},{6,10},{7,11},{8,4},{9,5},... | collective-permute-start | bytes 98312 | tf_op jit(solution)/shard_map/ppermute | solution.py:298
  28.9 4.8 %collective-permute-start.7 = (bf16[128,128]{1,0:T(8,128)(2,1)S(1)}, bf16[128,128]{1,0:T(8,128)(2,1)S(1)}, u32[]{:S(2)}, u32[]{:S(2)}) collective-permute-start(bf16[128,128]{1,0:T(8,128)(2,1)S(1)} %add_convert_fusion.refs_0_), channel_id=1, source_target_pairs={{0,8},{1,9},{2,10},{3,11},{4,12},{5,13},{6,14},{7,15},{8,0},{9,1},... | collective-permute-start | bytes 98312 | tf_op jit(solution)/shard_map/ppermute | solution.py:298
  28.9 4.8 %collective-permute-start.6 = (bf16[128,128]{1,0:T(8,128)(2,1)S(1)}, bf16[128,128]{1,0:T(8,128)(2,1)S(1)}, u32[]{:S(2)}, u32[]{:S(2)}) collective-permute-start(bf16[128,128]{1,0:T(8,128)(2,1)S(1)} %add_convert_fusion.refs_0_), channel_id=1, source_target_pairs={{0,4},{1,5},{2,6},{3,7},{4,0},{5,1},{6,2},{7,3},{8,12},{9,13},{10,... | collective-permute-start | bytes 98312 | tf_op jit(solution)/shard_map/ppermute | solution.py:298
  33.9 1.3 %collective-permute-start.10 = (bf16[128,128]{1,0:T(8,128)(2,1)S(1)}, bf16[128,128]{1,0:T(8,128)(2,1)S(1)}, u32[]{:S(2)}, u32[]{:S(2)}) collective-permute-start(bf16[128,128]{1,0:T(8,128)(2,1)S(1)} %get-tuple-element.41.cots_mine), channel_id=1, source_target_pairs={{0,1},{1,0},{2,3},{3,2},{4,5},{5,4},{6,7},{7,6},{8,9},{9,8},{10,11... | collective-permute-start | bytes 98312 | tf_op jit(solution)/shard_map/ppermute | solution.py:298
  36.4 1.4 %collective-permute-start.11 = (bf16[512,128]{1,0:T(8,128)(2,1)S(1)}, bf16[512,128]{1,0:T(8,128)(2,1)S(1)}, u32[]{:S(2)}, u32[]{:S(2)}) collective-permute-start(bf16[512,128]{1,0:T(8,128)(2,1)S(1)} %get-tuple-element.46), channel_id=1, source_target_pairs={{0,1},{1,0},{2,3},{3,2},{4,5},{5,4},{6,7},{7,6},{8,9},{9,8},{10,11... | collective-permute-start | bytes 393224 | tf_op jit(solution)/shard_map/ppermute | solution.py:298
  37.8 4.3 %collective-permute-start.12 = (bf16[256,128]{1,0:T(8,128)(2,1)S(1)}, bf16[256,128]{1,0:T(8,128)(2,1)S(1)}, u32[]{:S(2)}, u32[]{:S(2)}) collective-permute-start(bf16[256,128]{1,0:T(8,128)(2,1)S(1)} %get-tuple-element.48), channel_id=1, source_target_pairs={{0,2},{1,3},{2,0},{3,1},{4,6},{5,7},{6,4},{7,5},{8,10},{9,11},{10,... | collective-permute-start | bytes 196616 | tf_op jit(solution)/shard_map/ppermute | solution.py:298
  42.2 4.0 %collective-permute-start.13 = (bf16[128,128]{1,0:T(8,128)(2,1)S(1)}, bf16[128,128]{1,0:T(8,128)(2,1)S(1)}, u32[]{:S(2)}, u32[]{:S(2)}) collective-permute-start(bf16[128,128]{1,0:T(8,128)(2,1)S(1)} %get-tuple-element.50), channel_id=1, source_target_pairs={{0,4},{1,5},{2,6},{3,7},{4,0},{5,1},{6,2},{7,3},{8,12},{9,13},{10,... | collective-permute-start | bytes 98312 | tf_op jit(solution)/shard_map/ppermute | solution.py:298
  42.2 6.2 %collective-permute-start.9 = (f32[16]{0:T(128)S(1)}, f32[16]{0:T(128)S(1)}, u32[]{:S(2)}, u32[]{:S(2)}) collective-permute-start(f32[16]{0:T(128)S(1)} %bitcast.16), channel_id=1, source_target_pairs={{0,16},{16,0},{1,17},{17,1},{2,18},{18,2},{3,19},{19,3},{4,20},{20... | collective-permute-start | bytes 200 | tf_op jit(solution)/shard_map/ppermute | solution.py:305
  46.1 4.7 %collective-permute-start.14 = (bf16[64,128]{1,0:T(8,128)(2,1)S(1)}, bf16[64,128]{1,0:T(8,128)(2,1)S(1)}, u32[]{:S(2)}, u32[]{:S(2)}) collective-permute-start(bf16[64,128]{1,0:T(8,128)(2,1)S(1)} %get-tuple-element.52), channel_id=1, source_target_pairs={{0,8},{1,9},{2,10},{3,11},{4,12},{5,13},{6,14},{7,15},{8,0},{9,1},... | collective-permute-start | bytes 49160 | tf_op jit(solution)/shard_map/ppermute | solution.py:298

commit v5 on v3

v5 whole, which is shorter than its diff:
```python
import functools
import math

import jax
import jax.numpy as jnp
from jax import lax
from jax.experimental import pallas as pl
from jax.experimental.pallas import tpu as pltpu
from jax.sharding import PartitionSpec as P

F32 = jnp.float32
BF16 = jnp.bfloat16
NT = (((1,), (1,)), ((), ()))
TN = (((0,), (0,)), ((), ()))
LANES = 128
TILE = 512
VMEM = pl.BlockSpec(memory_space=pltpu.VMEM)
HBM = pl.BlockSpec(memory_space=pltpu.HBM)
VMEM_LIMIT = 8 * 2**20


def log1p_unit(e):
    return jnp.where(e < 1e-4, (1.0 - 0.5 * e) * e, jnp.log(1.0 + e))


def split_bf16(x):
    high = x.astype(BF16)
    return high, (x - high.astype(F32)).astype(BF16)


def iota(shape, dim):
    return lax.broadcasted_iota(jnp.int32, shape, dim)


def block_basis(basis_t, factors, height):
    tenors, size = basis_t.shape
    down = (iota((factors, size), 0) % size == iota((factors, size), 1)).astype(BF16)
    across = (iota((tenors, height), 1) % tenors == iota((tenors, height), 0)).astype(BF16)
    spread = lax.dot_general(down, basis_t, NT, preferred_element_type=F32).astype(BF16)
    tiled = jnp.dot(spread, across, preferred_element_type=F32)
    same = iota((factors, height), 0) // size == iota((factors, height), 1) // tenors
    return jnp.where(same, tiled, 0.0).astype(BF16)


def bits_of(n):
    return int(math.log2(n))


def pair_order(ids, local, devices):
    core = lax.rem(lax.axis_index("trade"), 2)
    owner = jnp.right_shift(ids, bits_of(local))
    side = jnp.bitwise_xor(jnp.bitwise_and(owner, 1), core)
    place = side * (devices // 2) + jnp.right_shift(owner, 1)
    return place * local + jnp.bitwise_and(ids, local - 1)


def steps_of(devices):
    bits = [1 << k for k in range(1, bits_of(devices))]
    return bits[2:][::-1], bits[:2]


def cube_place(owner, devices):
    distance = jnp.bitwise_xor(owner, lax.axis_index("trade"))
    single, group = steps_of(devices)
    place = jnp.zeros_like(distance)
    for k, mask in enumerate(single + group + [1]):
        bit = jnp.bitwise_and(jnp.right_shift(distance, bits_of(mask)), 1)
        place = jnp.bitwise_or(place, jnp.left_shift(bit, k))
    return place


def cube_order(ids, local, devices):
    place = cube_place(jnp.right_shift(ids, bits_of(local)), devices)
    return place * local + jnp.bitwise_and(ids, local - 1)


def fetch(pairs, sems):
    copies = [pltpu.make_async_copy(src, dst, sems.at[k]) for k, (src, dst) in enumerate(pairs)]
    for copy in copies:
        copy.start()
    for copy in copies:
        copy.wait()


def curves_of(basis, factors):
    dims = (((0,), (1,)), ((), ()))
    return lax.dot_general(basis, factors, dims, preferred_element_type=F32).astype(BF16)


def curve_kernel(
    factors_hbm, basis_hbm, weight_hbm, out, basis_out, weight_ref, extra, factors_ref,
    basis_ref, sems,
):
    fetch(
        [(factors_hbm, factors_ref), (basis_hbm, basis_ref), (weight_hbm, weight_ref)], sems
    )
    factors = factors_ref.shape[1]
    tenors, size = basis_ref.shape
    basis = block_basis(basis_ref[...], factors, factors // size * tenors)
    basis_out[...] = basis
    out[...] = curves_of(basis, factors_ref[...])
    dates, sets = weight_ref.shape
    rows, lanes = extra.shape
    first = lax.axis_index("trade") // 2 * sets
    spot = (iota((sets, lanes), 1) == iota((sets, lanes), 0) + lax.rem(first, lanes)).astype(BF16)
    total = jnp.zeros((rows, lanes), F32)
    for k, part in enumerate(split_bf16(weight_ref[...])):
        top = (first // lanes * 2 + k) * dates
        lift = (iota((rows, dates), 0) == iota((rows, dates), 1) + top).astype(BF16)
        lifted = jnp.dot(lift, part, preferred_element_type=F32).astype(BF16)
        total += jnp.dot(lifted, spot, preferred_element_type=F32)
    extra[...] = total.astype(BF16)


def next_curve_kernel(own, arrived, basis, out):
    height = own.shape[0]
    out[:height, :] = own[...]
    out[height:, :] = curves_of(basis[...], arrived[...])


def join_kernel(*refs):
    *parts, _, out = refs
    height = parts[0].shape[0]
    for k, part in enumerate(parts):
        out[k * height : (k + 1) * height, :] = part[...]


def prep_kernel(devices, *refs):
    sources, rest = refs[:8], refs[9:]
    w_fwd, w_disc, onehot = rest[:3]
    params, (blocks_ref, set_ref, weights_ref, sems) = rest[3:8], rest[8:]
    fetch(list(zip(sources, (blocks_ref, set_ref, weights_ref) + tuple(params))), sems)
    tenors, trades = weights_ref.shape
    height = w_fwd.shape[0]
    blocks = height // tenors
    sets = onehot.shape[0]
    zero = jnp.zeros((tenors, LANES), F32)
    row = iota((16, LANES), 0)
    set_rows = pair_order(set_ref[...], sets // devices, devices)
    block_rows = cube_order(blocks_ref[...], blocks // devices, devices)
    for t in range(0, trades, LANES):
        lanes = slice(t, t + LANES)
        weights = weights_ref[:, lanes]
        for k, out in enumerate((w_fwd, w_disc)):
            ids = jnp.broadcast_to(block_rows[k : k + 1, lanes], (tenors, LANES))
            for b in range(blocks):
                out[b * tenors : (b + 1) * tenors, lanes] = jnp.where(
                    ids == b, weights, zero
                ).astype(BF16)
        ids = jnp.broadcast_to(set_rows[t // LANES : t // LANES + 1, :], (16, LANES))
        for n in range(0, sets, 16):
            onehot[n : n + 16, lanes] = jnp.where(ids == row + n, 1.0, 0.0).astype(BF16)


def param_row(ref, start, tile):
    return jnp.concatenate(
        [ref[j : j + 1, :] for j in range(start // LANES, (start + tile) // LANES)], axis=1
    )


def half_price_kernel(curves, w_fwd, w_disc, forward, annuity):
    half, trades = curves.shape[0], w_fwd.shape[1]
    tile = TILE if trades % TILE == 0 else trades
    curve = curves[...]
    discount = jnp.exp(-0.5 * curve.astype(F32)).astype(BF16)
    for t in range(0, trades, tile):
        lanes = slice(t, t + tile)
        forward[:, lanes] = lax.dot_general(
            curve, w_fwd[:half, lanes], TN, preferred_element_type=F32
        )
        annuity[:, lanes] = lax.dot_general(
            discount, w_disc[:half, lanes], TN, preferred_element_type=F32
        )


def price_kernel(
    curves, forward_ref, annuity_ref, w_fwd, w_disc, onehot, kind_ref, notional_ref, strike_ref,
    vol_ref, threshold_ref, keep, send, fwd_scale, ann_scale,
):
    near, rows = curves.shape
    trades = w_fwd.shape[1]
    half = keep.shape[0]
    tile = TILE if trades % TILE == 0 else trades
    curve = curves[...]
    discount = jnp.exp(-0.5 * curve.astype(F32)).astype(BF16)
    total = jnp.zeros((2 * half, rows), F32)
    for t in range(0, trades, tile):
        lanes = slice(t, t + tile)
        forward = forward_ref[:, lanes] + lax.dot_general(
            curve, w_fwd[near:, lanes], TN, preferred_element_type=F32
        )
        annuity = annuity_ref[:, lanes] + lax.dot_general(
            discount, w_disc[near:, lanes], TN, preferred_element_type=F32
        )
        vol = param_row(vol_ref, t, tile)
        notional = param_row(notional_ref, t, tile)
        option = jnp.broadcast_to(param_row(kind_ref, t, tile) == 1, (rows, tile))
        moneyness = forward - param_row(strike_ref, t, tile)
        scaled = moneyness * (1.0 / vol)
        e = jnp.exp(-jnp.abs(scaled))
        softplus = jnp.maximum(scaled, 0.0) + log1p_unit(e)
        sigmoid = jnp.where(scaled >= 0.0, 1.0, e) / (1.0 + e)
        payoff = jnp.where(option, vol * softplus, moneyness)
        slope = jnp.where(option, sigmoid, 1.0)
        scaled_annuity = notional * annuity
        value = (scaled_annuity * payoff).astype(BF16)
        fwd_scale[:, lanes] = scaled_annuity * slope
        ann_scale[:, lanes] = notional * payoff
        total += lax.dot_general(onehot[:, lanes], value, NT, preferred_element_type=F32)
    keep[...] = total[:half]
    send[...] = total[half:].astype(BF16)
    sets = threshold_ref.shape[1]
    chip = lax.axis_index("trade") // 2
    own = pl.ds(pl.multiple_of(chip * sets, sets), sets)
    square = iota((sets, sets), 0) == iota((sets, sets), 1)
    column = jnp.sum(jnp.where(square, threshold_ref[...], 0.0), axis=1, keepdims=True)
    keep[own, :] = keep[own, :] - column


def pair_kernel(keep, arrived, extra, out):
    half = keep.shape[0]
    out[:half, :] = (keep[...] + arrived[...].astype(F32)).astype(BF16)
    out[half:, :] = extra[...]


def sets_kernel(weight_ref, *refs):
    parts, (cots, cva, excess_ref) = refs[:-3], refs[-3:]
    dates, sets = weight_ref.shape
    half, rows = excess_ref.shape
    me = lax.axis_index("trade")
    total = parts[0][...].astype(F32)
    for part in parts[1:]:
        total += part[...].astype(F32)
    excess = total[:half]
    excess_ref[...] = excess
    span = rows // dates
    pieces = total[half:].astype(BF16)
    line = iota((pieces.shape[0], rows), 0)
    weights = []
    for k in range(max(1, half // rows)):
        spread = (line % dates == iota(line.shape, 1) // span) & (line // (2 * dates) == k)
        weights.append(
            lax.dot_general(pieces, spread.astype(BF16), TN, preferred_element_type=F32)
        )
    weights = jnp.concatenate(weights, axis=0)[:half]
    e = jnp.exp(-jnp.abs(excess))
    sigmoid = jnp.where(excess >= 0.0, 1.0, e) / (1.0 + e)
    cots[...] = (weights * sigmoid).astype(BF16)
    chip = me // 2
    own = excess_ref[pl.ds(pl.multiple_of(chip * sets, sets), sets), :]
    exposure = jnp.maximum(own, 0.0) + log1p_unit(jnp.exp(-jnp.abs(own)))
    square = iota((sets, sets), 0) == iota((sets, sets), 1)
    date = iota((sets, rows), 1) // span
    column = jnp.zeros((sets, 1), F32)
    for d in range(dates):
        weight = jnp.where(square, weight_ref[d : d + 1, :], 0.0)
        weight = jnp.sum(weight, axis=1, keepdims=True)
        column += weight * jnp.sum(jnp.where(date == d, exposure, 0.0), axis=1, keepdims=True)
    cva[...] = jnp.sum(jnp.where(square, column, 0.0), axis=0, keepdims=True)


def half_cot(side, curves, fwd_cots, ann_cots, w_fwd, w_disc):
    half, trades = curves.shape[0], w_fwd.shape[1]
    tile = TILE if trades % TILE == 0 else trades
    band = slice(side * half, (side + 1) * half)
    from_fwd = from_disc = 0.0
    for t in range(0, trades, tile):
        lanes = slice(t, t + tile)
        from_fwd += lax.dot_general(
            w_fwd[band, lanes], fwd_cots[:, lanes], NT, preferred_element_type=F32
        )
        from_disc += lax.dot_general(
            w_disc[band, lanes], ann_cots[:, lanes], NT, preferred_element_type=F32
        )
    return from_fwd - 0.5 * jnp.exp(-0.5 * curves[...].astype(F32)) * from_disc


def adjoint_kernel(
    partner, cots_mine, cots_partner, fwd_scale, ann_scale, w_fwd, w_disc, onehot, send,
    fwd_cots, ann_cots,
):
    trades = fwd_scale.shape[1]
    tile = TILE if trades % TILE == 0 else trades
    cots = jnp.concatenate([cots_mine[...], cots_partner[...]], axis=0)
    for t in range(0, trades, tile):
        lanes = slice(t, t + tile)
        trade_cot = lax.dot_general(cots, onehot[:, lanes], TN, preferred_element_type=F32)
        fwd_cots[:, lanes] = (trade_cot * fwd_scale[:, lanes]).astype(BF16)
        ann_cots[:, lanes] = (trade_cot * ann_scale[:, lanes]).astype(BF16)
    send[...] = half_cot(1, partner, fwd_cots, ann_cots, w_fwd, w_disc).astype(BF16)


def keep_kernel(mine, fwd_cots, ann_cots, w_fwd, w_disc, keep):
    keep[...] = half_cot(0, mine, fwd_cots, ann_cots, w_fwd, w_disc)


def fold_kernel(count, kept, *refs):
    arrived, (keep, *sends) = refs[:count], refs[count:]
    total = kept[...]
    for part in arrived:
        total += part[...].astype(F32)
    size = keep.shape[0]
    keep[...] = total[:size]
    for k, send in enumerate(sends):
        send[...] = total[(k + 1) * size : (k + 2) * size].astype(BF16)


def factor_kernel(kept, arrived, basis, out):
    total = kept[...] + arrived[...].astype(F32)
    dims = (((0,), (1,)), ((), ()))
    high, low = split_bf16(total)
    out[...] = lax.dot_general(high, basis[...], dims, preferred_element_type=F32)
    out[...] += lax.dot_general(low, basis[...], dims, preferred_element_type=F32)


def call(
    kernel, name, out_shape, scratch=(), flops=1_000_000, moved=1_000_000, space=VMEM, last=None
):
    def run(*args):
        spaces = [space] * len(args)
        if last is not None:
            spaces[-1] = last
        args = [
            pltpu.with_memory_space_constraint(x, pltpu.HBM) if where is HBM else x
            for x, where in zip(args, spaces)
        ]
        return pl.pallas_call(
            kernel,
            in_specs=spaces,
            out_specs=jax.tree.map(lambda _: VMEM, out_shape),
            out_shape=out_shape,
            scratch_shapes=scratch,
            cost_estimate=pl.CostEstimate(flops=flops, bytes_accessed=moved, transcendentals=0),
            compiler_params=pltpu.CompilerParams(vmem_limit_bytes=VMEM_LIMIT),
            name=name,
        )(*args)

    return run


def swap(x, mask):
    n = lax.axis_size("trade")
    return lax.ppermute(x, "trade", [(i, i ^ mask) for i in range(n)])


def swaps(x, step):
    masks = [sum(b for k, b in enumerate(step) if j >> k & 1) for j in range(1, 2 ** len(step))]
    parts = {}
    for j in sorted(range(len(masks)), key=lambda j: -bin(masks[j]).count("1")):
        parts[j] = swap(x[j] if isinstance(x, (list, tuple)) else x, masks[j])
    return [parts[j] for j in range(len(masks))]


def sum_over(x, axis):
    n = lax.axis_size(axis)
    total = x
    for shift in range(1, n):
        total = total + lax.ppermute(x, axis, [(i, (i + shift) % n) for i in range(n)])
    return total


def shards(
    factor_paths, tenor_basis, trade_blocks, trade_set, trade_type, notional, strike,
    vol_level, cash_weights, set_threshold, date_weight,
):
    factor_rows, dates, paths = factor_paths.shape
    block_size, tenors = tenor_basis.shape
    rows = dates * paths
    devices = lax.axis_size("trade")
    local_blocks = factor_rows // block_size
    height = local_blocks * tenors
    local_sets = set_threshold.shape[0]
    half_sets = local_sets * devices // 2
    all_rows = height * devices
    trades = trade_set.shape[0]
    shape = jax.ShapeDtypeStruct
    extra_rows = -(-max(1, half_sets // rows) * 2 * dates // 16) * 16
    lane_rows = (trades // LANES, LANES)
    dma = pltpu.SemaphoreType.DMA

    factors = jnp.transpose(factor_paths, (1, 2, 0)).reshape(rows, factor_rows)
    single, group = steps_of(devices)
    arrived = swap(factors, single[0])
    curves, basis, weights, extra = call(
        curve_kernel, "curves",
        [shape((height, rows), BF16), shape((factor_rows, height), BF16),
         shape((dates, local_sets), F32), shape((extra_rows, rows), BF16)],
        [pltpu.VMEM((rows, factor_rows), BF16), pltpu.VMEM((tenors, block_size), BF16), dma((3,))],
        space=HBM,
    )(factors, jnp.transpose(tenor_basis), jnp.transpose(date_weight))
    curves = call(next_curve_kernel, "curves2", shape((2 * height, rows), BF16))(
        curves, arrived, basis
    )
    for mask in single[1:]:
        curves = jnp.concatenate([curves, swap(curves, mask)], axis=0)
    near = [curves] + swaps(curves, group)
    w_fwd, w_disc, onehot, *params = call(
        functools.partial(prep_kernel, devices), "prep",
        [shape((all_rows, trades), BF16)] * 2 + [shape((2 * half_sets, trades), BF16)]
        + [shape(lane_rows, jnp.int32)] + [shape(lane_rows, F32)] * 3 + [shape((1, local_sets), F32)],
        [pltpu.VMEM((2, trades), jnp.int32), pltpu.VMEM(lane_rows, jnp.int32),
         pltpu.VMEM((tenors, trades), F32), dma((8,))],
        flops=400_000_000, moved=8_000_000, space=HBM,
        last=VMEM,
    )(
        trade_blocks, trade_set.reshape(lane_rows), cash_weights, trade_type.reshape(lane_rows),
        notional.reshape(lane_rows), strike.reshape(lane_rows), vol_level.reshape(lane_rows),
        set_threshold[None], curves,
    )
    mine = call(join_kernel, "join", shape((all_rows // 2, rows), BF16))(*near, params[-1])
    partner = swap(mine, 1)
    forward, annuity = call(
        half_price_kernel, "price1", [shape((rows, trades), F32)] * 2,
        flops=400_000_000, moved=4_000_000,
    )(mine, w_fwd, w_disc)
    keep, send, fwd_scale, ann_scale = call(
        price_kernel, "price2",
        [shape((half_sets, rows), F32), shape((half_sets, rows), BF16),
         shape((rows, trades), F32), shape((rows, trades), F32)],
    )(partner, forward, annuity, w_fwd, w_disc, onehot, *params)

    total = call(pair_kernel, "pair", shape((half_sets + extra_rows, rows), BF16))(
        keep, swap(send, 1), extra
    )
    bits = [1 << k for k in range(1, bits_of(devices))]
    steps = [bits[:1]] if len(bits) % 2 else []
    steps += [bits[k : k + 2] for k in range(len(bits) % 2, len(bits), 2)]
    for step in steps:
        parts = [total] + swaps(total, step)
        if step is not steps[-1]:
            total = functools.reduce(jnp.add, [p.astype(F32) for p in parts]).astype(BF16)
    cots_mine, cva = call(
        sets_kernel, "sets",
        [shape((half_sets, rows), BF16), shape((1, local_sets), F32)],
        [pltpu.VMEM((half_sets, rows), F32)],
    )(weights, *parts)
    cots_partner = swap(cots_mine, 1)

    send, fwd_cots, ann_cots = call(
        adjoint_kernel, "adjoint",
        [shape((all_rows // 2, rows), BF16)] + [shape((rows, trades), BF16)] * 2,
    )(partner, cots_mine, cots_partner, fwd_scale, ann_scale, w_fwd, w_disc, onehot)
    keep = call(
        keep_kernel, "keep", shape((all_rows // 2, rows), F32),
        flops=200_000_000, moved=4_000_000,
    )(mine, fwd_cots, ann_cots, w_fwd, w_disc)
    arrived = [swap(send, 1)]
    size = all_rows // 2
    for step in [group] + [[mask] for mask in single[::-1]]:
        size >>= len(step)
        shapes = [shape((size, rows), F32)]
        shapes += [shape((size, rows), BF16)] * (2 ** len(step) - 1)
        keep, *sends = call(
            functools.partial(fold_kernel, len(arrived)), f"fold{step[0]}", shapes
        )(keep, *arrived)
        arrived = swaps(sends, step)
    factor_cot = call(factor_kernel, "factors", shape((rows, factor_rows), F32))(
        keep, *arrived, basis
    )
    factor_cot = jnp.transpose(factor_cot.reshape(dates, paths, factor_rows), (2, 0, 1))
    netting_cva = sum_over(cva[0], "path") / (paths * lax.axis_size("path"))
    return netting_cva, factor_cot


def solution(mesh):
    return jax.shard_map(
        shards,
        mesh=mesh,
        in_specs=(
            P("trade", None, "path"), P(), P(None, "trade"), P("trade"), P("trade"),
            P("trade"), P("trade"), P("trade"), P(None, "trade"), P("trade"),
            P("trade", None),
        ),
        out_specs=(P("trade"), P("trade", None, "path")),
        check_vma=False,
    )
```

time: 57.8 us -> 47.1 us (0.81)
  local copies, waits for them, and re-layouts: 7.91 us -> 0 us
  waiting for transfers between devices: 21.1 us -> 15.9 us
  Pallas kernels: 7.12 us -> 9.28 us
  starting transfers between devices: 19.8 us -> 20.5 us
    unnamed x26 -> x0, local copies, waits for them, and re-layouts: 7.89 us -> none
    ppermute x14 -> x16, waiting for transfers between devices: 21.1 us -> 15.9 us  [swap(): return lax.ppermute(x, 'trade', [(i, i ^ mask) for i in range(n)])]
    pallas_call x10 -> x13, Pallas kernels: 7.12 us -> 9.28 us  [run(): pl.pallas_call(kernel, in_specs=spaces, out_specs=jax.tree.map(lambda _:...]
    ppermute x14 -> x16, starting transfers between devices: 18.3 us -> 19 us  [swap(): return lax.ppermute(x, 'trade', [(i, i ^ mask) for i in range(n)])]
  transfers between devices with their start and end apart: 15 -> 17, of which waited for: 12 -> 12; matrix products, arithmetic and copies ran while one was open for 1% -> 1% of each run, Pallas kernels for 5% -> 11%
where the time goes in v5:
time: 47.1 us; the launch traced here: 46.9 us
  starting transfers between devices  20.5 us (44%)
  waiting for transfers between devices  15.9 us (34%)
  Pallas kernels  9.28 us (20%)
  between operations  0.74 us (2%)
  other arithmetic  0.53 us (1%)
    ppermute x16, starting transfers between devices, swap(): return lax.ppermute(x, 'trade', [(i, i ^ mask) for i in range(n)])  19 us
    ppermute x16, waiting for transfers between devices, swap(): return lax.ppermute(x, 'trade', [(i, i ^ mask) for i in range(n)])  15.9 us
    pallas_call x13, Pallas kernels, run(): pl.pallas_call(kernel, in_specs=spaces, out_specs=jax.tree.map(lambda _:...  9.28 us
    ppermute x1, starting transfers between devices, sum_over(): lax.ppermute(x, axis, [(i, (i + shift) % n) for i in range(n)])  1.49 us
  transfers between devices with their start and end apart: 17, of which 12 were waited for; matrix products, arithmetic and copies ran while one was open for 1% of the time, Pallas kernels for 11%

profile of v5, /device:TPU:0, one launch (start us, length us, event | category | flops | bytes accessed | tf_op | source)
XLA Modules:
  0.0 46.9 jit_solution(4891907963846064629)
XLA Ops:
  0.6 4.1 %collective-permute-start = (bf16[128,128]{1,0:T(8,128)(2,1)}, bf16[128,128]{1,0:T(8,128)(2,1)S(1)}, u32[]{:S(2)}, u32[]{:S(2)}) collective-permute-start(bf16[128,128]{1,0:T(8,128)(2,1)} %bitcast.18), channel_id=1, source_target_pairs={{0,8},{1,9},{2,10},{3,11},{4,12},{5,13},{6,14},{7,15},{8,0},{9,1},... | collective-permute-start | bytes 98312 | tf_op jit(solution)/shard_map/ppermute | solution.py:343
  4.8 1.2 %curves.1 = (bf16[64,128]{1,0:T(8,128)(2,1)S(1)}, bf16[128,64]{1,0:T(8,128)(2,1)S(1)}, f32[2,16]{1,0:T(2,128)S(1)}, bf16[16,128]{1,0:T(8,128)(2,1)S(1)}) custom-call(bf16[128,128]{1,0:T(8,128)(2,1)} %bitcast.19, bf16[16,32]{1,0:T(8,128)(2,1)} %bitcast.20, f32[2,16]{1,0:T(2,128)} %bitcast.21), custom_call_target="tpu_custom_call" | custom-call | flops 1000000 | bytes 1000000 | tf_op jit(solution)/shard_map/curves/pallas_call | solution.py:327
  6.0 1.2 %collective-permute-done.arrived = bf16[128,128]{1,0:T(8,128)(2,1)S(1)} collective-permute-done((bf16[128,128]{1,0:T(8,128)(2,1)}, bf16[128,128]{1,0:T(8,128)(2,1)S(1)}, u32[]{:S(2)}, u32[]{:S(2)}) %collective-permute-start) | collective-permute-done | bytes 32800 | tf_op jit(solution)/shard_map/ppermute | solution.py:343
  7.4 2.5 %collective-permute-start.3 = (bf16[128,128]{1,0:T(8,128)(2,1)S(1)}, bf16[128,128]{1,0:T(8,128)(2,1)S(1)}, u32[]{:S(2)}, u32[]{:S(2)}) collective-permute-start(bf16[128,128]{1,0:T(8,128)(2,1)S(1)} %curves2.1.refs_8_.refs_0_), channel_id=1, source_target_pairs={{0,6},{1,7},{2,4},{3,5},{4,2},{5,3},{6,0},{7,1},{8,14},{9,15},{10,... | collective-permute-start | bytes 98312 | tf_op jit(solution)/shard_map/ppermute | solution.py:343
  9.9 0.7 %collective-permute-start.2 = (bf16[128,128]{1,0:T(8,128)(2,1)S(1)}, bf16[128,128]{1,0:T(8,128)(2,1)S(1)}, u32[]{:S(2)}, u32[]{:S(2)}) collective-permute-start(bf16[128,128]{1,0:T(8,128)(2,1)S(1)} %curves2.1.refs_8_.refs_0_), channel_id=1, source_target_pairs={{0,4},{1,5},{2,6},{3,7},{4,0},{5,1},{6,2},{7,3},{8,12},{9,13},{10,... | collective-permute-start | bytes 98312 | tf_op jit(solution)/shard_map/ppermute | solution.py:343
  10.9 2.4 %prep.1 = (bf16[1024,1536]{1,0:T(8,128)(2,1)S(1)}, bf16[1024,1536]{1,0:T(8,128)(2,1)S(1)}, bf16[256,1536]{1,0:T(8,128)(2,1)S(1)}, s32[12,128]{1,0:T(8,128)S(1)},...) custom-call(s32[2,1536]{1,0:T(2,128)} %refs_0_.1, ...), custom_call_target="tpu_custom_call" | custom-call | flops 400000000 | bytes 8000000 | tf_op jit(solution)/shard_map/prep/pallas_call | solution.py:327
  13.8 0.7 %collective-permute-done.1.refs_1_ = bf16[128,128]{1,0:T(8,128)(2,1)S(1)} collective-permute-done((bf16[128,128]{1,0:T(8,128)(2,1)S(1)}, bf16[128,128]{1,0:T(8,128)(2,1)S(1)}, u32[]{:S(2)}, u32[]{:S(2)}) %collective-permute-start.1) | collective-permute-done | bytes 32800 | tf_op jit(solution)/shard_map/ppermute | solution.py:343
  15.2 0.7 %collective-permute-done.4.curves.partner = bf16[512,128]{1,0:T(8,128)(2,1)S(1)} collective-permute-done((bf16[512,128]{1,0:T(8,128)(2,1)S(1)}, bf16[512,128]{1,0:T(8,128)(2,1)S(1)}, u32[]{:S(2)}, u32[]{:S(2)}) %collective-permute-start.4) | collective-permute-done | bytes 131104 | tf_op jit(solution)/shard_map/ppermute | solution.py:343
  15.9 1.6 %price2.1 = (f32[128,128]{1,0:T(8,128)S(1)}, bf16[128,128]{1,0:T(8,128)(2,1)S(1)}, f32[128,1536]{1,0:T(8,128)S(1)}, f32[128,1536]{1,0:T(8,128)S(1)}) custom-call(bf16[512,128]{1,0:T(8,128)(2,1)S(1)} %collective-permute-done.4.curves.partner, f32[128,1536]{1,0:T(8,128)S(1)} %get-tuple-element.37.forward_ref, f32[128,1536]{1,0:T(8,128)S(1)} %get-tuple-element.38.annuity_ref, ...), custom_call_target="tpu_custom_call" | custom-call | flops 1000000 | bytes 1000000 | tf_op jit(solution)/shard_map/price2/pallas_call | solution.py:327
  17.8 1.1 %collective-permute-done.5.arrived = bf16[128,128]{1,0:T(8,128)(2,1)S(1)} collective-permute-done((bf16[128,128]{1,0:T(8,128)(2,1)S(1)}, bf16[128,128]{1,0:T(8,128)(2,1)S(1)}, u32[]{:S(2)}, u32[]{:S(2)}) %collective-permute-start.5) | collective-permute-done | bytes 32800 | tf_op jit(solution)/shard_map/ppermute | solution.py:343
  19.5 3.4 %collective-permute-done.6 = bf16[144,128]{1,0:T(8,128)(2,1)S(1)} collective-permute-done((bf16[144,128]{1,0:T(8,128)(2,1)S(1)}, bf16[144,128]{1,0:T(8,128)(2,1)S(1)}, u32[]{:S(2)}, u32[]{:S(2)}) %collective-permute-start.6) | collective-permute-done | bytes 36896 | tf_op jit(solution)/shard_map/ppermute | solution.py:343
  22.9 3.7 %collective-permute-start.9 = (bf16[144,128]{1,0:T(8,128)(2,1)S(1)}, bf16[144,128]{1,0:T(8,128)(2,1)S(1)}, u32[]{:S(2)}, u32[]{:S(2)}) collective-permute-start(bf16[144,128]{1,0:T(8,128)(2,1)S(1)} %add_convert_fusion.refs_0_), channel_id=1, source_target_pairs={{0,12},{1,13},{2,14},{3,15},{4,8},{5,9},{6,10},{7,11},{8,4},{9,5},... | collective-permute-start | bytes 110600 | tf_op jit(solution)/shard_map/ppermute | solution.py:343
  26.6 0.8 %collective-permute-start.7 = (bf16[144,128]{1,0:T(8,128)(2,1)S(1)}, bf16[144,128]{1,0:T(8,128)(2,1)S(1)}, u32[]{:S(2)}, u32[]{:S(2)}) collective-permute-start(bf16[144,128]{1,0:T(8,128)(2,1)S(1)} %add_convert_fusion.refs_0_), channel_id=1, source_target_pairs={{0,4},{1,5},{2,6},{3,7},{4,0},{5,1},{6,2},{7,3},{8,12},{9,13},{10,... | collective-permute-start | bytes 110600 | tf_op jit(solution)/shard_map/ppermute | solution.py:343
  27.3 1.4 %collective-permute-done.9.refs_3_ = bf16[144,128]{1,0:T(8,128)(2,1)S(1)} collective-permute-done((bf16[144,128]{1,0:T(8,128)(2,1)S(1)}, bf16[144,128]{1,0:T(8,128)(2,1)S(1)}, u32[]{:S(2)}, u32[]{:S(2)}) %collective-permute-start.9) | collective-permute-done | bytes 36896 | tf_op jit(solution)/shard_map/ppermute | solution.py:343
  28.7 2.7 %collective-permute-done.8.refs_2_ = bf16[144,128]{1,0:T(8,128)(2,1)S(1)} collective-permute-done((bf16[144,128]{1,0:T(8,128)(2,1)S(1)}, bf16[144,128]{1,0:T(8,128)(2,1)S(1)}, u32[]{:S(2)}, u32[]{:S(2)}) %collective-permute-start.8) | collective-permute-done | bytes 36896 | tf_op jit(solution)/shard_map/ppermute | solution.py:343
  31.7 1.2 %collective-permute-done.11.cots_partner = bf16[128,128]{1,0:T(8,128)(2,1)S(1)} collective-permute-done((bf16[128,128]{1,0:T(8,128)(2,1)S(1)}, bf16[128,128]{1,0:T(8,128)(2,1)S(1)}, u32[]{:S(2)}, u32[]{:S(2)}) %collective-permute-start.11) | collective-permute-done | bytes 32800 | tf_op jit(solution)/shard_map/ppermute | solution.py:343
  32.9 1.2 %adjoint.1 = (bf16[512,128]{1,0:T(8,128)(2,1)S(1)}, bf16[128,1536]{1,0:T(8,128)(2,1)S(1)}, bf16[128,1536]{1,0:T(8,128)(2,1)S(1)}) custom-call(bf16[512,128]{1,0:T(8,128)(2,1)S(1)} %collective-permute-done.4.curves.partner, bf16[128,128]{1,0:T(8,128)(2,1)S(1)} %get-tuple-element.48.cots_mine, bf16[128,128]{1,0:T(8,128)(2,1)S(1)} %collective-permute-done.11.cots_partner, ...), custom_call_target="tpu_custom_call" | custom-call | flops 1000000 | bytes 1000000 | tf_op jit(solution)/shard_map/adjoint/pallas_call | solution.py:327
  34.3 1.0 %keep.1.kept = f32[512,128]{1,0:T(8,128)S(1)} custom-call(bf16[512,128]{1,0:T(8,128)(2,1)S(1)} %join.1.curves.mine, bf16[128,1536]{1,0:T(8,128)(2,1)S(1)} %get-tuple-element.51.fwd_cots, bf16[128,1536]{1,0:T(8,128)(2,1)S(1)} %get-tuple-element.52.ann_cots, bf16[1024,1536]{1,0:T(8,128)(2,1)S(1)} %get-tuple-element.35.w_fwd, ...), custom_call_target="tpu_custom_call" | custom-call | flops 200000000 | bytes 4000000 | tf_op jit(solution)/shard_map/keep/pallas_call | solution.py:327
  36.2 2.9 %collective-permute-start.15 = (bf16[128,128]{1,0:T(8,128)(2,1)S(1)}, bf16[128,128]{1,0:T(8,128)(2,1)S(1)}, u32[]{:S(2)}, u32[]{:S(2)}) collective-permute-start(bf16[128,128]{1,0:T(8,128)(2,1)S(1)} %get-tuple-element.57), channel_id=1, source_target_pairs={{0,6},{1,7},{2,4},{3,5},{4,2},{5,3},{6,0},{7,1},{8,14},{9,15},{10,... | collective-permute-start | bytes 98312 | tf_op jit(solution)/shard_map/ppermute | solution.py:343
  39.1 1.5 %collective-permute-start.10 = (f32[16]{0:T(128)S(1)}, f32[16]{0:T(128)S(1)}, u32[]{:S(2)}, u32[]{:S(2)}) collective-permute-start(f32[16]{0:T(128)S(1)} %bitcast.16), channel_id=1, source_target_pairs={{0,16},{16,0},{1,17},{17,1},{2,18},{18,2},{3,19},{19,3},{4,20},{20... | collective-permute-start | bytes 200 | tf_op jit(solution)/shard_map/ppermute | solution.py:358
  40.6 0.7 %collective-permute-done.15.refs_2_ = bf16[128,128]{1,0:T(8,128)(2,1)S(1)} collective-permute-done((bf16[128,128]{1,0:T(8,128)(2,1)S(1)}, bf16[128,128]{1,0:T(8,128)(2,1)S(1)}, u32[]{:S(2)}, u32[]{:S(2)}) %collective-permute-start.15) | collective-permute-done | bytes 32800 | tf_op jit(solution)/shard_map/ppermute | solution.py:343
  41.4 2.1 %collective-permute-start.16 = (bf16[64,128]{1,0:T(8,128)(2,1)S(1)}, bf16[64,128]{1,0:T(8,128)(2,1)S(1)}, u32[]{:S(2)}, u32[]{:S(2)}) collective-permute-start(bf16[64,128]{1,0:T(8,128)(2,1)S(1)} %get-tuple-element.59), channel_id=1, source_target_pairs={{0,8},{1,9},{2,10},{3,11},{4,12},{5,13},{6,14},{7,15},{8,0},{9,1},... | collective-permute-start | bytes 49160 | tf_op jit(solution)/shard_map/ppermute | solution.py:343
  44.0 2.1 %collective-permute-done.16.arrived = bf16[64,128]{1,0:T(8,128)(2,1)S(1)} collective-permute-done((bf16[64,128]{1,0:T(8,128)(2,1)S(1)}, bf16[64,128]{1,0:T(8,128)(2,1)S(1)}, u32[]{:S(2)}, u32[]{:S(2)}) %collective-permute-start.16) | collective-permute-done | bytes 16416 | tf_op jit(solution)/shard_map/ppermute | solution.py:343
  46.1 0.8 %factors.1 = f32[128,128]{1,0:T(8,128)} custom-call(f32[64,128]{1,0:T(8,128)S(1)} %get-tuple-element.58.kept, bf16[64,128]{1,0:T(8,128)(2,1)S(1)} %collective-permute-done.16.arrived, bf16[128,64]{1,0:T(8,128)(2,1)S(1)} %get-tuple-element.33.basis), custom_call_target="tpu_custom_call" | custom-call | flops 1000000 | bytes 1000000 | tf_op jit(solution)/shard_map/factors/pallas_call | solution.py:327
  (25 shorter events, 4.4 us)
Async XLA Ops:
  0.6 6.6 %collective-permute-start = (bf16[128,128]{1,0:T(8,128)(2,1)}, bf16[128,128]{1,0:T(8,128)(2,1)S(1)}, u32[]{:S(2)}, u32[]{:S(2)}) collective-permute-start(bf16[128,128]{1,0:T(8,128)(2,1)} %bitcast.18), channel_id=1, source_target_pairs={{0,8},{1,9},{2,10},{3,11},{4,12},{5,13},{6,14},{7,15},{8,0},{9,1},... | collective-permute-start | bytes 98312 | tf_op jit(solution)/shard_map/ppermute | solution.py:343
  7.4 5.9 %collective-permute-start.3 = (bf16[128,128]{1,0:T(8,128)(2,1)S(1)}, bf16[128,128]{1,0:T(8,128)(2,1)S(1)}, u32[]{:S(2)}, u32[]{:S(2)}) collective-permute-start(bf16[128,128]{1,0:T(8,128)(2,1)S(1)} %curves2.1.refs_8_.refs_0_), channel_id=1, source_target_pairs={{0,6},{1,7},{2,4},{3,5},{4,2},{5,3},{6,0},{7,1},{8,14},{9,15},{10,... | collective-permute-start | bytes 98312 | tf_op jit(solution)/shard_map/ppermute | solution.py:343
  9.9 3.9 %collective-permute-start.2 = (bf16[128,128]{1,0:T(8,128)(2,1)S(1)}, bf16[128,128]{1,0:T(8,128)(2,1)S(1)}, u32[]{:S(2)}, u32[]{:S(2)}) collective-permute-start(bf16[128,128]{1,0:T(8,128)(2,1)S(1)} %curves2.1.refs_8_.refs_0_), channel_id=1, source_target_pairs={{0,4},{1,5},{2,6},{3,7},{4,0},{5,1},{6,2},{7,3},{8,12},{9,13},{10,... | collective-permute-start | bytes 98312 | tf_op jit(solution)/shard_map/ppermute | solution.py:343
  10.6 3.9 %collective-permute-start.1 = (bf16[128,128]{1,0:T(8,128)(2,1)S(1)}, bf16[128,128]{1,0:T(8,128)(2,1)S(1)}, u32[]{:S(2)}, u32[]{:S(2)}) collective-permute-start(bf16[128,128]{1,0:T(8,128)(2,1)S(1)} %curves2.1.refs_8_.refs_0_), channel_id=1, source_target_pairs={{0,2},{1,3},{2,0},{3,1},{4,6},{5,7},{6,4},{7,5},{8,10},{9,11},{10,... | collective-permute-start | bytes 98312 | tf_op jit(solution)/shard_map/ppermute | solution.py:343
  14.5 1.4 %collective-permute-start.4 = (bf16[512,128]{1,0:T(8,128)(2,1)S(1)}, bf16[512,128]{1,0:T(8,128)(2,1)S(1)}, u32[]{:S(2)}, u32[]{:S(2)}) collective-permute-start(bf16[512,128]{1,0:T(8,128)(2,1)S(1)} %join.1.curves.mine), channel_id=1, source_target_pairs={{0,1},{1,0},{2,3},{3,2},{4,5},{5,4},{6,7},{7,6},{8,9},{9,8},{10,11... | collective-permute-start | bytes 393224 | tf_op jit(solution)/shard_map/ppermute | solution.py:343
  17.5 1.3 %collective-permute-start.5 = (bf16[128,128]{1,0:T(8,128)(2,1)S(1)}, bf16[128,128]{1,0:T(8,128)(2,1)S(1)}, u32[]{:S(2)}, u32[]{:S(2)}) collective-permute-start(bf16[128,128]{1,0:T(8,128)(2,1)S(1)} %get-tuple-element.45), channel_id=1, source_target_pairs={{0,1},{1,0},{2,3},{3,2},{4,5},{5,4},{6,7},{7,6},{8,9},{9,8},{10,11... | collective-permute-start | bytes 98312 | tf_op jit(solution)/shard_map/ppermute | solution.py:343
  18.8 4.0 %collective-permute-start.6 = (bf16[144,128]{1,0:T(8,128)(2,1)S(1)}, bf16[144,128]{1,0:T(8,128)(2,1)S(1)}, u32[]{:S(2)}, u32[]{:S(2)}) collective-permute-start(bf16[144,128]{1,0:T(8,128)(2,1)S(1)} %pair.1), channel_id=1, source_target_pairs={{0,2},{1,3},{2,0},{3,1},{4,6},{5,7},{6,4},{7,5},{8,10},{9,11},{10,... | collective-permute-start | bytes 110600 | tf_op jit(solution)/shard_map/ppermute | solution.py:343
  22.9 5.8 %collective-permute-start.9 = (bf16[144,128]{1,0:T(8,128)(2,1)S(1)}, bf16[144,128]{1,0:T(8,128)(2,1)S(1)}, u32[]{:S(2)}, u32[]{:S(2)}) collective-permute-start(bf16[144,128]{1,0:T(8,128)(2,1)S(1)} %add_convert_fusion.refs_0_), channel_id=1, source_target_pairs={{0,12},{1,13},{2,14},{3,15},{4,8},{5,9},{6,10},{7,11},{8,4},{9,5},... | collective-permute-start | bytes 110600 | tf_op jit(solution)/shard_map/ppermute | solution.py:343
  26.5 4.9 %collective-permute-start.8 = (bf16[144,128]{1,0:T(8,128)(2,1)S(1)}, bf16[144,128]{1,0:T(8,128)(2,1)S(1)}, u32[]{:S(2)}, u32[]{:S(2)}) collective-permute-start(bf16[144,128]{1,0:T(8,128)(2,1)S(1)} %add_convert_fusion.refs_0_), channel_id=1, source_target_pairs={{0,8},{1,9},{2,10},{3,11},{4,12},{5,13},{6,14},{7,15},{8,0},{9,1},... | collective-permute-start | bytes 110600 | tf_op jit(solution)/shard_map/ppermute | solution.py:343
  26.6 4.9 %collective-permute-start.7 = (bf16[144,128]{1,0:T(8,128)(2,1)S(1)}, bf16[144,128]{1,0:T(8,128)(2,1)S(1)}, u32[]{:S(2)}, u32[]{:S(2)}) collective-permute-start(bf16[144,128]{1,0:T(8,128)(2,1)S(1)} %add_convert_fusion.refs_0_), channel_id=1, source_target_pairs={{0,4},{1,5},{2,6},{3,7},{4,0},{5,1},{6,2},{7,3},{8,12},{9,13},{10,... | collective-permute-start | bytes 110600 | tf_op jit(solution)/shard_map/ppermute | solution.py:343
  31.6 1.3 %collective-permute-start.11 = (bf16[128,128]{1,0:T(8,128)(2,1)S(1)}, bf16[128,128]{1,0:T(8,128)(2,1)S(1)}, u32[]{:S(2)}, u32[]{:S(2)}) collective-permute-start(bf16[128,128]{1,0:T(8,128)(2,1)S(1)} %get-tuple-element.48.cots_mine), channel_id=1, source_target_pairs={{0,1},{1,0},{2,3},{3,2},{4,5},{5,4},{6,7},{7,6},{8,9},{9,8},{10,11... | collective-permute-start | bytes 98312 | tf_op jit(solution)/shard_map/ppermute | solution.py:343
  34.1 1.4 %collective-permute-start.12 = (bf16[512,128]{1,0:T(8,128)(2,1)S(1)}, bf16[512,128]{1,0:T(8,128)(2,1)S(1)}, u32[]{:S(2)}, u32[]{:S(2)}) collective-permute-start(bf16[512,128]{1,0:T(8,128)(2,1)S(1)} %get-tuple-element.53), channel_id=1, source_target_pairs={{0,1},{1,0},{2,3},{3,2},{4,5},{5,4},{6,7},{7,6},{8,9},{9,8},{10,11... | collective-permute-start | bytes 393224 | tf_op jit(solution)/shard_map/ppermute | solution.py:343
  35.5 5.0 %collective-permute-start.13 = (bf16[128,128]{1,0:T(8,128)(2,1)S(1)}, bf16[128,128]{1,0:T(8,128)(2,1)S(1)}, u32[]{:S(2)}, u32[]{:S(2)}) collective-permute-start(bf16[128,128]{1,0:T(8,128)(2,1)S(1)} %get-tuple-element.55), channel_id=1, source_target_pairs={{0,2},{1,3},{2,0},{3,1},{4,6},{5,7},{6,4},{7,5},{8,10},{9,11},{10,... | collective-permute-start | bytes 98312 | tf_op jit(solution)/shard_map/ppermute | solution.py:343
  36.2 4.4 %collective-permute-start.14 = (bf16[128,128]{1,0:T(8,128)(2,1)S(1)}, bf16[128,128]{1,0:T(8,128)(2,1)S(1)}, u32[]{:S(2)}, u32[]{:S(2)}) collective-permute-start(bf16[128,128]{1,0:T(8,128)(2,1)S(1)} %get-tuple-element.56), channel_id=1, source_target_pairs={{0,4},{1,5},{2,6},{3,7},{4,0},{5,1},{6,2},{7,3},{8,12},{9,13},{10,... | collective-permute-start | bytes 98312 | tf_op jit(solution)/shard_map/ppermute | solution.py:343
  36.2 5.1 %collective-permute-start.15 = (bf16[128,128]{1,0:T(8,128)(2,1)S(1)}, bf16[128,128]{1,0:T(8,128)(2,1)S(1)}, u32[]{:S(2)}, u32[]{:S(2)}) collective-permute-start(bf16[128,128]{1,0:T(8,128)(2,1)S(1)} %get-tuple-element.57), channel_id=1, source_target_pairs={{0,6},{1,7},{2,4},{3,5},{4,2},{5,3},{6,0},{7,1},{8,14},{9,15},{10,... | collective-permute-start | bytes 98312 | tf_op jit(solution)/shard_map/ppermute | solution.py:343
  39.1 4.4 %collective-permute-start.10 = (f32[16]{0:T(128)S(1)}, f32[16]{0:T(128)S(1)}, u32[]{:S(2)}, u32[]{:S(2)}) collective-permute-start(f32[16]{0:T(128)S(1)} %bitcast.16), channel_id=1, source_target_pairs={{0,16},{16,0},{1,17},{17,1},{2,18},{18,2},{3,19},{19,3},{4,20},{20... | collective-permute-start | bytes 200 | tf_op jit(solution)/shard_map/ppermute | solution.py:358
  41.4 4.7 %collective-permute-start.16 = (bf16[64,128]{1,0:T(8,128)(2,1)S(1)}, bf16[64,128]{1,0:T(8,128)(2,1)S(1)}, u32[]{:S(2)}, u32[]{:S(2)}) collective-permute-start(bf16[64,128]{1,0:T(8,128)(2,1)S(1)} %get-tuple-element.59), channel_id=1, source_target_pairs={{0,8},{1,9},{2,10},{3,11},{4,12},{5,13},{6,14},{7,15},{8,0},{9,1},... | collective-permute-start | bytes 49160 | tf_op jit(solution)/shard_map/ppermute | solution.py:343

commit v6 on v5

--- a/solution.py
+++ b/solution.py
@@ -13,7 +13,7 @@
 NT = (((1,), (1,)), ((), ()))
 TN = (((0,), (0,)), ((), ()))
 LANES = 128
-TILE = 512
+TILE = 768
 VMEM = pl.BlockSpec(memory_space=pltpu.VMEM)
 HBM = pl.BlockSpec(memory_space=pltpu.HBM)
 VMEM_LIMIT = 8 * 2**20
@@ -173,9 +173,18 @@
         )
 
 
+def option_terms(forward, strike, vol):
+    moneyness = forward - strike
+    return moneyness, jnp.exp(jnp.abs(moneyness) * (-1.0 / vol))
+
+
+def swaption_payoff(moneyness, e, vol):
+    return jnp.maximum(moneyness, 0.0) + vol * log1p_unit(e)
+
+
 def price_kernel(
     curves, forward_ref, annuity_ref, w_fwd, w_disc, onehot, kind_ref, notional_ref, strike_ref,
-    vol_ref, threshold_ref, keep, send, fwd_scale, ann_scale,
+    vol_ref, threshold_ref, keep, send, forward_out, annuity_out,
 ):
     near, rows = curves.shape
     trades = w_fwd.shape[1]
@@ -192,20 +201,13 @@
         annuity = annuity_ref[:, lanes] + lax.dot_general(
             discount, w_disc[near:, lanes], TN, preferred_element_type=F32
         )
+        forward_out[:, lanes] = forward
+        annuity_out[:, lanes] = annuity
         vol = param_row(vol_ref, t, tile)
-        notional = param_row(notional_ref, t, tile)
         option = jnp.broadcast_to(param_row(kind_ref, t, tile) == 1, (rows, tile))
-        moneyness = forward - param_row(strike_ref, t, tile)
-        scaled = moneyness * (1.0 / vol)
-        e = jnp.exp(-jnp.abs(scaled))
-        softplus = jnp.maximum(scaled, 0.0) + log1p_unit(e)
-        sigmoid = jnp.where(scaled >= 0.0, 1.0, e) / (1.0 + e)
-        payoff = jnp.where(option, vol * softplus, moneyness)
-        slope = jnp.where(option, sigmoid, 1.0)
-        scaled_annuity = notional * annuity
-        value = (scaled_annuity * payoff).astype(BF16)
-        fwd_scale[:, lanes] = scaled_annuity * slope
-        ann_scale[:, lanes] = notional * payoff
+        moneyness, e = option_terms(forward, param_row(strike_ref, t, tile), vol)
+        payoff = jnp.where(option, swaption_payoff(moneyness, e, vol), moneyness)
+        value = (param_row(notional_ref, t, tile) * annuity * payoff).astype(BF16)
         total += lax.dot_general(onehot[:, lanes], value, NT, preferred_element_type=F32)
     keep[...] = total[:half]
     send[...] = total[half:].astype(BF16)
@@ -215,6 +217,23 @@
     square = iota((sets, sets), 0) == iota((sets, sets), 1)
     column = jnp.sum(jnp.where(square, threshold_ref[...], 0.0), axis=1, keepdims=True)
     keep[own, :] = keep[own, :] - column
+
+
+def scale_kernel(
+    forward_ref, annuity_ref, kind_ref, notional_ref, strike_ref, vol_ref, fwd_scale, ann_scale
+):
+    rows, trades = forward_ref.shape
+    tile = TILE if trades % TILE == 0 else trades
+    for t in range(0, trades, tile):
+        lanes = slice(t, t + tile)
+        vol = param_row(vol_ref, t, tile)
+        notional = param_row(notional_ref, t, tile)
+        option = jnp.broadcast_to(param_row(kind_ref, t, tile) == 1, (rows, tile))
+        moneyness, e = option_terms(forward_ref[:, lanes], param_row(strike_ref, t, tile), vol)
+        payoff = jnp.where(option, swaption_payoff(moneyness, e, vol), moneyness)
+        sigmoid = jnp.where(moneyness >= 0.0, 1.0, e) / (1.0 + e)
+        fwd_scale[:, lanes] = notional * annuity_ref[:, lanes] * jnp.where(option, sigmoid, 1.0)
+        ann_scale[:, lanes] = notional * payoff
 
 
 def pair_kernel(keep, arrived, extra, out):
@@ -374,7 +393,7 @@
     all_rows = height * devices
     trades = trade_set.shape[0]
     shape = jax.ShapeDtypeStruct
-    extra_rows = -(-max(1, half_sets // rows) * 2 * dates // 16) * 16
+    extra_rows = -(-max(1, half_sets // rows) * 2 * dates // 8) * 8
     lane_rows = (trades // LANES, LANES)
     dma = pltpu.SemaphoreType.DMA
 
@@ -413,11 +432,15 @@
         half_price_kernel, "price1", [shape((rows, trades), F32)] * 2,
         flops=400_000_000, moved=4_000_000,
     )(mine, w_fwd, w_disc)
-    keep, send, fwd_scale, ann_scale = call(
+    keep, send, forward, annuity = call(
         price_kernel, "price2",
         [shape((half_sets, rows), F32), shape((half_sets, rows), BF16),
          shape((rows, trades), F32), shape((rows, trades), F32)],
     )(partner, forward, annuity, w_fwd, w_disc, onehot, *params)
+    fwd_scale, ann_scale = call(
+        scale_kernel, "scales", [shape((rows, trades), F32)] * 2,
+        flops=400_000_000, moved=4_000_000,
+    )(forward, annuity, *params[:-1])
 
     total = call(pair_kernel, "pair", shape((half_sets + extra_rows, rows), BF16))(
         keep, swap(send, 1), extra

time: 47.1 us -> 46.8 us (level)
  waiting for transfers between devices: 15.9 us -> 15.2 us
    ppermute x16, waiting for transfers between devices: 15.9 us -> 15.1 us  [swap(): return lax.ppermute(x, 'trade', [(i, i ^ mask) for i in range(n)])]
    pallas_call x13 -> x14, Pallas kernels: 9.28 us -> 9.72 us  [run(): pl.pallas_call(kernel, in_specs=spaces, out_specs=jax.tree.map(lambda _:...]
  transfers between devices with their start and end apart: 17 -> 17, of which waited for: 12 -> 12; matrix products, arithmetic and copies ran while one was open for 1% -> 1% of each run, Pallas kernels for 11% -> 13%
where the time goes in v6:
time: 46.8 us; the launch traced here: 46.6 us
  starting transfers between devices  20.4 us (44%)
  waiting for transfers between devices  15.2 us (32%)
  Pallas kernels  9.72 us (21%)
  between operations  0.74 us (2%)
  other arithmetic  0.53 us (1%)
    ppermute x16, starting transfers between devices, swap(): return lax.ppermute(x, 'trade', [(i, i ^ mask) for i in range(n)])  18.9 us
    ppermute x16, waiting for transfers between devices, swap(): return lax.ppermute(x, 'trade', [(i, i ^ mask) for i in range(n)])  15.1 us
    pallas_call x14, Pallas kernels, run(): pl.pallas_call(kernel, in_specs=spaces, out_specs=jax.tree.map(lambda _:...  9.72 us
    ppermute x1, starting transfers between devices, sum_over(): lax.ppermute(x, axis, [(i, (i + shift) % n) for i in range(n)])  1.49 us
  transfers between devices with their start and end apart: 17, of which 12 were waited for; matrix products, arithmetic and copies ran while one was open for 1% of the time, Pallas kernels for 13%

profile of v6, /device:TPU:0, one launch (start us, length us, event | category | flops | bytes accessed | tf_op | source)
XLA Modules:
  0.0 46.6 jit_solution(3194309513202950934)
XLA Ops:
  0.6 4.1 %collective-permute-start = (bf16[128,128]{1,0:T(8,128)(2,1)}, bf16[128,128]{1,0:T(8,128)(2,1)S(1)}, u32[]{:S(2)}, u32[]{:S(2)}) collective-permute-start(bf16[128,128]{1,0:T(8,128)(2,1)} %bitcast.18), channel_id=1, source_target_pairs={{0,8},{1,9},{2,10},{3,11},{4,12},{5,13},{6,14},{7,15},{8,0},{9,1},... | collective-permute-start | bytes 98312 | tf_op jit(solution)/shard_map/ppermute | solution.py:362
  4.8 1.2 %curves.1 = (bf16[64,128]{1,0:T(8,128)(2,1)S(1)}, bf16[128,64]{1,0:T(8,128)(2,1)S(1)}, f32[2,16]{1,0:T(2,128)S(1)}, bf16[8,128]{1,0:T(8,128)(2,1)S(1)}) custom-call(bf16[128,128]{1,0:T(8,128)(2,1)} %bitcast.19, bf16[16,32]{1,0:T(8,128)(2,1)} %bitcast.20, f32[2,16]{1,0:T(2,128)} %bitcast.21), custom_call_target="tpu_custom_call" | custom-call | flops 1000000 | bytes 1000000 | tf_op jit(solution)/shard_map/curves/pallas_call | solution.py:346
  6.0 1.2 %collective-permute-done.arrived = bf16[128,128]{1,0:T(8,128)(2,1)S(1)} collective-permute-done((bf16[128,128]{1,0:T(8,128)(2,1)}, bf16[128,128]{1,0:T(8,128)(2,1)S(1)}, u32[]{:S(2)}, u32[]{:S(2)}) %collective-permute-start) | collective-permute-done | bytes 32800 | tf_op jit(solution)/shard_map/ppermute | solution.py:362
  7.4 2.5 %collective-permute-start.3 = (bf16[128,128]{1,0:T(8,128)(2,1)S(1)}, bf16[128,128]{1,0:T(8,128)(2,1)S(1)}, u32[]{:S(2)}, u32[]{:S(2)}) collective-permute-start(bf16[128,128]{1,0:T(8,128)(2,1)S(1)} %curves2.1.refs_8_.refs_0_), channel_id=1, source_target_pairs={{0,6},{1,7},{2,4},{3,5},{4,2},{5,3},{6,0},{7,1},{8,14},{9,15},{10,... | collective-permute-start | bytes 98312 | tf_op jit(solution)/shard_map/ppermute | solution.py:362
  9.9 0.7 %collective-permute-start.2 = (bf16[128,128]{1,0:T(8,128)(2,1)S(1)}, bf16[128,128]{1,0:T(8,128)(2,1)S(1)}, u32[]{:S(2)}, u32[]{:S(2)}) collective-permute-start(bf16[128,128]{1,0:T(8,128)(2,1)S(1)} %curves2.1.refs_8_.refs_0_), channel_id=1, source_target_pairs={{0,4},{1,5},{2,6},{3,7},{4,0},{5,1},{6,2},{7,3},{8,12},{9,13},{10,... | collective-permute-start | bytes 98312 | tf_op jit(solution)/shard_map/ppermute | solution.py:362
  10.9 2.4 %prep.1 = (bf16[1024,1536]{1,0:T(8,128)(2,1)S(1)}, bf16[1024,1536]{1,0:T(8,128)(2,1)S(1)}, bf16[256,1536]{1,0:T(8,128)(2,1)S(1)}, s32[12,128]{1,0:T(8,128)S(1)},...) custom-call(s32[2,1536]{1,0:T(2,128)} %refs_0_.1, ...), custom_call_target="tpu_custom_call" | custom-call | flops 400000000 | bytes 8000000 | tf_op jit(solution)/shard_map/prep/pallas_call | solution.py:346
  13.8 0.7 %collective-permute-done.1.refs_1_ = bf16[128,128]{1,0:T(8,128)(2,1)S(1)} collective-permute-done((bf16[128,128]{1,0:T(8,128)(2,1)S(1)}, bf16[128,128]{1,0:T(8,128)(2,1)S(1)}, u32[]{:S(2)}, u32[]{:S(2)}) %collective-permute-start.1) | collective-permute-done | bytes 32800 | tf_op jit(solution)/shard_map/ppermute | solution.py:362
  15.2 0.7 %collective-permute-done.4.curves.partner = bf16[512,128]{1,0:T(8,128)(2,1)S(1)} collective-permute-done((bf16[512,128]{1,0:T(8,128)(2,1)S(1)}, bf16[512,128]{1,0:T(8,128)(2,1)S(1)}, u32[]{:S(2)}, u32[]{:S(2)}) %collective-permute-start.4) | collective-permute-done | bytes 131104 | tf_op jit(solution)/shard_map/ppermute | solution.py:362
  15.9 1.3 %price2.1 = (f32[128,128]{1,0:T(8,128)S(1)}, bf16[128,128]{1,0:T(8,128)(2,1)S(1)}, f32[128,1536]{1,0:T(8,128)S(1)}, f32[128,1536]{1,0:T(8,128)S(1)}) custom-call(bf16[512,128]{1,0:T(8,128)(2,1)S(1)} %collective-permute-done.4.curves.partner, f32[128,1536]{1,0:T(8,128)S(1)} %get-tuple-element.39.forward_ref, f32[128,1536]{1,0:T(8,128)S(1)} %get-tuple-element.40.annuity_ref, ...), custom_call_target="tpu_custom_call" | custom-call | flops 1000000 | bytes 1000000 | tf_op jit(solution)/shard_map/price2/pallas_call | solution.py:346
  17.5 1.1 %collective-permute-done.5.arrived = bf16[128,128]{1,0:T(8,128)(2,1)S(1)} collective-permute-done((bf16[128,128]{1,0:T(8,128)(2,1)S(1)}, bf16[128,128]{1,0:T(8,128)(2,1)S(1)}, u32[]{:S(2)}, u32[]{:S(2)}) %collective-permute-start.5) | collective-permute-done | bytes 32800 | tf_op jit(solution)/shard_map/ppermute | solution.py:362
  19.2 3.4 %collective-permute-done.6 = bf16[136,128]{1,0:T(8,128)(2,1)S(1)} collective-permute-done((bf16[136,128]{1,0:T(8,128)(2,1)S(1)}, bf16[136,128]{1,0:T(8,128)(2,1)S(1)}, u32[]{:S(2)}, u32[]{:S(2)}) %collective-permute-start.6) | collective-permute-done | bytes 34848 | tf_op jit(solution)/shard_map/ppermute | solution.py:362
  22.6 3.7 %collective-permute-start.9 = (bf16[136,128]{1,0:T(8,128)(2,1)S(1)}, bf16[136,128]{1,0:T(8,128)(2,1)S(1)}, u32[]{:S(2)}, u32[]{:S(2)}) collective-permute-start(bf16[136,128]{1,0:T(8,128)(2,1)S(1)} %add_convert_fusion.refs_0_), channel_id=1, source_target_pairs={{0,12},{1,13},{2,14},{3,15},{4,8},{5,9},{6,10},{7,11},{8,4},{9,5},... | collective-permute-start | bytes 104456 | tf_op jit(solution)/shard_map/ppermute | solution.py:362
  26.2 0.8 %collective-permute-start.7 = (bf16[136,128]{1,0:T(8,128)(2,1)S(1)}, bf16[136,128]{1,0:T(8,128)(2,1)S(1)}, u32[]{:S(2)}, u32[]{:S(2)}) collective-permute-start(bf16[136,128]{1,0:T(8,128)(2,1)S(1)} %add_convert_fusion.refs_0_), channel_id=1, source_target_pairs={{0,4},{1,5},{2,6},{3,7},{4,0},{5,1},{6,2},{7,3},{8,12},{9,13},{10,... | collective-permute-start | bytes 104456 | tf_op jit(solution)/shard_map/ppermute | solution.py:362
  27.0 1.3 %collective-permute-done.9.refs_3_ = bf16[136,128]{1,0:T(8,128)(2,1)S(1)} collective-permute-done((bf16[136,128]{1,0:T(8,128)(2,1)S(1)}, bf16[136,128]{1,0:T(8,128)(2,1)S(1)}, u32[]{:S(2)}, u32[]{:S(2)}) %collective-permute-start.9) | collective-permute-done | bytes 34848 | tf_op jit(solution)/shard_map/ppermute | solution.py:362
  28.4 2.7 %collective-permute-done.8.refs_2_ = bf16[136,128]{1,0:T(8,128)(2,1)S(1)} collective-permute-done((bf16[136,128]{1,0:T(8,128)(2,1)S(1)}, bf16[136,128]{1,0:T(8,128)(2,1)S(1)}, u32[]{:S(2)}, u32[]{:S(2)}) %collective-permute-start.8) | collective-permute-done | bytes 34848 | tf_op jit(solution)/shard_map/ppermute | solution.py:362
  31.4 0.7 %scales.1 = (f32[128,1536]{1,0:T(8,128)S(1)}, f32[128,1536]{1,0:T(8,128)S(1)}) custom-call(f32[128,1536]{1,0:T(8,128)S(1)} %get-tuple-element.51.forward_ref, f32[128,1536]{1,0:T(8,128)S(1)} %get-tuple-element.52.annuity_ref, s32[12,128]{1,0:T(8,128)S(1)} %get-tuple-element.42.kind_ref, f32[12,128]{1,0:T(8,128)S(1)} %get-tuple-element.43.notional_ref, ...), custom_call_target="tpu_custom_call" | custom-call | flops 400000000 | bytes 4000000 | tf_op jit(solution)/shard_map/scales/pallas_call | solution.py:346
  32.5 1.2 %adjoint.1 = (bf16[512,128]{1,0:T(8,128)(2,1)S(1)}, bf16[128,1536]{1,0:T(8,128)(2,1)S(1)}, bf16[128,1536]{1,0:T(8,128)(2,1)S(1)}) custom-call(bf16[512,128]{1,0:T(8,128)(2,1)S(1)} %collective-permute-done.4.curves.partner, bf16[128,128]{1,0:T(8,128)(2,1)S(1)} %get-tuple-element.50.cots_mine, bf16[128,128]{1,0:T(8,128)(2,1)S(1)} %collective-permute-done.11.cots_partner, ...), custom_call_target="tpu_custom_call" | custom-call | flops 1000000 | bytes 1000000 | tf_op jit(solution)/shard_map/adjoint/pallas_call | solution.py:346
  34.0 1.0 %keep.1.kept = f32[512,128]{1,0:T(8,128)S(1)} custom-call(bf16[512,128]{1,0:T(8,128)(2,1)S(1)} %join.1.curves.mine, bf16[128,1536]{1,0:T(8,128)(2,1)S(1)} %get-tuple-element.55.fwd_cots, bf16[128,1536]{1,0:T(8,128)(2,1)S(1)} %get-tuple-element.56.ann_cots, bf16[1024,1536]{1,0:T(8,128)(2,1)S(1)} %get-tuple-element.37.w_fwd, ...), custom_call_target="tpu_custom_call" | custom-call | flops 200000000 | bytes 4000000 | tf_op jit(solution)/shard_map/keep/pallas_call | solution.py:346
  35.9 2.9 %collective-permute-start.15 = (bf16[128,128]{1,0:T(8,128)(2,1)S(1)}, bf16[128,128]{1,0:T(8,128)(2,1)S(1)}, u32[]{:S(2)}, u32[]{:S(2)}) collective-permute-start(bf16[128,128]{1,0:T(8,128)(2,1)S(1)} %get-tuple-element.61), channel_id=1, source_target_pairs={{0,6},{1,7},{2,4},{3,5},{4,2},{5,3},{6,0},{7,1},{8,14},{9,15},{10,... | collective-permute-start | bytes 98312 | tf_op jit(solution)/shard_map/ppermute | solution.py:362
  38.8 1.5 %collective-permute-start.10 = (f32[16]{0:T(128)S(1)}, f32[16]{0:T(128)S(1)}, u32[]{:S(2)}, u32[]{:S(2)}) collective-permute-start(f32[16]{0:T(128)S(1)} %bitcast.16), channel_id=1, source_target_pairs={{0,16},{16,0},{1,17},{17,1},{2,18},{18,2},{3,19},{19,3},{4,20},{20... | collective-permute-start | bytes 200 | tf_op jit(solution)/shard_map/ppermute | solution.py:377
  40.3 0.7 %collective-permute-done.15.refs_2_ = bf16[128,128]{1,0:T(8,128)(2,1)S(1)} collective-permute-done((bf16[128,128]{1,0:T(8,128)(2,1)S(1)}, bf16[128,128]{1,0:T(8,128)(2,1)S(1)}, u32[]{:S(2)}, u32[]{:S(2)}) %collective-permute-start.15) | collective-permute-done | bytes 32800 | tf_op jit(solution)/shard_map/ppermute | solution.py:362
  41.0 2.1 %collective-permute-start.16 = (bf16[64,128]{1,0:T(8,128)(2,1)S(1)}, bf16[64,128]{1,0:T(8,128)(2,1)S(1)}, u32[]{:S(2)}, u32[]{:S(2)}) collective-permute-start(bf16[64,128]{1,0:T(8,128)(2,1)S(1)} %get-tuple-element.63), channel_id=1, source_target_pairs={{0,8},{1,9},{2,10},{3,11},{4,12},{5,13},{6,14},{7,15},{8,0},{9,1},... | collective-permute-start | bytes 49160 | tf_op jit(solution)/shard_map/ppermute | solution.py:362
  43.6 2.1 %collective-permute-done.16.arrived = bf16[64,128]{1,0:T(8,128)(2,1)S(1)} collective-permute-done((bf16[64,128]{1,0:T(8,128)(2,1)S(1)}, bf16[64,128]{1,0:T(8,128)(2,1)S(1)}, u32[]{:S(2)}, u32[]{:S(2)}) %collective-permute-start.16) | collective-permute-done | bytes 16416 | tf_op jit(solution)/shard_map/ppermute | solution.py:362
  45.7 0.8 %factors.1 = f32[128,128]{1,0:T(8,128)} custom-call(f32[64,128]{1,0:T(8,128)S(1)} %get-tuple-element.62.kept, bf16[64,128]{1,0:T(8,128)(2,1)S(1)} %collective-permute-done.16.arrived, bf16[128,64]{1,0:T(8,128)(2,1)S(1)} %get-tuple-element.35.basis), custom_call_target="tpu_custom_call" | custom-call | flops 1000000 | bytes 1000000 | tf_op jit(solution)/shard_map/factors/pallas_call | solution.py:346
  (26 shorter events, 4.9 us)
Async XLA Ops:
  0.6 6.6 %collective-permute-start = (bf16[128,128]{1,0:T(8,128)(2,1)}, bf16[128,128]{1,0:T(8,128)(2,1)S(1)}, u32[]{:S(2)}, u32[]{:S(2)}) collective-permute-start(bf16[128,128]{1,0:T(8,128)(2,1)} %bitcast.18), channel_id=1, source_target_pairs={{0,8},{1,9},{2,10},{3,11},{4,12},{5,13},{6,14},{7,15},{8,0},{9,1},... | collective-permute-start | bytes 98312 | tf_op jit(solution)/shard_map/ppermute | solution.py:362
  7.4 5.9 %collective-permute-start.3 = (bf16[128,128]{1,0:T(8,128)(2,1)S(1)}, bf16[128,128]{1,0:T(8,128)(2,1)S(1)}, u32[]{:S(2)}, u32[]{:S(2)}) collective-permute-start(bf16[128,128]{1,0:T(8,128)(2,1)S(1)} %curves2.1.refs_8_.refs_0_), channel_id=1, source_target_pairs={{0,6},{1,7},{2,4},{3,5},{4,2},{5,3},{6,0},{7,1},{8,14},{9,15},{10,... | collective-permute-start | bytes 98312 | tf_op jit(solution)/shard_map/ppermute | solution.py:362
  9.9 3.9 %collective-permute-start.2 = (bf16[128,128]{1,0:T(8,128)(2,1)S(1)}, bf16[128,128]{1,0:T(8,128)(2,1)S(1)}, u32[]{:S(2)}, u32[]{:S(2)}) collective-permute-start(bf16[128,128]{1,0:T(8,128)(2,1)S(1)} %curves2.1.refs_8_.refs_0_), channel_id=1, source_target_pairs={{0,4},{1,5},{2,6},{3,7},{4,0},{5,1},{6,2},{7,3},{8,12},{9,13},{10,... | collective-permute-start | bytes 98312 | tf_op jit(solution)/shard_map/ppermute | solution.py:362
  10.6 3.9 %collective-permute-start.1 = (bf16[128,128]{1,0:T(8,128)(2,1)S(1)}, bf16[128,128]{1,0:T(8,128)(2,1)S(1)}, u32[]{:S(2)}, u32[]{:S(2)}) collective-permute-start(bf16[128,128]{1,0:T(8,128)(2,1)S(1)} %curves2.1.refs_8_.refs_0_), channel_id=1, source_target_pairs={{0,2},{1,3},{2,0},{3,1},{4,6},{5,7},{6,4},{7,5},{8,10},{9,11},{10,... | collective-permute-start | bytes 98312 | tf_op jit(solution)/shard_map/ppermute | solution.py:362
  14.5 1.4 %collective-permute-start.4 = (bf16[512,128]{1,0:T(8,128)(2,1)S(1)}, bf16[512,128]{1,0:T(8,128)(2,1)S(1)}, u32[]{:S(2)}, u32[]{:S(2)}) collective-permute-start(bf16[512,128]{1,0:T(8,128)(2,1)S(1)} %join.1.curves.mine), channel_id=1, source_target_pairs={{0,1},{1,0},{2,3},{3,2},{4,5},{5,4},{6,7},{7,6},{8,9},{9,8},{10,11... | collective-permute-start | bytes 393224 | tf_op jit(solution)/shard_map/ppermute | solution.py:362
  17.3 1.3 %collective-permute-start.5 = (bf16[128,128]{1,0:T(8,128)(2,1)S(1)}, bf16[128,128]{1,0:T(8,128)(2,1)S(1)}, u32[]{:S(2)}, u32[]{:S(2)}) collective-permute-start(bf16[128,128]{1,0:T(8,128)(2,1)S(1)} %get-tuple-element.47), channel_id=1, source_target_pairs={{0,1},{1,0},{2,3},{3,2},{4,5},{5,4},{6,7},{7,6},{8,9},{9,8},{10,11... | collective-permute-start | bytes 98312 | tf_op jit(solution)/shard_map/ppermute | solution.py:362
  18.5 4.0 %collective-permute-start.6 = (bf16[136,128]{1,0:T(8,128)(2,1)S(1)}, bf16[136,128]{1,0:T(8,128)(2,1)S(1)}, u32[]{:S(2)}, u32[]{:S(2)}) collective-permute-start(bf16[136,128]{1,0:T(8,128)(2,1)S(1)} %pair.1), channel_id=1, source_target_pairs={{0,2},{1,3},{2,0},{3,1},{4,6},{5,7},{6,4},{7,5},{8,10},{9,11},{10,... | collective-permute-start | bytes 104456 | tf_op jit(solution)/shard_map/ppermute | solution.py:362
  22.6 5.8 %collective-permute-start.9 = (bf16[136,128]{1,0:T(8,128)(2,1)S(1)}, bf16[136,128]{1,0:T(8,128)(2,1)S(1)}, u32[]{:S(2)}, u32[]{:S(2)}) collective-permute-start(bf16[136,128]{1,0:T(8,128)(2,1)S(1)} %add_convert_fusion.refs_0_), channel_id=1, source_target_pairs={{0,12},{1,13},{2,14},{3,15},{4,8},{5,9},{6,10},{7,11},{8,4},{9,5},... | collective-permute-start | bytes 104456 | tf_op jit(solution)/shard_map/ppermute | solution.py:362
  26.2 4.8 %collective-permute-start.8 = (bf16[136,128]{1,0:T(8,128)(2,1)S(1)}, bf16[136,128]{1,0:T(8,128)(2,1)S(1)}, u32[]{:S(2)}, u32[]{:S(2)}) collective-permute-start(bf16[136,128]{1,0:T(8,128)(2,1)S(1)} %add_convert_fusion.refs_0_), channel_id=1, source_target_pairs={{0,8},{1,9},{2,10},{3,11},{4,12},{5,13},{6,14},{7,15},{8,0},{9,1},... | collective-permute-start | bytes 104456 | tf_op jit(solution)/shard_map/ppermute | solution.py:362
  26.2 4.8 %collective-permute-start.7 = (bf16[136,128]{1,0:T(8,128)(2,1)S(1)}, bf16[136,128]{1,0:T(8,128)(2,1)S(1)}, u32[]{:S(2)}, u32[]{:S(2)}) collective-permute-start(bf16[136,128]{1,0:T(8,128)(2,1)S(1)} %add_convert_fusion.refs_0_), channel_id=1, source_target_pairs={{0,4},{1,5},{2,6},{3,7},{4,0},{5,1},{6,2},{7,3},{8,12},{9,13},{10,... | collective-permute-start | bytes 104456 | tf_op jit(solution)/shard_map/ppermute | solution.py:362
  31.3 1.3 %collective-permute-start.11 = (bf16[128,128]{1,0:T(8,128)(2,1)S(1)}, bf16[128,128]{1,0:T(8,128)(2,1)S(1)}, u32[]{:S(2)}, u32[]{:S(2)}) collective-permute-start(bf16[128,128]{1,0:T(8,128)(2,1)S(1)} %get-tuple-element.50.cots_mine), channel_id=1, source_target_pairs={{0,1},{1,0},{2,3},{3,2},{4,5},{5,4},{6,7},{7,6},{8,9},{9,8},{10,11... | collective-permute-start | bytes 98312 | tf_op jit(solution)/shard_map/ppermute | solution.py:362
  33.8 1.4 %collective-permute-start.12 = (bf16[512,128]{1,0:T(8,128)(2,1)S(1)}, bf16[512,128]{1,0:T(8,128)(2,1)S(1)}, u32[]{:S(2)}, u32[]{:S(2)}) collective-permute-start(bf16[512,128]{1,0:T(8,128)(2,1)S(1)} %get-tuple-element.57), channel_id=1, source_target_pairs={{0,1},{1,0},{2,3},{3,2},{4,5},{5,4},{6,7},{7,6},{8,9},{9,8},{10,11... | collective-permute-start | bytes 393224 | tf_op jit(solution)/shard_map/ppermute | solution.py:362
  35.2 5.0 %collective-permute-start.13 = (bf16[128,128]{1,0:T(8,128)(2,1)S(1)}, bf16[128,128]{1,0:T(8,128)(2,1)S(1)}, u32[]{:S(2)}, u32[]{:S(2)}) collective-permute-start(bf16[128,128]{1,0:T(8,128)(2,1)S(1)} %get-tuple-element.59), channel_id=1, source_target_pairs={{0,2},{1,3},{2,0},{3,1},{4,6},{5,7},{6,4},{7,5},{8,10},{9,11},{10,... | collective-permute-start | bytes 98312 | tf_op jit(solution)/shard_map/ppermute | solution.py:362
  35.8 4.4 %collective-permute-start.14 = (bf16[128,128]{1,0:T(8,128)(2,1)S(1)}, bf16[128,128]{1,0:T(8,128)(2,1)S(1)}, u32[]{:S(2)}, u32[]{:S(2)}) collective-permute-start(bf16[128,128]{1,0:T(8,128)(2,1)S(1)} %get-tuple-element.60), channel_id=1, source_target_pairs={{0,4},{1,5},{2,6},{3,7},{4,0},{5,1},{6,2},{7,3},{8,12},{9,13},{10,... | collective-permute-start | bytes 98312 | tf_op jit(solution)/shard_map/ppermute | solution.py:362
  35.9 5.2 %collective-permute-start.15 = (bf16[128,128]{1,0:T(8,128)(2,1)S(1)}, bf16[128,128]{1,0:T(8,128)(2,1)S(1)}, u32[]{:S(2)}, u32[]{:S(2)}) collective-permute-start(bf16[128,128]{1,0:T(8,128)(2,1)S(1)} %get-tuple-element.61), channel_id=1, source_target_pairs={{0,6},{1,7},{2,4},{3,5},{4,2},{5,3},{6,0},{7,1},{8,14},{9,15},{10,... | collective-permute-start | bytes 98312 | tf_op jit(solution)/shard_map/ppermute | solution.py:362
  38.8 4.4 %collective-permute-start.10 = (f32[16]{0:T(128)S(1)}, f32[16]{0:T(128)S(1)}, u32[]{:S(2)}, u32[]{:S(2)}) collective-permute-start(f32[16]{0:T(128)S(1)} %bitcast.16), channel_id=1, source_target_pairs={{0,16},{16,0},{1,17},{17,1},{2,18},{18,2},{3,19},{19,3},{4,20},{20... | collective-permute-start | bytes 200 | tf_op jit(solution)/shard_map/ppermute | solution.py:377
  41.0 4.7 %collective-permute-start.16 = (bf16[64,128]{1,0:T(8,128)(2,1)S(1)}, bf16[64,128]{1,0:T(8,128)(2,1)S(1)}, u32[]{:S(2)}, u32[]{:S(2)}) collective-permute-start(bf16[64,128]{1,0:T(8,128)(2,1)S(1)} %get-tuple-element.63), channel_id=1, source_target_pairs={{0,8},{1,9},{2,10},{3,11},{4,12},{5,13},{6,14},{7,15},{8,0},{9,1},... | collective-permute-start | bytes 49160 | tf_op jit(solution)/shard_map/ppermute | solution.py:362

commit v7 on v6

--- a/solution.py
+++ b/solution.py
@@ -370,6 +370,10 @@
     return [parts[j] for j in range(len(masks))]
 
 
+def ordered(parts, order):
+    return [parts[k] for k in order] if len(parts) == len(order) else parts
+
+
 def sum_over(x, axis):
     n = lax.axis_size(axis)
     total = x
@@ -456,7 +460,7 @@
         sets_kernel, "sets",
         [shape((half_sets, rows), BF16), shape((1, local_sets), F32)],
         [pltpu.VMEM((half_sets, rows), F32)],
-    )(weights, *parts)
+    )(weights, *ordered(parts, (0, 1, 3, 2)))
     cots_partner = swap(cots_mine, 1)
 
     send, fwd_cots, ann_cots = call(
@@ -475,7 +479,7 @@
         shapes += [shape((size, rows), BF16)] * (2 ** len(step) - 1)
         keep, *sends = call(
             functools.partial(fold_kernel, len(arrived)), f"fold{step[0]}", shapes
-        )(keep, *arrived)
+        )(keep, *ordered(arrived, (2, 0, 1)))
         arrived = swaps(sends, step)
     factor_cot = call(factor_kernel, "factors", shape((rows, factor_rows), F32))(
         keep, *arrived, basis

time: 46.8 us -> 46.1 us (0.985)
  waiting for transfers between devices: 15.2 us -> 14.1 us
    ppermute x16, waiting for transfers between devices: 15.1 us -> 14.1 us  [swap(): return lax.ppermute(x, 'trade', [(i, i ^ mask) for i in range(n)])]
where the time goes in v7:
time: 46.1 us; the launch traced here: 45.9 us
  starting transfers between devices  20.8 us (45%)
  waiting for transfers between devices  14.1 us (31%)
  Pallas kernels  9.72 us (21%)
  between operations  0.75 us (2%)
  other arithmetic  0.53 us (1%)
    ppermute x16, starting transfers between devices, swap(): return lax.ppermute(x, 'trade', [(i, i ^ mask) for i in range(n)])  19.3 us
    ppermute x16, waiting for transfers between devices, swap(): return lax.ppermute(x, 'trade', [(i, i ^ mask) for i in range(n)])  14.1 us
    pallas_call x14, Pallas kernels, run(): pl.pallas_call(kernel, in_specs=spaces, out_specs=jax.tree.map(lambda _:...  9.72 us
    ppermute x1, starting transfers between devices, sum_over(): lax.ppermute(x, axis, [(i, (i + shift) % n) for i in range(n)])  1.48 us
  transfers between devices with their start and end apart: 17, of which 12 were waited for; matrix products, arithmetic and copies ran while one was open for 1% of the time, Pallas kernels for 13%

profile of v7, /device:TPU:0, one launch (start us, length us, event | category | flops | bytes accessed | tf_op | source)
XLA Modules:
  0.0 45.9 jit_solution(2624655404399818715)
XLA Ops:
  0.6 4.1 %collective-permute-start = (bf16[128,128]{1,0:T(8,128)(2,1)}, bf16[128,128]{1,0:T(8,128)(2,1)S(1)}, u32[]{:S(2)}, u32[]{:S(2)}) collective-permute-start(bf16[128,128]{1,0:T(8,128)(2,1)} %bitcast.18), channel_id=1, source_target_pairs={{0,8},{1,9},{2,10},{3,11},{4,12},{5,13},{6,14},{7,15},{8,0},{9,1},... | collective-permute-start | bytes 98312 | tf_op jit(solution)/shard_map/ppermute | solution.py:362
  4.8 1.2 %curves.1 = (bf16[64,128]{1,0:T(8,128)(2,1)S(1)}, bf16[128,64]{1,0:T(8,128)(2,1)S(1)}, f32[2,16]{1,0:T(2,128)S(1)}, bf16[8,128]{1,0:T(8,128)(2,1)S(1)}) custom-call(bf16[128,128]{1,0:T(8,128)(2,1)} %bitcast.19, bf16[16,32]{1,0:T(8,128)(2,1)} %bitcast.20, f32[2,16]{1,0:T(2,128)} %bitcast.21), custom_call_target="tpu_custom_call" | custom-call | flops 1000000 | bytes 1000000 | tf_op jit(solution)/shard_map/curves/pallas_call | solution.py:346
  6.0 1.2 %collective-permute-done.arrived = bf16[128,128]{1,0:T(8,128)(2,1)S(1)} collective-permute-done((bf16[128,128]{1,0:T(8,128)(2,1)}, bf16[128,128]{1,0:T(8,128)(2,1)S(1)}, u32[]{:S(2)}, u32[]{:S(2)}) %collective-permute-start) | collective-permute-done | bytes 32800 | tf_op jit(solution)/shard_map/ppermute | solution.py:362
  7.4 2.5 %collective-permute-start.3 = (bf16[128,128]{1,0:T(8,128)(2,1)S(1)}, bf16[128,128]{1,0:T(8,128)(2,1)S(1)}, u32[]{:S(2)}, u32[]{:S(2)}) collective-permute-start(bf16[128,128]{1,0:T(8,128)(2,1)S(1)} %curves2.1.refs_8_.refs_0_), channel_id=1, source_target_pairs={{0,6},{1,7},{2,4},{3,5},{4,2},{5,3},{6,0},{7,1},{8,14},{9,15},{10,... | collective-permute-start | bytes 98312 | tf_op jit(solution)/shard_map/ppermute | solution.py:362
  9.9 0.7 %collective-permute-start.2 = (bf16[128,128]{1,0:T(8,128)(2,1)S(1)}, bf16[128,128]{1,0:T(8,128)(2,1)S(1)}, u32[]{:S(2)}, u32[]{:S(2)}) collective-permute-start(bf16[128,128]{1,0:T(8,128)(2,1)S(1)} %curves2.1.refs_8_.refs_0_), channel_id=1, source_target_pairs={{0,4},{1,5},{2,6},{3,7},{4,0},{5,1},{6,2},{7,3},{8,12},{9,13},{10,... | collective-permute-start | bytes 98312 | tf_op jit(solution)/shard_map/ppermute | solution.py:362
  10.9 2.4 %prep.1 = (bf16[1024,1536]{1,0:T(8,128)(2,1)S(1)}, bf16[1024,1536]{1,0:T(8,128)(2,1)S(1)}, bf16[256,1536]{1,0:T(8,128)(2,1)S(1)}, s32[12,128]{1,0:T(8,128)S(1)},...) custom-call(s32[2,1536]{1,0:T(2,128)} %refs_0_.1, ...), custom_call_target="tpu_custom_call" | custom-call | flops 400000000 | bytes 8000000 | tf_op jit(solution)/shard_map/prep/pallas_call | solution.py:346
  13.8 0.7 %collective-permute-done.1.refs_1_ = bf16[128,128]{1,0:T(8,128)(2,1)S(1)} collective-permute-done((bf16[128,128]{1,0:T(8,128)(2,1)S(1)}, bf16[128,128]{1,0:T(8,128)(2,1)S(1)}, u32[]{:S(2)}, u32[]{:S(2)}) %collective-permute-start.1) | collective-permute-done | bytes 32800 | tf_op jit(solution)/shard_map/ppermute | solution.py:362
  15.2 0.7 %collective-permute-done.4.curves.partner = bf16[512,128]{1,0:T(8,128)(2,1)S(1)} collective-permute-done((bf16[512,128]{1,0:T(8,128)(2,1)S(1)}, bf16[512,128]{1,0:T(8,128)(2,1)S(1)}, u32[]{:S(2)}, u32[]{:S(2)}) %collective-permute-start.4) | collective-permute-done | bytes 131104 | tf_op jit(solution)/shard_map/ppermute | solution.py:362
  15.9 1.3 %price2.1 = (f32[128,128]{1,0:T(8,128)S(1)}, bf16[128,128]{1,0:T(8,128)(2,1)S(1)}, f32[128,1536]{1,0:T(8,128)S(1)}, f32[128,1536]{1,0:T(8,128)S(1)}) custom-call(bf16[512,128]{1,0:T(8,128)(2,1)S(1)} %collective-permute-done.4.curves.partner, f32[128,1536]{1,0:T(8,128)S(1)} %get-tuple-element.39.forward_ref, f32[128,1536]{1,0:T(8,128)S(1)} %get-tuple-element.40.annuity_ref, ...), custom_call_target="tpu_custom_call" | custom-call | flops 1000000 | bytes 1000000 | tf_op jit(solution)/shard_map/price2/pallas_call | solution.py:346
  17.5 1.1 %collective-permute-done.5.arrived = bf16[128,128]{1,0:T(8,128)(2,1)S(1)} collective-permute-done((bf16[128,128]{1,0:T(8,128)(2,1)S(1)}, bf16[128,128]{1,0:T(8,128)(2,1)S(1)}, u32[]{:S(2)}, u32[]{:S(2)}) %collective-permute-start.5) | collective-permute-done | bytes 32800 | tf_op jit(solution)/shard_map/ppermute | solution.py:362
  19.2 3.4 %collective-permute-done.6 = bf16[136,128]{1,0:T(8,128)(2,1)S(1)} collective-permute-done((bf16[136,128]{1,0:T(8,128)(2,1)S(1)}, bf16[136,128]{1,0:T(8,128)(2,1)S(1)}, u32[]{:S(2)}, u32[]{:S(2)}) %collective-permute-start.6) | collective-permute-done | bytes 34848 | tf_op jit(solution)/shard_map/ppermute | solution.py:362
  22.6 2.4 %collective-permute-start.9 = (bf16[136,128]{1,0:T(8,128)(2,1)S(1)}, bf16[136,128]{1,0:T(8,128)(2,1)S(1)}, u32[]{:S(2)}, u32[]{:S(2)}) collective-permute-start(bf16[136,128]{1,0:T(8,128)(2,1)S(1)} %add_convert_fusion.refs_0_), channel_id=1, source_target_pairs={{0,8},{1,9},{2,10},{3,11},{4,12},{5,13},{6,14},{7,15},{8,0},{9,1},... | collective-permute-start | bytes 104456 | tf_op jit(solution)/shard_map/ppermute | solution.py:362
  25.0 1.3 %collective-permute-start.8 = (bf16[136,128]{1,0:T(8,128)(2,1)S(1)}, bf16[136,128]{1,0:T(8,128)(2,1)S(1)}, u32[]{:S(2)}, u32[]{:S(2)}) collective-permute-start(bf16[136,128]{1,0:T(8,128)(2,1)S(1)} %add_convert_fusion.refs_0_), channel_id=1, source_target_pairs={{0,12},{1,13},{2,14},{3,15},{4,8},{5,9},{6,10},{7,11},{8,4},{9,5},... | collective-permute-start | bytes 104456 | tf_op jit(solution)/shard_map/ppermute | solution.py:362
  26.8 0.7 %collective-permute-done.9.refs_3_ = bf16[136,128]{1,0:T(8,128)(2,1)S(1)} collective-permute-done((bf16[136,128]{1,0:T(8,128)(2,1)S(1)}, bf16[136,128]{1,0:T(8,128)(2,1)S(1)}, u32[]{:S(2)}, u32[]{:S(2)}) %collective-permute-start.9) | collective-permute-done | bytes 34848 | tf_op jit(solution)/shard_map/ppermute | solution.py:362
  27.5 3.3 %collective-permute-done.8.refs_2_ = bf16[136,128]{1,0:T(8,128)(2,1)S(1)} collective-permute-done((bf16[136,128]{1,0:T(8,128)(2,1)S(1)}, bf16[136,128]{1,0:T(8,128)(2,1)S(1)}, u32[]{:S(2)}, u32[]{:S(2)}) %collective-permute-start.8) | collective-permute-done | bytes 34848 | tf_op jit(solution)/shard_map/ppermute | solution.py:362
  31.0 0.7 %scales.1 = (f32[128,1536]{1,0:T(8,128)S(1)}, f32[128,1536]{1,0:T(8,128)S(1)}) custom-call(f32[128,1536]{1,0:T(8,128)S(1)} %get-tuple-element.51.forward_ref, f32[128,1536]{1,0:T(8,128)S(1)} %get-tuple-element.52.annuity_ref, s32[12,128]{1,0:T(8,128)S(1)} %get-tuple-element.42.kind_ref, f32[12,128]{1,0:T(8,128)S(1)} %get-tuple-element.43.notional_ref, ...), custom_call_target="tpu_custom_call" | custom-call | flops 400000000 | bytes 4000000 | tf_op jit(solution)/shard_map/scales/pallas_call | solution.py:346
  32.2 1.2 %adjoint.1 = (bf16[512,128]{1,0:T(8,128)(2,1)S(1)}, bf16[128,1536]{1,0:T(8,128)(2,1)S(1)}, bf16[128,1536]{1,0:T(8,128)(2,1)S(1)}) custom-call(bf16[512,128]{1,0:T(8,128)(2,1)S(1)} %collective-permute-done.4.curves.partner, bf16[128,128]{1,0:T(8,128)(2,1)S(1)} %get-tuple-element.50.cots_mine, bf16[128,128]{1,0:T(8,128)(2,1)S(1)} %collective-permute-done.11.cots_partner, ...), custom_call_target="tpu_custom_call" | custom-call | flops 1000000 | bytes 1000000 | tf_op jit(solution)/shard_map/adjoint/pallas_call | solution.py:346
  33.7 1.0 %keep.1.kept = f32[512,128]{1,0:T(8,128)S(1)} custom-call(bf16[512,128]{1,0:T(8,128)(2,1)S(1)} %join.1.curves.mine, bf16[128,1536]{1,0:T(8,128)(2,1)S(1)} %get-tuple-element.55.fwd_cots, bf16[128,1536]{1,0:T(8,128)(2,1)S(1)} %get-tuple-element.56.ann_cots, bf16[1024,1536]{1,0:T(8,128)(2,1)S(1)} %get-tuple-element.37.w_fwd, ...), custom_call_target="tpu_custom_call" | custom-call | flops 200000000 | bytes 4000000 | tf_op jit(solution)/shard_map/keep/pallas_call | solution.py:346
  35.0 1.4 %collective-permute-start.14 = (bf16[128,128]{1,0:T(8,128)(2,1)S(1)}, bf16[128,128]{1,0:T(8,128)(2,1)S(1)}, u32[]{:S(2)}, u32[]{:S(2)}) collective-permute-start(bf16[128,128]{1,0:T(8,128)(2,1)S(1)} %get-tuple-element.60), channel_id=1, source_target_pairs={{0,2},{1,3},{2,0},{3,1},{4,6},{5,7},{6,4},{7,5},{8,10},{9,11},{10,... | collective-permute-start | bytes 98312 | tf_op jit(solution)/shard_map/ppermute | solution.py:362
  36.4 2.0 %collective-permute-start.15 = (bf16[128,128]{1,0:T(8,128)(2,1)S(1)}, bf16[128,128]{1,0:T(8,128)(2,1)S(1)}, u32[]{:S(2)}, u32[]{:S(2)}) collective-permute-start(bf16[128,128]{1,0:T(8,128)(2,1)S(1)} %get-tuple-element.61), channel_id=1, source_target_pairs={{0,4},{1,5},{2,6},{3,7},{4,0},{5,1},{6,2},{7,3},{8,12},{9,13},{10,... | collective-permute-start | bytes 98312 | tf_op jit(solution)/shard_map/ppermute | solution.py:362
  38.4 1.5 %collective-permute-start.10 = (f32[16]{0:T(128)S(1)}, f32[16]{0:T(128)S(1)}, u32[]{:S(2)}, u32[]{:S(2)}) collective-permute-start(f32[16]{0:T(128)S(1)} %bitcast.16), channel_id=1, source_target_pairs={{0,16},{16,0},{1,17},{17,1},{2,18},{18,2},{3,19},{19,3},{4,20},{20... | collective-permute-start | bytes 200 | tf_op jit(solution)/shard_map/ppermute | solution.py:381
  40.4 2.6 %collective-permute-start.16 = (bf16[64,128]{1,0:T(8,128)(2,1)S(1)}, bf16[64,128]{1,0:T(8,128)(2,1)S(1)}, u32[]{:S(2)}, u32[]{:S(2)}) collective-permute-start(bf16[64,128]{1,0:T(8,128)(2,1)S(1)} %get-tuple-element.63), channel_id=1, source_target_pairs={{0,8},{1,9},{2,10},{3,11},{4,12},{5,13},{6,14},{7,15},{8,0},{9,1},... | collective-permute-start | bytes 49160 | tf_op jit(solution)/shard_map/ppermute | solution.py:362
  43.5 1.5 %collective-permute-done.16.arrived = bf16[64,128]{1,0:T(8,128)(2,1)S(1)} collective-permute-done((bf16[64,128]{1,0:T(8,128)(2,1)S(1)}, bf16[64,128]{1,0:T(8,128)(2,1)S(1)}, u32[]{:S(2)}, u32[]{:S(2)}) %collective-permute-start.16) | collective-permute-done | bytes 16416 | tf_op jit(solution)/shard_map/ppermute | solution.py:362
  45.1 0.8 %factors.1 = f32[128,128]{1,0:T(8,128)} custom-call(f32[64,128]{1,0:T(8,128)S(1)} %get-tuple-element.62.kept, bf16[64,128]{1,0:T(8,128)(2,1)S(1)} %collective-permute-done.16.arrived, bf16[128,64]{1,0:T(8,128)(2,1)S(1)} %get-tuple-element.35.basis), custom_call_target="tpu_custom_call" | custom-call | flops 1000000 | bytes 1000000 | tf_op jit(solution)/shard_map/factors/pallas_call | solution.py:346
  (26 shorter events, 5.2 us)
Async XLA Ops:
  0.6 6.6 %collective-permute-start = (bf16[128,128]{1,0:T(8,128)(2,1)}, bf16[128,128]{1,0:T(8,128)(2,1)S(1)}, u32[]{:S(2)}, u32[]{:S(2)}) collective-permute-start(bf16[128,128]{1,0:T(8,128)(2,1)} %bitcast.18), channel_id=1, source_target_pairs={{0,8},{1,9},{2,10},{3,11},{4,12},{5,13},{6,14},{7,15},{8,0},{9,1},... | collective-permute-start | bytes 98312 | tf_op jit(solution)/shard_map/ppermute | solution.py:362
  7.4 5.9 %collective-permute-start.3 = (bf16[128,128]{1,0:T(8,128)(2,1)S(1)}, bf16[128,128]{1,0:T(8,128)(2,1)S(1)}, u32[]{:S(2)}, u32[]{:S(2)}) collective-permute-start(bf16[128,128]{1,0:T(8,128)(2,1)S(1)} %curves2.1.refs_8_.refs_0_), channel_id=1, source_target_pairs={{0,6},{1,7},{2,4},{3,5},{4,2},{5,3},{6,0},{7,1},{8,14},{9,15},{10,... | collective-permute-start | bytes 98312 | tf_op jit(solution)/shard_map/ppermute | solution.py:362
  9.9 3.9 %collective-permute-start.2 = (bf16[128,128]{1,0:T(8,128)(2,1)S(1)}, bf16[128,128]{1,0:T(8,128)(2,1)S(1)}, u32[]{:S(2)}, u32[]{:S(2)}) collective-permute-start(bf16[128,128]{1,0:T(8,128)(2,1)S(1)} %curves2.1.refs_8_.refs_0_), channel_id=1, source_target_pairs={{0,4},{1,5},{2,6},{3,7},{4,0},{5,1},{6,2},{7,3},{8,12},{9,13},{10,... | collective-permute-start | bytes 98312 | tf_op jit(solution)/shard_map/ppermute | solution.py:362
  10.6 3.9 %collective-permute-start.1 = (bf16[128,128]{1,0:T(8,128)(2,1)S(1)}, bf16[128,128]{1,0:T(8,128)(2,1)S(1)}, u32[]{:S(2)}, u32[]{:S(2)}) collective-permute-start(bf16[128,128]{1,0:T(8,128)(2,1)S(1)} %curves2.1.refs_8_.refs_0_), channel_id=1, source_target_pairs={{0,2},{1,3},{2,0},{3,1},{4,6},{5,7},{6,4},{7,5},{8,10},{9,11},{10,... | collective-permute-start | bytes 98312 | tf_op jit(solution)/shard_map/ppermute | solution.py:362
  14.5 1.4 %collective-permute-start.4 = (bf16[512,128]{1,0:T(8,128)(2,1)S(1)}, bf16[512,128]{1,0:T(8,128)(2,1)S(1)}, u32[]{:S(2)}, u32[]{:S(2)}) collective-permute-start(bf16[512,128]{1,0:T(8,128)(2,1)S(1)} %join.1.curves.mine), channel_id=1, source_target_pairs={{0,1},{1,0},{2,3},{3,2},{4,5},{5,4},{6,7},{7,6},{8,9},{9,8},{10,11... | collective-permute-start | bytes 393224 | tf_op jit(solution)/shard_map/ppermute | solution.py:362
  17.3 1.3 %collective-permute-start.5 = (bf16[128,128]{1,0:T(8,128)(2,1)S(1)}, bf16[128,128]{1,0:T(8,128)(2,1)S(1)}, u32[]{:S(2)}, u32[]{:S(2)}) collective-permute-start(bf16[128,128]{1,0:T(8,128)(2,1)S(1)} %get-tuple-element.47), channel_id=1, source_target_pairs={{0,1},{1,0},{2,3},{3,2},{4,5},{5,4},{6,7},{7,6},{8,9},{9,8},{10,11... | collective-permute-start | bytes 98312 | tf_op jit(solution)/shard_map/ppermute | solution.py:362
  18.5 4.0 %collective-permute-start.6 = (bf16[136,128]{1,0:T(8,128)(2,1)S(1)}, bf16[136,128]{1,0:T(8,128)(2,1)S(1)}, u32[]{:S(2)}, u32[]{:S(2)}) collective-permute-start(bf16[136,128]{1,0:T(8,128)(2,1)S(1)} %pair.1), channel_id=1, source_target_pairs={{0,2},{1,3},{2,0},{3,1},{4,6},{5,7},{6,4},{7,5},{8,10},{9,11},{10,... | collective-permute-start | bytes 104456 | tf_op jit(solution)/shard_map/ppermute | solution.py:362
  22.6 4.9 %collective-permute-start.9 = (bf16[136,128]{1,0:T(8,128)(2,1)S(1)}, bf16[136,128]{1,0:T(8,128)(2,1)S(1)}, u32[]{:S(2)}, u32[]{:S(2)}) collective-permute-start(bf16[136,128]{1,0:T(8,128)(2,1)S(1)} %add_convert_fusion.refs_0_), channel_id=1, source_target_pairs={{0,8},{1,9},{2,10},{3,11},{4,12},{5,13},{6,14},{7,15},{8,0},{9,1},... | collective-permute-start | bytes 104456 | tf_op jit(solution)/shard_map/ppermute | solution.py:362
  25.0 5.7 %collective-permute-start.8 = (bf16[136,128]{1,0:T(8,128)(2,1)S(1)}, bf16[136,128]{1,0:T(8,128)(2,1)S(1)}, u32[]{:S(2)}, u32[]{:S(2)}) collective-permute-start(bf16[136,128]{1,0:T(8,128)(2,1)S(1)} %add_convert_fusion.refs_0_), channel_id=1, source_target_pairs={{0,12},{1,13},{2,14},{3,15},{4,8},{5,9},{6,10},{7,11},{8,4},{9,5},... | collective-permute-start | bytes 104456 | tf_op jit(solution)/shard_map/ppermute | solution.py:362
  26.3 4.4 %collective-permute-start.7 = (bf16[136,128]{1,0:T(8,128)(2,1)S(1)}, bf16[136,128]{1,0:T(8,128)(2,1)S(1)}, u32[]{:S(2)}, u32[]{:S(2)}) collective-permute-start(bf16[136,128]{1,0:T(8,128)(2,1)S(1)} %add_convert_fusion.refs_0_), channel_id=1, source_target_pairs={{0,4},{1,5},{2,6},{3,7},{4,0},{5,1},{6,2},{7,3},{8,12},{9,13},{10,... | collective-permute-start | bytes 104456 | tf_op jit(solution)/shard_map/ppermute | solution.py:362
  30.9 1.3 %collective-permute-start.11 = (bf16[128,128]{1,0:T(8,128)(2,1)S(1)}, bf16[128,128]{1,0:T(8,128)(2,1)S(1)}, u32[]{:S(2)}, u32[]{:S(2)}) collective-permute-start(bf16[128,128]{1,0:T(8,128)(2,1)S(1)} %get-tuple-element.50.cots_mine), channel_id=1, source_target_pairs={{0,1},{1,0},{2,3},{3,2},{4,5},{5,4},{6,7},{7,6},{8,9},{9,8},{10,11... | collective-permute-start | bytes 98312 | tf_op jit(solution)/shard_map/ppermute | solution.py:362
  33.4 1.4 %collective-permute-start.12 = (bf16[512,128]{1,0:T(8,128)(2,1)S(1)}, bf16[512,128]{1,0:T(8,128)(2,1)S(1)}, u32[]{:S(2)}, u32[]{:S(2)}) collective-permute-start(bf16[512,128]{1,0:T(8,128)(2,1)S(1)} %get-tuple-element.57), channel_id=1, source_target_pairs={{0,1},{1,0},{2,3},{3,2},{4,5},{5,4},{6,7},{7,6},{8,9},{9,8},{10,11... | collective-permute-start | bytes 393224 | tf_op jit(solution)/shard_map/ppermute | solution.py:362
  34.9 5.0 %collective-permute-start.13 = (bf16[128,128]{1,0:T(8,128)(2,1)S(1)}, bf16[128,128]{1,0:T(8,128)(2,1)S(1)}, u32[]{:S(2)}, u32[]{:S(2)}) collective-permute-start(bf16[128,128]{1,0:T(8,128)(2,1)S(1)} %get-tuple-element.59), channel_id=1, source_target_pairs={{0,6},{1,7},{2,4},{3,5},{4,2},{5,3},{6,0},{7,1},{8,14},{9,15},{10,... | collective-permute-start | bytes 98312 | tf_op jit(solution)/shard_map/ppermute | solution.py:362
  35.0 5.0 %collective-permute-start.14 = (bf16[128,128]{1,0:T(8,128)(2,1)S(1)}, bf16[128,128]{1,0:T(8,128)(2,1)S(1)}, u32[]{:S(2)}, u32[]{:S(2)}) collective-permute-start(bf16[128,128]{1,0:T(8,128)(2,1)S(1)} %get-tuple-element.60), channel_id=1, source_target_pairs={{0,2},{1,3},{2,0},{3,1},{4,6},{5,7},{6,4},{7,5},{8,10},{9,11},{10,... | collective-permute-start | bytes 98312 | tf_op jit(solution)/shard_map/ppermute | solution.py:362
  36.4 3.9 %collective-permute-start.15 = (bf16[128,128]{1,0:T(8,128)(2,1)S(1)}, bf16[128,128]{1,0:T(8,128)(2,1)S(1)}, u32[]{:S(2)}, u32[]{:S(2)}) collective-permute-start(bf16[128,128]{1,0:T(8,128)(2,1)S(1)} %get-tuple-element.61), channel_id=1, source_target_pairs={{0,4},{1,5},{2,6},{3,7},{4,0},{5,1},{6,2},{7,3},{8,12},{9,13},{10,... | collective-permute-start | bytes 98312 | tf_op jit(solution)/shard_map/ppermute | solution.py:362
  38.4 4.6 %collective-permute-start.10 = (f32[16]{0:T(128)S(1)}, f32[16]{0:T(128)S(1)}, u32[]{:S(2)}, u32[]{:S(2)}) collective-permute-start(f32[16]{0:T(128)S(1)} %bitcast.16), channel_id=1, source_target_pairs={{0,16},{16,0},{1,17},{17,1},{2,18},{18,2},{3,19},{19,3},{4,20},{20... | collective-permute-start | bytes 200 | tf_op jit(solution)/shard_map/ppermute | solution.py:381
  40.4 4.7 %collective-permute-start.16 = (bf16[64,128]{1,0:T(8,128)(2,1)S(1)}, bf16[64,128]{1,0:T(8,128)(2,1)S(1)}, u32[]{:S(2)}, u32[]{:S(2)}) collective-permute-start(bf16[64,128]{1,0:T(8,128)(2,1)S(1)} %get-tuple-element.63), channel_id=1, source_target_pairs={{0,8},{1,9},{2,10},{3,11},{4,12},{5,13},{6,14},{7,15},{8,0},{9,1},... | collective-permute-start | bytes 49160 | tf_op jit(solution)/shard_map/ppermute | solution.py:362

commit v8 on v7

--- a/solution.py
+++ b/solution.py
@@ -184,15 +184,15 @@
 
 def price_kernel(
     curves, forward_ref, annuity_ref, w_fwd, w_disc, onehot, kind_ref, notional_ref, strike_ref,
-    vol_ref, threshold_ref, keep, send, forward_out, annuity_out,
+    vol_ref, send, values, forward_out, annuity_out,
 ):
     near, rows = curves.shape
     trades = w_fwd.shape[1]
-    half = keep.shape[0]
+    half = send.shape[0]
     tile = TILE if trades % TILE == 0 else trades
     curve = curves[...]
     discount = jnp.exp(-0.5 * curve.astype(F32)).astype(BF16)
-    total = jnp.zeros((2 * half, rows), F32)
+    total = jnp.zeros((half, rows), F32)
     for t in range(0, trades, tile):
         lanes = slice(t, t + tile)
         forward = forward_ref[:, lanes] + lax.dot_general(
@@ -208,9 +208,14 @@
         moneyness, e = option_terms(forward, param_row(strike_ref, t, tile), vol)
         payoff = jnp.where(option, swaption_payoff(moneyness, e, vol), moneyness)
         value = (param_row(notional_ref, t, tile) * annuity * payoff).astype(BF16)
-        total += lax.dot_general(onehot[:, lanes], value, NT, preferred_element_type=F32)
-    keep[...] = total[:half]
-    send[...] = total[half:].astype(BF16)
+        values[:, lanes] = value
+        total += lax.dot_general(onehot[half:, lanes], value, NT, preferred_element_type=F32)
+    send[...] = total.astype(BF16)
+
+
+def own_sets_kernel(values, onehot, threshold_ref, keep):
+    half = keep.shape[0]
+    keep[...] = lax.dot_general(onehot[:half, :], values[...], NT, preferred_element_type=F32)
     sets = threshold_ref.shape[1]
     chip = lax.axis_index("trade") // 2
     own = pl.ds(pl.multiple_of(chip * sets, sets), sets)
@@ -436,11 +441,14 @@
         half_price_kernel, "price1", [shape((rows, trades), F32)] * 2,
         flops=400_000_000, moved=4_000_000,
     )(mine, w_fwd, w_disc)
-    keep, send, forward, annuity = call(
+    send, values, forward, annuity = call(
         price_kernel, "price2",
-        [shape((half_sets, rows), F32), shape((half_sets, rows), BF16),
+        [shape((half_sets, rows), BF16), shape((rows, trades), BF16),
          shape((rows, trades), F32), shape((rows, trades), F32)],
-    )(partner, forward, annuity, w_fwd, w_disc, onehot, *params)
+    )(partner, forward, annuity, w_fwd, w_disc, onehot, *params[:-1])
+    keep = call(own_sets_kernel, "ownsets", shape((half_sets, rows), F32))(
+        values, onehot, params[-1]
+    )
     fwd_scale, ann_scale = call(
         scale_kernel, "scales", [shape((rows, trades), F32)] * 2,
         flops=400_000_000, moved=4_000_000,

time: 46.1 us -> 46 us (level)
    pallas_call x14 -> x15, Pallas kernels: 9.72 us -> 9.8 us  [run(): pl.pallas_call(kernel, in_specs=spaces, out_specs=jax.tree.map(lambda _:...]
  transfers between devices with their start and end apart: 17 -> 17, of which waited for: 12 -> 12; matrix products, arithmetic and copies ran while one was open for 1% -> 1% of each run, Pallas kernels for 13% -> 14%
where the time goes in v8:
time: 46 us; the launch traced here: 45.7 us
  starting transfers between devices  20.8 us (45%)
  waiting for transfers between devices  13.8 us (30%)
  Pallas kernels  9.8 us (21%)
  between operations  0.75 us (2%)
  other arithmetic  0.53 us (1%)
    ppermute x16, starting transfers between devices, swap(): return lax.ppermute(x, 'trade', [(i, i ^ mask) for i in range(n)])  19.3 us
    ppermute x16, waiting for transfers between devices, swap(): return lax.ppermute(x, 'trade', [(i, i ^ mask) for i in range(n)])  13.8 us
    pallas_call x15, Pallas kernels, run(): pl.pallas_call(kernel, in_specs=spaces, out_specs=jax.tree.map(lambda _:...  9.8 us
    ppermute x1, starting transfers between devices, sum_over(): lax.ppermute(x, axis, [(i, (i + shift) % n) for i in range(n)])  1.5 us
  transfers between devices with their start and end apart: 17, of which 12 were waited for; matrix products, arithmetic and copies ran while one was open for 1% of the time, Pallas kernels for 14%

profile of v8, /device:TPU:0, one launch (start us, length us, event | category | flops | bytes accessed | tf_op | source)
XLA Modules:
  0.0 45.7 jit_solution(8466332069024302349)
XLA Ops:
  0.6 4.1 %collective-permute-start = (bf16[128,128]{1,0:T(8,128)(2,1)}, bf16[128,128]{1,0:T(8,128)(2,1)S(1)}, u32[]{:S(2)}, u32[]{:S(2)}) collective-permute-start(bf16[128,128]{1,0:T(8,128)(2,1)} %bitcast.18), channel_id=1, source_target_pairs={{0,8},{1,9},{2,10},{3,11},{4,12},{5,13},{6,14},{7,15},{8,0},{9,1},... | collective-permute-start | bytes 98312 | tf_op jit(solution)/shard_map/ppermute | solution.py:367
  4.8 1.2 %curves.1 = (bf16[64,128]{1,0:T(8,128)(2,1)S(1)}, bf16[128,64]{1,0:T(8,128)(2,1)S(1)}, f32[2,16]{1,0:T(2,128)S(1)}, bf16[8,128]{1,0:T(8,128)(2,1)S(1)}) custom-call(bf16[128,128]{1,0:T(8,128)(2,1)} %bitcast.19, bf16[16,32]{1,0:T(8,128)(2,1)} %bitcast.20, f32[2,16]{1,0:T(2,128)} %bitcast.21), custom_call_target="tpu_custom_call" | custom-call | flops 1000000 | bytes 1000000 | tf_op jit(solution)/shard_map/curves/pallas_call | solution.py:351
  6.0 1.2 %collective-permute-done.arrived = bf16[128,128]{1,0:T(8,128)(2,1)S(1)} collective-permute-done((bf16[128,128]{1,0:T(8,128)(2,1)}, bf16[128,128]{1,0:T(8,128)(2,1)S(1)}, u32[]{:S(2)}, u32[]{:S(2)}) %collective-permute-start) | collective-permute-done | bytes 32800 | tf_op jit(solution)/shard_map/ppermute | solution.py:367
  7.4 2.5 %collective-permute-start.3 = (bf16[128,128]{1,0:T(8,128)(2,1)S(1)}, bf16[128,128]{1,0:T(8,128)(2,1)S(1)}, u32[]{:S(2)}, u32[]{:S(2)}) collective-permute-start(bf16[128,128]{1,0:T(8,128)(2,1)S(1)} %curves2.1.refs_8_.refs_0_), channel_id=1, source_target_pairs={{0,6},{1,7},{2,4},{3,5},{4,2},{5,3},{6,0},{7,1},{8,14},{9,15},{10,... | collective-permute-start | bytes 98312 | tf_op jit(solution)/shard_map/ppermute | solution.py:367
  9.9 0.7 %collective-permute-start.2 = (bf16[128,128]{1,0:T(8,128)(2,1)S(1)}, bf16[128,128]{1,0:T(8,128)(2,1)S(1)}, u32[]{:S(2)}, u32[]{:S(2)}) collective-permute-start(bf16[128,128]{1,0:T(8,128)(2,1)S(1)} %curves2.1.refs_8_.refs_0_), channel_id=1, source_target_pairs={{0,4},{1,5},{2,6},{3,7},{4,0},{5,1},{6,2},{7,3},{8,12},{9,13},{10,... | collective-permute-start | bytes 98312 | tf_op jit(solution)/shard_map/ppermute | solution.py:367
  10.9 2.4 %prep.1 = (bf16[1024,1536]{1,0:T(8,128)(2,1)S(1)}, bf16[1024,1536]{1,0:T(8,128)(2,1)S(1)}, bf16[256,1536]{1,0:T(8,128)(2,1)S(1)}, s32[12,128]{1,0:T(8,128)S(1)},...) custom-call(s32[2,1536]{1,0:T(2,128)} %refs_0_.1, ...), custom_call_target="tpu_custom_call" | custom-call | flops 400000000 | bytes 8000000 | tf_op jit(solution)/shard_map/prep/pallas_call | solution.py:351
  13.8 0.7 %collective-permute-done.1.refs_1_ = bf16[128,128]{1,0:T(8,128)(2,1)S(1)} collective-permute-done((bf16[128,128]{1,0:T(8,128)(2,1)S(1)}, bf16[128,128]{1,0:T(8,128)(2,1)S(1)}, u32[]{:S(2)}, u32[]{:S(2)}) %collective-permute-start.1) | collective-permute-done | bytes 32800 | tf_op jit(solution)/shard_map/ppermute | solution.py:367
  15.2 0.7 %collective-permute-done.4.curves.partner = bf16[512,128]{1,0:T(8,128)(2,1)S(1)} collective-permute-done((bf16[512,128]{1,0:T(8,128)(2,1)S(1)}, bf16[512,128]{1,0:T(8,128)(2,1)S(1)}, u32[]{:S(2)}, u32[]{:S(2)}) %collective-permute-start.4) | collective-permute-done | bytes 131104 | tf_op jit(solution)/shard_map/ppermute | solution.py:367
  15.9 1.2 %price2.1 = (bf16[128,128]{1,0:T(8,128)(2,1)S(1)}, bf16[128,1536]{1,0:T(8,128)(2,1)S(1)}, f32[128,1536]{1,0:T(8,128)S(1)}, f32[128,1536]{1,0:T(8,128)S(1)}) custom-call(bf16[512,128]{1,0:T(8,128)(2,1)S(1)} %collective-permute-done.4.curves.partner, f32[128,1536]{1,0:T(8,128)S(1)} %get-tuple-element.39.forward_ref, ...), custom_call_target="tpu_custom_call" | custom-call | flops 1000000 | bytes 1000000 | tf_op jit(solution)/shard_map/price2/pallas_call | solution.py:351
  17.6 0.8 %collective-permute-done.5.arrived = bf16[128,128]{1,0:T(8,128)(2,1)S(1)} collective-permute-done((bf16[128,128]{1,0:T(8,128)(2,1)S(1)}, bf16[128,128]{1,0:T(8,128)(2,1)S(1)}, u32[]{:S(2)}, u32[]{:S(2)}) %collective-permute-start.5) | collective-permute-done | bytes 32800 | tf_op jit(solution)/shard_map/ppermute | solution.py:367
  19.0 3.4 %collective-permute-done.6 = bf16[136,128]{1,0:T(8,128)(2,1)S(1)} collective-permute-done((bf16[136,128]{1,0:T(8,128)(2,1)S(1)}, bf16[136,128]{1,0:T(8,128)(2,1)S(1)}, u32[]{:S(2)}, u32[]{:S(2)}) %collective-permute-start.6) | collective-permute-done | bytes 34848 | tf_op jit(solution)/shard_map/ppermute | solution.py:367
  22.4 2.4 %collective-permute-start.9 = (bf16[136,128]{1,0:T(8,128)(2,1)S(1)}, bf16[136,128]{1,0:T(8,128)(2,1)S(1)}, u32[]{:S(2)}, u32[]{:S(2)}) collective-permute-start(bf16[136,128]{1,0:T(8,128)(2,1)S(1)} %add_convert_fusion.refs_0_), channel_id=1, source_target_pairs={{0,8},{1,9},{2,10},{3,11},{4,12},{5,13},{6,14},{7,15},{8,0},{9,1},... | collective-permute-start | bytes 104456 | tf_op jit(solution)/shard_map/ppermute | solution.py:367
  24.8 1.3 %collective-permute-start.8 = (bf16[136,128]{1,0:T(8,128)(2,1)S(1)}, bf16[136,128]{1,0:T(8,128)(2,1)S(1)}, u32[]{:S(2)}, u32[]{:S(2)}) collective-permute-start(bf16[136,128]{1,0:T(8,128)(2,1)S(1)} %add_convert_fusion.refs_0_), channel_id=1, source_target_pairs={{0,12},{1,13},{2,14},{3,15},{4,8},{5,9},{6,10},{7,11},{8,4},{9,5},... | collective-permute-start | bytes 104456 | tf_op jit(solution)/shard_map/ppermute | solution.py:367
  26.6 0.7 %collective-permute-done.9.refs_3_ = bf16[136,128]{1,0:T(8,128)(2,1)S(1)} collective-permute-done((bf16[136,128]{1,0:T(8,128)(2,1)S(1)}, bf16[136,128]{1,0:T(8,128)(2,1)S(1)}, u32[]{:S(2)}, u32[]{:S(2)}) %collective-permute-start.9) | collective-permute-done | bytes 34848 | tf_op jit(solution)/shard_map/ppermute | solution.py:367
  27.3 3.3 %collective-permute-done.8.refs_2_ = bf16[136,128]{1,0:T(8,128)(2,1)S(1)} collective-permute-done((bf16[136,128]{1,0:T(8,128)(2,1)S(1)}, bf16[136,128]{1,0:T(8,128)(2,1)S(1)}, u32[]{:S(2)}, u32[]{:S(2)}) %collective-permute-start.8) | collective-permute-done | bytes 34848 | tf_op jit(solution)/shard_map/ppermute | solution.py:367
  30.9 0.7 %scales.1 = (f32[128,1536]{1,0:T(8,128)S(1)}, f32[128,1536]{1,0:T(8,128)S(1)}) custom-call(f32[128,1536]{1,0:T(8,128)S(1)} %get-tuple-element.51.forward_ref, f32[128,1536]{1,0:T(8,128)S(1)} %get-tuple-element.52.annuity_ref, s32[12,128]{1,0:T(8,128)S(1)} %get-tuple-element.42.kind_ref, f32[12,128]{1,0:T(8,128)S(1)} %get-tuple-element.43.notional_ref, ...), custom_call_target="tpu_custom_call" | custom-call | flops 400000000 | bytes 4000000 | tf_op jit(solution)/shard_map/scales/pallas_call | solution.py:351
  32.1 1.2 %adjoint.1 = (bf16[512,128]{1,0:T(8,128)(2,1)S(1)}, bf16[128,1536]{1,0:T(8,128)(2,1)S(1)}, bf16[128,1536]{1,0:T(8,128)(2,1)S(1)}) custom-call(bf16[512,128]{1,0:T(8,128)(2,1)S(1)} %collective-permute-done.4.curves.partner, bf16[128,128]{1,0:T(8,128)(2,1)S(1)} %get-tuple-element.50.cots_mine, bf16[128,128]{1,0:T(8,128)(2,1)S(1)} %collective-permute-done.11.cots_partner, ...), custom_call_target="tpu_custom_call" | custom-call | flops 1000000 | bytes 1000000 | tf_op jit(solution)/shard_map/adjoint/pallas_call | solution.py:351
  33.5 1.0 %keep.1.kept = f32[512,128]{1,0:T(8,128)S(1)} custom-call(bf16[512,128]{1,0:T(8,128)(2,1)S(1)} %join.1.curves.mine, bf16[128,1536]{1,0:T(8,128)(2,1)S(1)} %get-tuple-element.55.fwd_cots, bf16[128,1536]{1,0:T(8,128)(2,1)S(1)} %get-tuple-element.56.ann_cots, bf16[1024,1536]{1,0:T(8,128)(2,1)S(1)} %get-tuple-element.37.w_fwd, ...), custom_call_target="tpu_custom_call" | custom-call | flops 200000000 | bytes 4000000 | tf_op jit(solution)/shard_map/keep/pallas_call | solution.py:351
  34.8 1.4 %collective-permute-start.14 = (bf16[128,128]{1,0:T(8,128)(2,1)S(1)}, bf16[128,128]{1,0:T(8,128)(2,1)S(1)}, u32[]{:S(2)}, u32[]{:S(2)}) collective-permute-start(bf16[128,128]{1,0:T(8,128)(2,1)S(1)} %get-tuple-element.60), channel_id=1, source_target_pairs={{0,2},{1,3},{2,0},{3,1},{4,6},{5,7},{6,4},{7,5},{8,10},{9,11},{10,... | collective-permute-start | bytes 98312 | tf_op jit(solution)/shard_map/ppermute | solution.py:367
  36.2 2.0 %collective-permute-start.15 = (bf16[128,128]{1,0:T(8,128)(2,1)S(1)}, bf16[128,128]{1,0:T(8,128)(2,1)S(1)}, u32[]{:S(2)}, u32[]{:S(2)}) collective-permute-start(bf16[128,128]{1,0:T(8,128)(2,1)S(1)} %get-tuple-element.61), channel_id=1, source_target_pairs={{0,4},{1,5},{2,6},{3,7},{4,0},{5,1},{6,2},{7,3},{8,12},{9,13},{10,... | collective-permute-start | bytes 98312 | tf_op jit(solution)/shard_map/ppermute | solution.py:367
  38.3 1.5 %collective-permute-start.10 = (f32[16]{0:T(128)S(1)}, f32[16]{0:T(128)S(1)}, u32[]{:S(2)}, u32[]{:S(2)}) collective-permute-start(f32[16]{0:T(128)S(1)} %bitcast.16), channel_id=1, source_target_pairs={{0,16},{16,0},{1,17},{17,1},{2,18},{18,2},{3,19},{19,3},{4,20},{20... | collective-permute-start | bytes 200 | tf_op jit(solution)/shard_map/ppermute | solution.py:386
  40.2 2.6 %collective-permute-start.16 = (bf16[64,128]{1,0:T(8,128)(2,1)S(1)}, bf16[64,128]{1,0:T(8,128)(2,1)S(1)}, u32[]{:S(2)}, u32[]{:S(2)}) collective-permute-start(bf16[64,128]{1,0:T(8,128)(2,1)S(1)} %get-tuple-element.63), channel_id=1, source_target_pairs={{0,8},{1,9},{2,10},{3,11},{4,12},{5,13},{6,14},{7,15},{8,0},{9,1},... | collective-permute-start | bytes 49160 | tf_op jit(solution)/shard_map/ppermute | solution.py:367
  43.4 1.5 %collective-permute-done.16.arrived = bf16[64,128]{1,0:T(8,128)(2,1)S(1)} collective-permute-done((bf16[64,128]{1,0:T(8,128)(2,1)S(1)}, bf16[64,128]{1,0:T(8,128)(2,1)S(1)}, u32[]{:S(2)}, u32[]{:S(2)}) %collective-permute-start.16) | collective-permute-done | bytes 16416 | tf_op jit(solution)/shard_map/ppermute | solution.py:367
  44.9 0.8 %factors.1 = f32[128,128]{1,0:T(8,128)} custom-call(f32[64,128]{1,0:T(8,128)S(1)} %get-tuple-element.62.kept, bf16[64,128]{1,0:T(8,128)(2,1)S(1)} %collective-permute-done.16.arrived, bf16[128,64]{1,0:T(8,128)(2,1)S(1)} %get-tuple-element.35.basis), custom_call_target="tpu_custom_call" | custom-call | flops 1000000 | bytes 1000000 | tf_op jit(solution)/shard_map/factors/pallas_call | solution.py:351
  (27 shorter events, 5.5 us)
Async XLA Ops:
  0.6 6.6 %collective-permute-start = (bf16[128,128]{1,0:T(8,128)(2,1)}, bf16[128,128]{1,0:T(8,128)(2,1)S(1)}, u32[]{:S(2)}, u32[]{:S(2)}) collective-permute-start(bf16[128,128]{1,0:T(8,128)(2,1)} %bitcast.18), channel_id=1, source_target_pairs={{0,8},{1,9},{2,10},{3,11},{4,12},{5,13},{6,14},{7,15},{8,0},{9,1},... | collective-permute-start | bytes 98312 | tf_op jit(solution)/shard_map/ppermute | solution.py:367
  7.4 5.9 %collective-permute-start.3 = (bf16[128,128]{1,0:T(8,128)(2,1)S(1)}, bf16[128,128]{1,0:T(8,128)(2,1)S(1)}, u32[]{:S(2)}, u32[]{:S(2)}) collective-permute-start(bf16[128,128]{1,0:T(8,128)(2,1)S(1)} %curves2.1.refs_8_.refs_0_), channel_id=1, source_target_pairs={{0,6},{1,7},{2,4},{3,5},{4,2},{5,3},{6,0},{7,1},{8,14},{9,15},{10,... | collective-permute-start | bytes 98312 | tf_op jit(solution)/shard_map/ppermute | solution.py:367
  9.9 3.9 %collective-permute-start.2 = (bf16[128,128]{1,0:T(8,128)(2,1)S(1)}, bf16[128,128]{1,0:T(8,128)(2,1)S(1)}, u32[]{:S(2)}, u32[]{:S(2)}) collective-permute-start(bf16[128,128]{1,0:T(8,128)(2,1)S(1)} %curves2.1.refs_8_.refs_0_), channel_id=1, source_target_pairs={{0,4},{1,5},{2,6},{3,7},{4,0},{5,1},{6,2},{7,3},{8,12},{9,13},{10,... | collective-permute-start | bytes 98312 | tf_op jit(solution)/shard_map/ppermute | solution.py:367
  10.6 3.9 %collective-permute-start.1 = (bf16[128,128]{1,0:T(8,128)(2,1)S(1)}, bf16[128,128]{1,0:T(8,128)(2,1)S(1)}, u32[]{:S(2)}, u32[]{:S(2)}) collective-permute-start(bf16[128,128]{1,0:T(8,128)(2,1)S(1)} %curves2.1.refs_8_.refs_0_), channel_id=1, source_target_pairs={{0,2},{1,3},{2,0},{3,1},{4,6},{5,7},{6,4},{7,5},{8,10},{9,11},{10,... | collective-permute-start | bytes 98312 | tf_op jit(solution)/shard_map/ppermute | solution.py:367
  14.5 1.4 %collective-permute-start.4 = (bf16[512,128]{1,0:T(8,128)(2,1)S(1)}, bf16[512,128]{1,0:T(8,128)(2,1)S(1)}, u32[]{:S(2)}, u32[]{:S(2)}) collective-permute-start(bf16[512,128]{1,0:T(8,128)(2,1)S(1)} %join.1.curves.mine), channel_id=1, source_target_pairs={{0,1},{1,0},{2,3},{3,2},{4,5},{5,4},{6,7},{7,6},{8,9},{9,8},{10,11... | collective-permute-start | bytes 393224 | tf_op jit(solution)/shard_map/ppermute | solution.py:367
  17.1 1.3 %collective-permute-start.5 = (bf16[128,128]{1,0:T(8,128)(2,1)S(1)}, bf16[128,128]{1,0:T(8,128)(2,1)S(1)}, u32[]{:S(2)}, u32[]{:S(2)}) collective-permute-start(bf16[128,128]{1,0:T(8,128)(2,1)S(1)} %get-tuple-element.47), channel_id=1, source_target_pairs={{0,1},{1,0},{2,3},{3,2},{4,5},{5,4},{6,7},{7,6},{8,9},{9,8},{10,11... | collective-permute-start | bytes 98312 | tf_op jit(solution)/shard_map/ppermute | solution.py:367
  18.4 4.0 %collective-permute-start.6 = (bf16[136,128]{1,0:T(8,128)(2,1)S(1)}, bf16[136,128]{1,0:T(8,128)(2,1)S(1)}, u32[]{:S(2)}, u32[]{:S(2)}) collective-permute-start(bf16[136,128]{1,0:T(8,128)(2,1)S(1)} %pair.1), channel_id=1, source_target_pairs={{0,2},{1,3},{2,0},{3,1},{4,6},{5,7},{6,4},{7,5},{8,10},{9,11},{10,... | collective-permute-start | bytes 104456 | tf_op jit(solution)/shard_map/ppermute | solution.py:367
  22.4 4.9 %collective-permute-start.9 = (bf16[136,128]{1,0:T(8,128)(2,1)S(1)}, bf16[136,128]{1,0:T(8,128)(2,1)S(1)}, u32[]{:S(2)}, u32[]{:S(2)}) collective-permute-start(bf16[136,128]{1,0:T(8,128)(2,1)S(1)} %add_convert_fusion.refs_0_), channel_id=1, source_target_pairs={{0,8},{1,9},{2,10},{3,11},{4,12},{5,13},{6,14},{7,15},{8,0},{9,1},... | collective-permute-start | bytes 104456 | tf_op jit(solution)/shard_map/ppermute | solution.py:367
  24.8 5.7 %collective-permute-start.8 = (bf16[136,128]{1,0:T(8,128)(2,1)S(1)}, bf16[136,128]{1,0:T(8,128)(2,1)S(1)}, u32[]{:S(2)}, u32[]{:S(2)}) collective-permute-start(bf16[136,128]{1,0:T(8,128)(2,1)S(1)} %add_convert_fusion.refs_0_), channel_id=1, source_target_pairs={{0,12},{1,13},{2,14},{3,15},{4,8},{5,9},{6,10},{7,11},{8,4},{9,5},... | collective-permute-start | bytes 104456 | tf_op jit(solution)/shard_map/ppermute | solution.py:367
  26.2 4.4 %collective-permute-start.7 = (bf16[136,128]{1,0:T(8,128)(2,1)S(1)}, bf16[136,128]{1,0:T(8,128)(2,1)S(1)}, u32[]{:S(2)}, u32[]{:S(2)}) collective-permute-start(bf16[136,128]{1,0:T(8,128)(2,1)S(1)} %add_convert_fusion.refs_0_), channel_id=1, source_target_pairs={{0,4},{1,5},{2,6},{3,7},{4,0},{5,1},{6,2},{7,3},{8,12},{9,13},{10,... | collective-permute-start | bytes 104456 | tf_op jit(solution)/shard_map/ppermute | solution.py:367
  30.8 1.3 %collective-permute-start.11 = (bf16[128,128]{1,0:T(8,128)(2,1)S(1)}, bf16[128,128]{1,0:T(8,128)(2,1)S(1)}, u32[]{:S(2)}, u32[]{:S(2)}) collective-permute-start(bf16[128,128]{1,0:T(8,128)(2,1)S(1)} %get-tuple-element.50.cots_mine), channel_id=1, source_target_pairs={{0,1},{1,0},{2,3},{3,2},{4,5},{5,4},{6,7},{7,6},{8,9},{9,8},{10,11... | collective-permute-start | bytes 98312 | tf_op jit(solution)/shard_map/ppermute | solution.py:367
  33.3 1.4 %collective-permute-start.12 = (bf16[512,128]{1,0:T(8,128)(2,1)S(1)}, bf16[512,128]{1,0:T(8,128)(2,1)S(1)}, u32[]{:S(2)}, u32[]{:S(2)}) collective-permute-start(bf16[512,128]{1,0:T(8,128)(2,1)S(1)} %get-tuple-element.57), channel_id=1, source_target_pairs={{0,1},{1,0},{2,3},{3,2},{4,5},{5,4},{6,7},{7,6},{8,9},{9,8},{10,11... | collective-permute-start | bytes 393224 | tf_op jit(solution)/shard_map/ppermute | solution.py:367
  34.7 5.1 %collective-permute-start.13 = (bf16[128,128]{1,0:T(8,128)(2,1)S(1)}, bf16[128,128]{1,0:T(8,128)(2,1)S(1)}, u32[]{:S(2)}, u32[]{:S(2)}) collective-permute-start(bf16[128,128]{1,0:T(8,128)(2,1)S(1)} %get-tuple-element.59), channel_id=1, source_target_pairs={{0,6},{1,7},{2,4},{3,5},{4,2},{5,3},{6,0},{7,1},{8,14},{9,15},{10,... | collective-permute-start | bytes 98312 | tf_op jit(solution)/shard_map/ppermute | solution.py:367
  34.8 5.0 %collective-permute-start.14 = (bf16[128,128]{1,0:T(8,128)(2,1)S(1)}, bf16[128,128]{1,0:T(8,128)(2,1)S(1)}, u32[]{:S(2)}, u32[]{:S(2)}) collective-permute-start(bf16[128,128]{1,0:T(8,128)(2,1)S(1)} %get-tuple-element.60), channel_id=1, source_target_pairs={{0,2},{1,3},{2,0},{3,1},{4,6},{5,7},{6,4},{7,5},{8,10},{9,11},{10,... | collective-permute-start | bytes 98312 | tf_op jit(solution)/shard_map/ppermute | solution.py:367
  36.2 3.9 %collective-permute-start.15 = (bf16[128,128]{1,0:T(8,128)(2,1)S(1)}, bf16[128,128]{1,0:T(8,128)(2,1)S(1)}, u32[]{:S(2)}, u32[]{:S(2)}) collective-permute-start(bf16[128,128]{1,0:T(8,128)(2,1)S(1)} %get-tuple-element.61), channel_id=1, source_target_pairs={{0,4},{1,5},{2,6},{3,7},{4,0},{5,1},{6,2},{7,3},{8,12},{9,13},{10,... | collective-permute-start | bytes 98312 | tf_op jit(solution)/shard_map/ppermute | solution.py:367
  38.3 4.6 %collective-permute-start.10 = (f32[16]{0:T(128)S(1)}, f32[16]{0:T(128)S(1)}, u32[]{:S(2)}, u32[]{:S(2)}) collective-permute-start(f32[16]{0:T(128)S(1)} %bitcast.16), channel_id=1, source_target_pairs={{0,16},{16,0},{1,17},{17,1},{2,18},{18,2},{3,19},{19,3},{4,20},{20... | collective-permute-start | bytes 200 | tf_op jit(solution)/shard_map/ppermute | solution.py:386
  40.2 4.7 %collective-permute-start.16 = (bf16[64,128]{1,0:T(8,128)(2,1)S(1)}, bf16[64,128]{1,0:T(8,128)(2,1)S(1)}, u32[]{:S(2)}, u32[]{:S(2)}) collective-permute-start(bf16[64,128]{1,0:T(8,128)(2,1)S(1)} %get-tuple-element.63), channel_id=1, source_target_pairs={{0,8},{1,9},{2,10},{3,11},{4,12},{5,13},{6,14},{7,15},{8,0},{9,1},... | collective-permute-start | bytes 49160 | tf_op jit(solution)/shard_map/ppermute | solution.py:367

commit v9 on v8

--- a/solution.py
+++ b/solution.py
@@ -127,8 +127,8 @@
 
 def prep_kernel(devices, *refs):
     sources, rest = refs[:8], refs[9:]
-    w_fwd, w_disc, onehot = rest[:3]
-    params, (blocks_ref, set_ref, weights_ref, sems) = rest[3:8], rest[8:]
+    w_fwd, w_low, w_disc, onehot = rest[:4]
+    params, (blocks_ref, set_ref, weights_ref, sems) = rest[4:9], rest[9:]
     fetch(list(zip(sources, (blocks_ref, set_ref, weights_ref) + tuple(params))), sems)
     tenors, trades = weights_ref.shape
     height = w_fwd.shape[0]
@@ -141,12 +141,15 @@
     for t in range(0, trades, LANES):
         lanes = slice(t, t + LANES)
         weights = weights_ref[:, lanes]
+        low = weights - weights.astype(BF16).astype(F32)
         for k, out in enumerate((w_fwd, w_disc)):
             ids = jnp.broadcast_to(block_rows[k : k + 1, lanes], (tenors, LANES))
             for b in range(blocks):
-                out[b * tenors : (b + 1) * tenors, lanes] = jnp.where(
-                    ids == b, weights, zero
-                ).astype(BF16)
+                here = ids == b
+                band = slice(b * tenors, (b + 1) * tenors)
+                out[band, lanes] = jnp.where(here, weights, zero).astype(BF16)
+                if k == 0:
+                    w_low[band, lanes] = jnp.where(here, low, zero).astype(BF16)
         ids = jnp.broadcast_to(set_rows[t // LANES : t // LANES + 1, :], (16, LANES))
         for n in range(0, sets, 16):
             onehot[n : n + 16, lanes] = jnp.where(ids == row + n, 1.0, 0.0).astype(BF16)
@@ -158,7 +161,7 @@
     )
 
 
-def half_price_kernel(curves, w_fwd, w_disc, forward, annuity):
+def half_price_kernel(curves, w_fwd, w_low, w_disc, forward, annuity):
     half, trades = curves.shape[0], w_fwd.shape[1]
     tile = TILE if trades % TILE == 0 else trades
     curve = curves[...]
@@ -167,7 +170,7 @@
         lanes = slice(t, t + tile)
         forward[:, lanes] = lax.dot_general(
             curve, w_fwd[:half, lanes], TN, preferred_element_type=F32
-        )
+        ) + lax.dot_general(curve, w_low[:half, lanes], TN, preferred_element_type=F32)
         annuity[:, lanes] = lax.dot_general(
             discount, w_disc[:half, lanes], TN, preferred_element_type=F32
         )
@@ -183,7 +186,7 @@
 
 
 def price_kernel(
-    curves, forward_ref, annuity_ref, w_fwd, w_disc, onehot, kind_ref, notional_ref, strike_ref,
+    curves, forward_ref, annuity_ref, w_fwd, w_low, w_disc, onehot, kind_ref, notional_ref, strike_ref,
     vol_ref, send, values, forward_out, annuity_out,
 ):
     near, rows = curves.shape
@@ -197,7 +200,7 @@
         lanes = slice(t, t + tile)
         forward = forward_ref[:, lanes] + lax.dot_general(
             curve, w_fwd[near:, lanes], TN, preferred_element_type=F32
-        )
+        ) + lax.dot_general(curve, w_low[near:, lanes], TN, preferred_element_type=F32)
         annuity = annuity_ref[:, lanes] + lax.dot_general(
             discount, w_disc[near:, lanes], TN, preferred_element_type=F32
         )
@@ -422,9 +425,9 @@
     for mask in single[1:]:
         curves = jnp.concatenate([curves, swap(curves, mask)], axis=0)
     near = [curves] + swaps(curves, group)
-    w_fwd, w_disc, onehot, *params = call(
+    w_fwd, w_low, w_disc, onehot, *params = call(
         functools.partial(prep_kernel, devices), "prep",
-        [shape((all_rows, trades), BF16)] * 2 + [shape((2 * half_sets, trades), BF16)]
+        [shape((all_rows, trades), BF16)] * 3 + [shape((2 * half_sets, trades), BF16)]
         + [shape(lane_rows, jnp.int32)] + [shape(lane_rows, F32)] * 3 + [shape((1, local_sets), F32)],
         [pltpu.VMEM((2, trades), jnp.int32), pltpu.VMEM(lane_rows, jnp.int32),
          pltpu.VMEM((tenors, trades), F32), dma((8,))],
@@ -440,12 +443,12 @@
     forward, annuity = call(
         half_price_kernel, "price1", [shape((rows, trades), F32)] * 2,
         flops=400_000_000, moved=4_000_000,
-    )(mine, w_fwd, w_disc)
+    )(mine, w_fwd, w_low, w_disc)
     send, values, forward, annuity = call(
         price_kernel, "price2",
         [shape((half_sets, rows), BF16), shape((rows, trades), BF16),
          shape((rows, trades), F32), shape((rows, trades), F32)],
-    )(partner, forward, annuity, w_fwd, w_disc, onehot, *params[:-1])
+    )(partner, forward, annuity, w_fwd, w_low, w_disc, onehot, *params[:-1])
     keep = call(own_sets_kernel, "ownsets", shape((half_sets, rows), F32))(
         values, onehot, params[-1]
     )

time: 46 us -> 46.1 us (level)
  waiting for transfers between devices: 13.8 us -> 12.8 us
  Pallas kernels: 9.8 us -> 10.6 us
    ppermute x16, waiting for transfers between devices: 13.8 us -> 12.8 us  [swap(): return lax.ppermute(x, 'trade', [(i, i ^ mask) for i in range(n)])]
    pallas_call x15, Pallas kernels: 9.8 us -> 10.6 us  [run(): pl.pallas_call(kernel, in_specs=spaces, out_specs=jax.tree.map(lambda _:...]
  transfers between devices with their start and end apart: 17 -> 17, of which waited for: 12 -> 13; matrix products, arithmetic and copies ran while one was open for 1% -> 1% of each run, Pallas kernels for 14% -> 15%
where the time goes in v9:
time: 46.1 us; the launch traced here: 45.9 us
  starting transfers between devices  21.2 us (46%)
  waiting for transfers between devices  12.8 us (28%)
  Pallas kernels  10.6 us (23%)
  between operations  0.75 us (2%)
  other arithmetic  0.53 us (1%)
    ppermute x16, starting transfers between devices, swap(): return lax.ppermute(x, 'trade', [(i, i ^ mask) for i in range(n)])  19.7 us
    ppermute x16, waiting for transfers between devices, swap(): return lax.ppermute(x, 'trade', [(i, i ^ mask) for i in range(n)])  12.8 us
    pallas_call x15, Pallas kernels, run(): pl.pallas_call(kernel, in_specs=spaces, out_specs=jax.tree.map(lambda _:...  10.6 us
    ppermute x1, starting transfers between devices, sum_over(): lax.ppermute(x, axis, [(i, (i + shift) % n) for i in range(n)])  1.5 us
  transfers between devices with their start and end apart: 17, of which 13 were waited for; matrix products, arithmetic and copies ran while one was open for 1% of the time, Pallas kernels for 15%

profile of v9, /device:TPU:0, one launch (start us, length us, event | category | flops | bytes accessed | tf_op | source)
XLA Modules:
  0.0 45.9 jit_solution(9014442669220400095)
XLA Ops:
  0.6 4.1 %collective-permute-start = (bf16[128,128]{1,0:T(8,128)(2,1)}, bf16[128,128]{1,0:T(8,128)(2,1)S(1)}, u32[]{:S(2)}, u32[]{:S(2)}) collective-permute-start(bf16[128,128]{1,0:T(8,128)(2,1)} %bitcast.18), channel_id=1, source_target_pairs={{0,8},{1,9},{2,10},{3,11},{4,12},{5,13},{6,14},{7,15},{8,0},{9,1},... | collective-permute-start | bytes 98312 | tf_op jit(solution)/shard_map/ppermute | solution.py:370
  4.8 1.2 %curves.1 = (bf16[64,128]{1,0:T(8,128)(2,1)S(1)}, bf16[128,64]{1,0:T(8,128)(2,1)S(1)}, f32[2,16]{1,0:T(2,128)S(1)}, bf16[8,128]{1,0:T(8,128)(2,1)S(1)}) custom-call(bf16[128,128]{1,0:T(8,128)(2,1)} %bitcast.19, bf16[16,32]{1,0:T(8,128)(2,1)} %bitcast.20, f32[2,16]{1,0:T(2,128)} %bitcast.21), custom_call_target="tpu_custom_call" | custom-call | flops 1000000 | bytes 1000000 | tf_op jit(solution)/shard_map/curves/pallas_call | solution.py:354
  6.0 1.2 %collective-permute-done.arrived = bf16[128,128]{1,0:T(8,128)(2,1)S(1)} collective-permute-done((bf16[128,128]{1,0:T(8,128)(2,1)}, bf16[128,128]{1,0:T(8,128)(2,1)S(1)}, u32[]{:S(2)}, u32[]{:S(2)}) %collective-permute-start) | collective-permute-done | bytes 32800 | tf_op jit(solution)/shard_map/ppermute | solution.py:370
  7.4 2.5 %collective-permute-start.3 = (bf16[128,128]{1,0:T(8,128)(2,1)S(1)}, bf16[128,128]{1,0:T(8,128)(2,1)S(1)}, u32[]{:S(2)}, u32[]{:S(2)}) collective-permute-start(bf16[128,128]{1,0:T(8,128)(2,1)S(1)} %curves2.1.refs_8_.refs_0_), channel_id=1, source_target_pairs={{0,6},{1,7},{2,4},{3,5},{4,2},{5,3},{6,0},{7,1},{8,14},{9,15},{10,... | collective-permute-start | bytes 98312 | tf_op jit(solution)/shard_map/ppermute | solution.py:370
  9.9 0.7 %collective-permute-start.2 = (bf16[128,128]{1,0:T(8,128)(2,1)S(1)}, bf16[128,128]{1,0:T(8,128)(2,1)S(1)}, u32[]{:S(2)}, u32[]{:S(2)}) collective-permute-start(bf16[128,128]{1,0:T(8,128)(2,1)S(1)} %curves2.1.refs_8_.refs_0_), channel_id=1, source_target_pairs={{0,4},{1,5},{2,6},{3,7},{4,0},{5,1},{6,2},{7,3},{8,12},{9,13},{10,... | collective-permute-start | bytes 98312 | tf_op jit(solution)/shard_map/ppermute | solution.py:370
  10.9 2.8 %prep.1 = (bf16[1024,1536]{1,0:T(8,128)(2,1)S(1)}, bf16[1024,1536]{1,0:T(8,128)(2,1)S(1)}, bf16[1024,1536]{1,0:T(8,128)(2,1)S(1)}, bf16[256,1536]{1,0:T(8,128)(2...) custom-call(s32[2,1536]{1,0:T(2,128)} %refs_0_.1, ...), custom_call_target="tpu_custom_call" | custom-call | flops 400000000 | bytes 8000000 | tf_op jit(solution)/shard_map/prep/pallas_call | solution.py:354
  13.8 0.7 %collective-permute-done.1.refs_1_ = bf16[128,128]{1,0:T(8,128)(2,1)S(1)} collective-permute-done((bf16[128,128]{1,0:T(8,128)(2,1)S(1)}, bf16[128,128]{1,0:T(8,128)(2,1)S(1)}, u32[]{:S(2)}, u32[]{:S(2)}) %collective-permute-start.1) | collective-permute-done | bytes 32800 | tf_op jit(solution)/shard_map/ppermute | solution.py:370
  14.6 0.8 %price1.1 = (f32[128,1536]{1,0:T(8,128)S(1)}, f32[128,1536]{1,0:T(8,128)S(1)}) custom-call(bf16[512,128]{1,0:T(8,128)(2,1)S(1)} %join.1.curves.mine, bf16[1024,1536]{1,0:T(8,128)(2,1)S(1)} %get-tuple-element.38.w_fwd, bf16[1024,1536]{1,0:T(8,128)(2,1)S(1)} %get-tuple-element.39.w_low, bf16[1024,1536]{1,0:T(8,128)(2,1)S(1)} %get-tuple-element.40.w_disc), custom_call_target="tpu_custom_call" | custom-call | flops 400000000 | bytes 4000000 | tf_op jit(solution)/shard_map/price1/pallas_call | solution.py:354
  15.9 1.3 %price2.1 = (bf16[128,128]{1,0:T(8,128)(2,1)S(1)}, bf16[128,1536]{1,0:T(8,128)(2,1)S(1)}, f32[128,1536]{1,0:T(8,128)S(1)}, f32[128,1536]{1,0:T(8,128)S(1)}) custom-call(bf16[512,128]{1,0:T(8,128)(2,1)S(1)} %collective-permute-done.4.curves.partner, f32[128,1536]{1,0:T(8,128)S(1)} %get-tuple-element.41.forward_ref, ...), custom_call_target="tpu_custom_call" | custom-call | flops 1000000 | bytes 1000000 | tf_op jit(solution)/shard_map/price2/pallas_call | solution.py:354
  17.7 0.8 %collective-permute-done.5.arrived = bf16[128,128]{1,0:T(8,128)(2,1)S(1)} collective-permute-done((bf16[128,128]{1,0:T(8,128)(2,1)S(1)}, bf16[128,128]{1,0:T(8,128)(2,1)S(1)}, u32[]{:S(2)}, u32[]{:S(2)}) %collective-permute-start.5) | collective-permute-done | bytes 32800 | tf_op jit(solution)/shard_map/ppermute | solution.py:370
  18.5 1.0 %collective-permute-start.6 = (bf16[136,128]{1,0:T(8,128)(2,1)S(1)}, bf16[136,128]{1,0:T(8,128)(2,1)S(1)}, u32[]{:S(2)}, u32[]{:S(2)}) collective-permute-start(bf16[136,128]{1,0:T(8,128)(2,1)S(1)} %pair.1), channel_id=1, source_target_pairs={{0,2},{1,3},{2,0},{3,1},{4,6},{5,7},{6,4},{7,5},{8,10},{9,11},{10,... | collective-permute-start | bytes 104456 | tf_op jit(solution)/shard_map/ppermute | solution.py:370
  19.6 3.0 %collective-permute-done.6 = bf16[136,128]{1,0:T(8,128)(2,1)S(1)} collective-permute-done((bf16[136,128]{1,0:T(8,128)(2,1)S(1)}, bf16[136,128]{1,0:T(8,128)(2,1)S(1)}, u32[]{:S(2)}, u32[]{:S(2)}) %collective-permute-start.6) | collective-permute-done | bytes 34848 | tf_op jit(solution)/shard_map/ppermute | solution.py:370
  22.5 2.4 %collective-permute-start.9 = (bf16[136,128]{1,0:T(8,128)(2,1)S(1)}, bf16[136,128]{1,0:T(8,128)(2,1)S(1)}, u32[]{:S(2)}, u32[]{:S(2)}) collective-permute-start(bf16[136,128]{1,0:T(8,128)(2,1)S(1)} %add_convert_fusion.refs_0_), channel_id=1, source_target_pairs={{0,8},{1,9},{2,10},{3,11},{4,12},{5,13},{6,14},{7,15},{8,0},{9,1},... | collective-permute-start | bytes 104456 | tf_op jit(solution)/shard_map/ppermute | solution.py:370
  25.0 1.3 %collective-permute-start.8 = (bf16[136,128]{1,0:T(8,128)(2,1)S(1)}, bf16[136,128]{1,0:T(8,128)(2,1)S(1)}, u32[]{:S(2)}, u32[]{:S(2)}) collective-permute-start(bf16[136,128]{1,0:T(8,128)(2,1)S(1)} %add_convert_fusion.refs_0_), channel_id=1, source_target_pairs={{0,12},{1,13},{2,14},{3,15},{4,8},{5,9},{6,10},{7,11},{8,4},{9,5},... | collective-permute-start | bytes 104456 | tf_op jit(solution)/shard_map/ppermute | solution.py:370
  27.4 3.3 %collective-permute-done.8.refs_2_ = bf16[136,128]{1,0:T(8,128)(2,1)S(1)} collective-permute-done((bf16[136,128]{1,0:T(8,128)(2,1)S(1)}, bf16[136,128]{1,0:T(8,128)(2,1)S(1)}, u32[]{:S(2)}, u32[]{:S(2)}) %collective-permute-start.8) | collective-permute-done | bytes 34848 | tf_op jit(solution)/shard_map/ppermute | solution.py:370
  31.0 0.7 %scales.1 = (f32[128,1536]{1,0:T(8,128)S(1)}, f32[128,1536]{1,0:T(8,128)S(1)}) custom-call(f32[128,1536]{1,0:T(8,128)S(1)} %get-tuple-element.53.forward_ref, f32[128,1536]{1,0:T(8,128)S(1)} %get-tuple-element.54.annuity_ref, s32[12,128]{1,0:T(8,128)S(1)} %get-tuple-element.44.kind_ref, f32[12,128]{1,0:T(8,128)S(1)} %get-tuple-element.45.notional_ref, ...), custom_call_target="tpu_custom_call" | custom-call | flops 400000000 | bytes 4000000 | tf_op jit(solution)/shard_map/scales/pallas_call | solution.py:354
  32.2 1.2 %adjoint.1 = (bf16[512,128]{1,0:T(8,128)(2,1)S(1)}, bf16[128,1536]{1,0:T(8,128)(2,1)S(1)}, bf16[128,1536]{1,0:T(8,128)(2,1)S(1)}) custom-call(bf16[512,128]{1,0:T(8,128)(2,1)S(1)} %collective-permute-done.4.curves.partner, bf16[128,128]{1,0:T(8,128)(2,1)S(1)} %get-tuple-element.52.cots_mine, bf16[128,128]{1,0:T(8,128)(2,1)S(1)} %collective-permute-done.11.cots_partner, ...), custom_call_target="tpu_custom_call" | custom-call | flops 1000000 | bytes 1000000 | tf_op jit(solution)/shard_map/adjoint/pallas_call | solution.py:354
  33.7 1.0 %keep.1.kept = f32[512,128]{1,0:T(8,128)S(1)} custom-call(bf16[512,128]{1,0:T(8,128)(2,1)S(1)} %join.1.curves.mine, bf16[128,1536]{1,0:T(8,128)(2,1)S(1)} %get-tuple-element.57.fwd_cots, bf16[128,1536]{1,0:T(8,128)(2,1)S(1)} %get-tuple-element.58.ann_cots, bf16[1024,1536]{1,0:T(8,128)(2,1)S(1)} %get-tuple-element.38.w_fwd, ...), custom_call_target="tpu_custom_call" | custom-call | flops 200000000 | bytes 4000000 | tf_op jit(solution)/shard_map/keep/pallas_call | solution.py:354
  35.3 1.0 %collective-permute-start.14 = (bf16[128,128]{1,0:T(8,128)(2,1)S(1)}, bf16[128,128]{1,0:T(8,128)(2,1)S(1)}, u32[]{:S(2)}, u32[]{:S(2)}) collective-permute-start(bf16[128,128]{1,0:T(8,128)(2,1)S(1)} %get-tuple-element.62), channel_id=1, source_target_pairs={{0,2},{1,3},{2,0},{3,1},{4,6},{5,7},{6,4},{7,5},{8,10},{9,11},{10,... | collective-permute-start | bytes 98312 | tf_op jit(solution)/shard_map/ppermute | solution.py:370
  36.4 2.0 %collective-permute-start.15 = (bf16[128,128]{1,0:T(8,128)(2,1)S(1)}, bf16[128,128]{1,0:T(8,128)(2,1)S(1)}, u32[]{:S(2)}, u32[]{:S(2)}) collective-permute-start(bf16[128,128]{1,0:T(8,128)(2,1)S(1)} %get-tuple-element.63), channel_id=1, source_target_pairs={{0,4},{1,5},{2,6},{3,7},{4,0},{5,1},{6,2},{7,3},{8,12},{9,13},{10,... | collective-permute-start | bytes 98312 | tf_op jit(solution)/shard_map/ppermute | solution.py:370
  38.4 1.5 %collective-permute-start.10 = (f32[16]{0:T(128)S(1)}, f32[16]{0:T(128)S(1)}, u32[]{:S(2)}, u32[]{:S(2)}) collective-permute-start(f32[16]{0:T(128)S(1)} %bitcast.16), channel_id=1, source_target_pairs={{0,16},{16,0},{1,17},{17,1},{2,18},{18,2},{3,19},{19,3},{4,20},{20... | collective-permute-start | bytes 200 | tf_op jit(solution)/shard_map/ppermute | solution.py:389
  40.3 2.6 %collective-permute-start.16 = (bf16[64,128]{1,0:T(8,128)(2,1)S(1)}, bf16[64,128]{1,0:T(8,128)(2,1)S(1)}, u32[]{:S(2)}, u32[]{:S(2)}) collective-permute-start(bf16[64,128]{1,0:T(8,128)(2,1)S(1)} %get-tuple-element.65), channel_id=1, source_target_pairs={{0,8},{1,9},{2,10},{3,11},{4,12},{5,13},{6,14},{7,15},{8,0},{9,1},... | collective-permute-start | bytes 49160 | tf_op jit(solution)/shard_map/ppermute | solution.py:370
  43.5 1.5 %collective-permute-done.16.arrived = bf16[64,128]{1,0:T(8,128)(2,1)S(1)} collective-permute-done((bf16[64,128]{1,0:T(8,128)(2,1)S(1)}, bf16[64,128]{1,0:T(8,128)(2,1)S(1)}, u32[]{:S(2)}, u32[]{:S(2)}) %collective-permute-start.16) | collective-permute-done | bytes 16416 | tf_op jit(solution)/shard_map/ppermute | solution.py:370
  45.0 0.8 %factors.1 = f32[128,128]{1,0:T(8,128)} custom-call(f32[64,128]{1,0:T(8,128)S(1)} %get-tuple-element.64.kept, bf16[64,128]{1,0:T(8,128)(2,1)S(1)} %collective-permute-done.16.arrived, bf16[128,64]{1,0:T(8,128)(2,1)S(1)} %get-tuple-element.36.basis), custom_call_target="tpu_custom_call" | custom-call | flops 1000000 | bytes 1000000 | tf_op jit(solution)/shard_map/factors/pallas_call | solution.py:354
  (27 shorter events, 5.4 us)
Async XLA Ops:
  0.6 6.6 %collective-permute-start = (bf16[128,128]{1,0:T(8,128)(2,1)}, bf16[128,128]{1,0:T(8,128)(2,1)S(1)}, u32[]{:S(2)}, u32[]{:S(2)}) collective-permute-start(bf16[128,128]{1,0:T(8,128)(2,1)} %bitcast.18), channel_id=1, source_target_pairs={{0,8},{1,9},{2,10},{3,11},{4,12},{5,13},{6,14},{7,15},{8,0},{9,1},... | collective-permute-start | bytes 98312 | tf_op jit(solution)/shard_map/ppermute | solution.py:370
  7.4 6.3 %collective-permute-start.3 = (bf16[128,128]{1,0:T(8,128)(2,1)S(1)}, bf16[128,128]{1,0:T(8,128)(2,1)S(1)}, u32[]{:S(2)}, u32[]{:S(2)}) collective-permute-start(bf16[128,128]{1,0:T(8,128)(2,1)S(1)} %curves2.1.refs_8_.refs_0_), channel_id=1, source_target_pairs={{0,6},{1,7},{2,4},{3,5},{4,2},{5,3},{6,0},{7,1},{8,14},{9,15},{10,... | collective-permute-start | bytes 98312 | tf_op jit(solution)/shard_map/ppermute | solution.py:370
  9.9 3.9 %collective-permute-start.2 = (bf16[128,128]{1,0:T(8,128)(2,1)S(1)}, bf16[128,128]{1,0:T(8,128)(2,1)S(1)}, u32[]{:S(2)}, u32[]{:S(2)}) collective-permute-start(bf16[128,128]{1,0:T(8,128)(2,1)S(1)} %curves2.1.refs_8_.refs_0_), channel_id=1, source_target_pairs={{0,4},{1,5},{2,6},{3,7},{4,0},{5,1},{6,2},{7,3},{8,12},{9,13},{10,... | collective-permute-start | bytes 98312 | tf_op jit(solution)/shard_map/ppermute | solution.py:370
  10.6 3.9 %collective-permute-start.1 = (bf16[128,128]{1,0:T(8,128)(2,1)S(1)}, bf16[128,128]{1,0:T(8,128)(2,1)S(1)}, u32[]{:S(2)}, u32[]{:S(2)}) collective-permute-start(bf16[128,128]{1,0:T(8,128)(2,1)S(1)} %curves2.1.refs_8_.refs_0_), channel_id=1, source_target_pairs={{0,2},{1,3},{2,0},{3,1},{4,6},{5,7},{6,4},{7,5},{8,10},{9,11},{10,... | collective-permute-start | bytes 98312 | tf_op jit(solution)/shard_map/ppermute | solution.py:370
  14.5 1.4 %collective-permute-start.4 = (bf16[512,128]{1,0:T(8,128)(2,1)S(1)}, bf16[512,128]{1,0:T(8,128)(2,1)S(1)}, u32[]{:S(2)}, u32[]{:S(2)}) collective-permute-start(bf16[512,128]{1,0:T(8,128)(2,1)S(1)} %join.1.curves.mine), channel_id=1, source_target_pairs={{0,1},{1,0},{2,3},{3,2},{4,5},{5,4},{6,7},{7,6},{8,9},{9,8},{10,11... | collective-permute-start | bytes 393224 | tf_op jit(solution)/shard_map/ppermute | solution.py:370
  17.2 1.3 %collective-permute-start.5 = (bf16[128,128]{1,0:T(8,128)(2,1)S(1)}, bf16[128,128]{1,0:T(8,128)(2,1)S(1)}, u32[]{:S(2)}, u32[]{:S(2)}) collective-permute-start(bf16[128,128]{1,0:T(8,128)(2,1)S(1)} %get-tuple-element.49), channel_id=1, source_target_pairs={{0,1},{1,0},{2,3},{3,2},{4,5},{5,4},{6,7},{7,6},{8,9},{9,8},{10,11... | collective-permute-start | bytes 98312 | tf_op jit(solution)/shard_map/ppermute | solution.py:370
  18.5 4.0 %collective-permute-start.6 = (bf16[136,128]{1,0:T(8,128)(2,1)S(1)}, bf16[136,128]{1,0:T(8,128)(2,1)S(1)}, u32[]{:S(2)}, u32[]{:S(2)}) collective-permute-start(bf16[136,128]{1,0:T(8,128)(2,1)S(1)} %pair.1), channel_id=1, source_target_pairs={{0,2},{1,3},{2,0},{3,1},{4,6},{5,7},{6,4},{7,5},{8,10},{9,11},{10,... | collective-permute-start | bytes 104456 | tf_op jit(solution)/shard_map/ppermute | solution.py:370
  22.5 4.9 %collective-permute-start.9 = (bf16[136,128]{1,0:T(8,128)(2,1)S(1)}, bf16[136,128]{1,0:T(8,128)(2,1)S(1)}, u32[]{:S(2)}, u32[]{:S(2)}) collective-permute-start(bf16[136,128]{1,0:T(8,128)(2,1)S(1)} %add_convert_fusion.refs_0_), channel_id=1, source_target_pairs={{0,8},{1,9},{2,10},{3,11},{4,12},{5,13},{6,14},{7,15},{8,0},{9,1},... | collective-permute-start | bytes 104456 | tf_op jit(solution)/shard_map/ppermute | solution.py:370
  25.0 5.7 %collective-permute-start.8 = (bf16[136,128]{1,0:T(8,128)(2,1)S(1)}, bf16[136,128]{1,0:T(8,128)(2,1)S(1)}, u32[]{:S(2)}, u32[]{:S(2)}) collective-permute-start(bf16[136,128]{1,0:T(8,128)(2,1)S(1)} %add_convert_fusion.refs_0_), channel_id=1, source_target_pairs={{0,12},{1,13},{2,14},{3,15},{4,8},{5,9},{6,10},{7,11},{8,4},{9,5},... | collective-permute-start | bytes 104456 | tf_op jit(solution)/shard_map/ppermute | solution.py:370
  26.3 4.4 %collective-permute-start.7 = (bf16[136,128]{1,0:T(8,128)(2,1)S(1)}, bf16[136,128]{1,0:T(8,128)(2,1)S(1)}, u32[]{:S(2)}, u32[]{:S(2)}) collective-permute-start(bf16[136,128]{1,0:T(8,128)(2,1)S(1)} %add_convert_fusion.refs_0_), channel_id=1, source_target_pairs={{0,4},{1,5},{2,6},{3,7},{4,0},{5,1},{6,2},{7,3},{8,12},{9,13},{10,... | collective-permute-start | bytes 104456 | tf_op jit(solution)/shard_map/ppermute | solution.py:370
  30.9 1.3 %collective-permute-start.11 = (bf16[128,128]{1,0:T(8,128)(2,1)S(1)}, bf16[128,128]{1,0:T(8,128)(2,1)S(1)}, u32[]{:S(2)}, u32[]{:S(2)}) collective-permute-start(bf16[128,128]{1,0:T(8,128)(2,1)S(1)} %get-tuple-element.52.cots_mine), channel_id=1, source_target_pairs={{0,1},{1,0},{2,3},{3,2},{4,5},{5,4},{6,7},{7,6},{8,9},{9,8},{10,11... | collective-permute-start | bytes 98312 | tf_op jit(solution)/shard_map/ppermute | solution.py:370
  33.4 1.4 %collective-permute-start.12 = (bf16[512,128]{1,0:T(8,128)(2,1)S(1)}, bf16[512,128]{1,0:T(8,128)(2,1)S(1)}, u32[]{:S(2)}, u32[]{:S(2)}) collective-permute-start(bf16[512,128]{1,0:T(8,128)(2,1)S(1)} %get-tuple-element.59), channel_id=1, source_target_pairs={{0,1},{1,0},{2,3},{3,2},{4,5},{5,4},{6,7},{7,6},{8,9},{9,8},{10,11... | collective-permute-start | bytes 393224 | tf_op jit(solution)/shard_map/ppermute | solution.py:370
  34.9 5.1 %collective-permute-start.13 = (bf16[128,128]{1,0:T(8,128)(2,1)S(1)}, bf16[128,128]{1,0:T(8,128)(2,1)S(1)}, u32[]{:S(2)}, u32[]{:S(2)}) collective-permute-start(bf16[128,128]{1,0:T(8,128)(2,1)S(1)} %get-tuple-element.61), channel_id=1, source_target_pairs={{0,6},{1,7},{2,4},{3,5},{4,2},{5,3},{6,0},{7,1},{8,14},{9,15},{10,... | collective-permute-start | bytes 98312 | tf_op jit(solution)/shard_map/ppermute | solution.py:370
  35.3 4.6 %collective-permute-start.14 = (bf16[128,128]{1,0:T(8,128)(2,1)S(1)}, bf16[128,128]{1,0:T(8,128)(2,1)S(1)}, u32[]{:S(2)}, u32[]{:S(2)}) collective-permute-start(bf16[128,128]{1,0:T(8,128)(2,1)S(1)} %get-tuple-element.62), channel_id=1, source_target_pairs={{0,2},{1,3},{2,0},{3,1},{4,6},{5,7},{6,4},{7,5},{8,10},{9,11},{10,... | collective-permute-start | bytes 98312 | tf_op jit(solution)/shard_map/ppermute | solution.py:370
  36.4 3.9 %collective-permute-start.15 = (bf16[128,128]{1,0:T(8,128)(2,1)S(1)}, bf16[128,128]{1,0:T(8,128)(2,1)S(1)}, u32[]{:S(2)}, u32[]{:S(2)}) collective-permute-start(bf16[128,128]{1,0:T(8,128)(2,1)S(1)} %get-tuple-element.63), channel_id=1, source_target_pairs={{0,4},{1,5},{2,6},{3,7},{4,0},{5,1},{6,2},{7,3},{8,12},{9,13},{10,... | collective-permute-start | bytes 98312 | tf_op jit(solution)/shard_map/ppermute | solution.py:370
  38.4 4.6 %collective-permute-start.10 = (f32[16]{0:T(128)S(1)}, f32[16]{0:T(128)S(1)}, u32[]{:S(2)}, u32[]{:S(2)}) collective-permute-start(f32[16]{0:T(128)S(1)} %bitcast.16), channel_id=1, source_target_pairs={{0,16},{16,0},{1,17},{17,1},{2,18},{18,2},{3,19},{19,3},{4,20},{20... | collective-permute-start | bytes 200 | tf_op jit(solution)/shard_map/ppermute | solution.py:389
  40.3 4.7 %collective-permute-start.16 = (bf16[64,128]{1,0:T(8,128)(2,1)S(1)}, bf16[64,128]{1,0:T(8,128)(2,1)S(1)}, u32[]{:S(2)}, u32[]{:S(2)}) collective-permute-start(bf16[64,128]{1,0:T(8,128)(2,1)S(1)} %get-tuple-element.65), channel_id=1, source_target_pairs={{0,8},{1,9},{2,10},{3,11},{4,12},{5,13},{6,14},{7,15},{8,0},{9,1},... | collective-permute-start | bytes 49160 | tf_op jit(solution)/shard_map/ppermute | solution.py:370

commit v10 on v9

--- a/solution.py
+++ b/solution.py
@@ -13,7 +13,7 @@
 NT = (((1,), (1,)), ((), ()))
 TN = (((0,), (0,)), ((), ()))
 LANES = 128
-TILE = 768
+TILE = 1536
 VMEM = pl.BlockSpec(memory_space=pltpu.VMEM)
 HBM = pl.BlockSpec(memory_space=pltpu.HBM)
 VMEM_LIMIT = 8 * 2**20

time: 46.1 us -> 46 us (level)
  no operation moved by 1% of the time
where the time goes in v10:
time: 46 us; the launch traced here: 45.8 us
  starting transfers between devices  21.2 us (46%)
  waiting for transfers between devices  12.8 us (28%)
  Pallas kernels  10.5 us (23%)
  between operations  0.75 us (2%)
  other arithmetic  0.53 us (1%)
    ppermute x16, starting transfers between devices, swap(): return lax.ppermute(x, 'trade', [(i, i ^ mask) for i in range(n)])  19.7 us
    ppermute x16, waiting for transfers between devices, swap(): return lax.ppermute(x, 'trade', [(i, i ^ mask) for i in range(n)])  12.8 us
    pallas_call x15, Pallas kernels, run(): pl.pallas_call(kernel, in_specs=spaces, out_specs=jax.tree.map(lambda _:...  10.5 us
    ppermute x1, starting transfers between devices, sum_over(): lax.ppermute(x, axis, [(i, (i + shift) % n) for i in range(n)])  1.49 us
  transfers between devices with their start and end apart: 17, of which 13 were waited for; matrix products, arithmetic and copies ran while one was open for 1% of the time, Pallas kernels for 15%

profile of v10, /device:TPU:0, one launch (start us, length us, event | category | flops | bytes accessed | tf_op | source)
XLA Modules:
  0.0 45.8 jit_solution(16251062189573308266)
XLA Ops:
  0.6 4.1 %collective-permute-start = (bf16[128,128]{1,0:T(8,128)(2,1)}, bf16[128,128]{1,0:T(8,128)(2,1)S(1)}, u32[]{:S(2)}, u32[]{:S(2)}) collective-permute-start(bf16[128,128]{1,0:T(8,128)(2,1)} %bitcast.18), channel_id=1, source_target_pairs={{0,8},{1,9},{2,10},{3,11},{4,12},{5,13},{6,14},{7,15},{8,0},{9,1},... | collective-permute-start | bytes 98312 | tf_op jit(solution)/shard_map/ppermute | solution.py:370
  4.8 1.2 %curves.1 = (bf16[64,128]{1,0:T(8,128)(2,1)S(1)}, bf16[128,64]{1,0:T(8,128)(2,1)S(1)}, f32[2,16]{1,0:T(2,128)S(1)}, bf16[8,128]{1,0:T(8,128)(2,1)S(1)}) custom-call(bf16[128,128]{1,0:T(8,128)(2,1)} %bitcast.19, bf16[16,32]{1,0:T(8,128)(2,1)} %bitcast.20, f32[2,16]{1,0:T(2,128)} %bitcast.21), custom_call_target="tpu_custom_call" | custom-call | flops 1000000 | bytes 1000000 | tf_op jit(solution)/shard_map/curves/pallas_call | solution.py:354
  6.0 1.2 %collective-permute-done.arrived = bf16[128,128]{1,0:T(8,128)(2,1)S(1)} collective-permute-done((bf16[128,128]{1,0:T(8,128)(2,1)}, bf16[128,128]{1,0:T(8,128)(2,1)S(1)}, u32[]{:S(2)}, u32[]{:S(2)}) %collective-permute-start) | collective-permute-done | bytes 32800 | tf_op jit(solution)/shard_map/ppermute | solution.py:370
  7.4 2.5 %collective-permute-start.3 = (bf16[128,128]{1,0:T(8,128)(2,1)S(1)}, bf16[128,128]{1,0:T(8,128)(2,1)S(1)}, u32[]{:S(2)}, u32[]{:S(2)}) collective-permute-start(bf16[128,128]{1,0:T(8,128)(2,1)S(1)} %curves2.1.refs_8_.refs_0_), channel_id=1, source_target_pairs={{0,6},{1,7},{2,4},{3,5},{4,2},{5,3},{6,0},{7,1},{8,14},{9,15},{10,... | collective-permute-start | bytes 98312 | tf_op jit(solution)/shard_map/ppermute | solution.py:370
  9.9 0.7 %collective-permute-start.2 = (bf16[128,128]{1,0:T(8,128)(2,1)S(1)}, bf16[128,128]{1,0:T(8,128)(2,1)S(1)}, u32[]{:S(2)}, u32[]{:S(2)}) collective-permute-start(bf16[128,128]{1,0:T(8,128)(2,1)S(1)} %curves2.1.refs_8_.refs_0_), channel_id=1, source_target_pairs={{0,4},{1,5},{2,6},{3,7},{4,0},{5,1},{6,2},{7,3},{8,12},{9,13},{10,... | collective-permute-start | bytes 98312 | tf_op jit(solution)/shard_map/ppermute | solution.py:370
  10.9 2.8 %prep.1 = (bf16[1024,1536]{1,0:T(8,128)(2,1)S(1)}, bf16[1024,1536]{1,0:T(8,128)(2,1)S(1)}, bf16[1024,1536]{1,0:T(8,128)(2,1)S(1)}, bf16[256,1536]{1,0:T(8,128)(2...) custom-call(s32[2,1536]{1,0:T(2,128)} %refs_0_.1, ...), custom_call_target="tpu_custom_call" | custom-call | flops 400000000 | bytes 8000000 | tf_op jit(solution)/shard_map/prep/pallas_call | solution.py:354
  13.8 0.7 %collective-permute-done.1.refs_1_ = bf16[128,128]{1,0:T(8,128)(2,1)S(1)} collective-permute-done((bf16[128,128]{1,0:T(8,128)(2,1)S(1)}, bf16[128,128]{1,0:T(8,128)(2,1)S(1)}, u32[]{:S(2)}, u32[]{:S(2)}) %collective-permute-start.1) | collective-permute-done | bytes 32800 | tf_op jit(solution)/shard_map/ppermute | solution.py:370
  14.6 0.8 %price1.1 = (f32[128,1536]{1,0:T(8,128)S(1)}, f32[128,1536]{1,0:T(8,128)S(1)}) custom-call(bf16[512,128]{1,0:T(8,128)(2,1)S(1)} %join.1.curves.mine, bf16[1024,1536]{1,0:T(8,128)(2,1)S(1)} %get-tuple-element.38.w_fwd, bf16[1024,1536]{1,0:T(8,128)(2,1)S(1)} %get-tuple-element.39.w_low, bf16[1024,1536]{1,0:T(8,128)(2,1)S(1)} %get-tuple-element.40.w_disc), custom_call_target="tpu_custom_call" | custom-call | flops 400000000 | bytes 4000000 | tf_op jit(solution)/shard_map/price1/pallas_call | solution.py:354
  15.9 1.3 %price2.1 = (bf16[128,128]{1,0:T(8,128)(2,1)S(1)}, bf16[128,1536]{1,0:T(8,128)(2,1)S(1)}, f32[128,1536]{1,0:T(8,128)S(1)}, f32[128,1536]{1,0:T(8,128)S(1)}) custom-call(bf16[512,128]{1,0:T(8,128)(2,1)S(1)} %collective-permute-done.4.curves.partner, f32[128,1536]{1,0:T(8,128)S(1)} %get-tuple-element.41.forward_ref, ...), custom_call_target="tpu_custom_call" | custom-call | flops 1000000 | bytes 1000000 | tf_op jit(solution)/shard_map/price2/pallas_call | solution.py:354
  17.7 0.8 %collective-permute-done.5.arrived = bf16[128,128]{1,0:T(8,128)(2,1)S(1)} collective-permute-done((bf16[128,128]{1,0:T(8,128)(2,1)S(1)}, bf16[128,128]{1,0:T(8,128)(2,1)S(1)}, u32[]{:S(2)}, u32[]{:S(2)}) %collective-permute-start.5) | collective-permute-done | bytes 32800 | tf_op jit(solution)/shard_map/ppermute | solution.py:370
  18.5 1.0 %collective-permute-start.6 = (bf16[136,128]{1,0:T(8,128)(2,1)S(1)}, bf16[136,128]{1,0:T(8,128)(2,1)S(1)}, u32[]{:S(2)}, u32[]{:S(2)}) collective-permute-start(bf16[136,128]{1,0:T(8,128)(2,1)S(1)} %pair.1), channel_id=1, source_target_pairs={{0,2},{1,3},{2,0},{3,1},{4,6},{5,7},{6,4},{7,5},{8,10},{9,11},{10,... | collective-permute-start | bytes 104456 | tf_op jit(solution)/shard_map/ppermute | solution.py:370
  19.5 3.0 %collective-permute-done.6 = bf16[136,128]{1,0:T(8,128)(2,1)S(1)} collective-permute-done((bf16[136,128]{1,0:T(8,128)(2,1)S(1)}, bf16[136,128]{1,0:T(8,128)(2,1)S(1)}, u32[]{:S(2)}, u32[]{:S(2)}) %collective-permute-start.6) | collective-permute-done | bytes 34848 | tf_op jit(solution)/shard_map/ppermute | solution.py:370
  22.5 2.4 %collective-permute-start.9 = (bf16[136,128]{1,0:T(8,128)(2,1)S(1)}, bf16[136,128]{1,0:T(8,128)(2,1)S(1)}, u32[]{:S(2)}, u32[]{:S(2)}) collective-permute-start(bf16[136,128]{1,0:T(8,128)(2,1)S(1)} %add_convert_fusion.refs_0_), channel_id=1, source_target_pairs={{0,8},{1,9},{2,10},{3,11},{4,12},{5,13},{6,14},{7,15},{8,0},{9,1},... | collective-permute-start | bytes 104456 | tf_op jit(solution)/shard_map/ppermute | solution.py:370
  25.0 1.3 %collective-permute-start.8 = (bf16[136,128]{1,0:T(8,128)(2,1)S(1)}, bf16[136,128]{1,0:T(8,128)(2,1)S(1)}, u32[]{:S(2)}, u32[]{:S(2)}) collective-permute-start(bf16[136,128]{1,0:T(8,128)(2,1)S(1)} %add_convert_fusion.refs_0_), channel_id=1, source_target_pairs={{0,12},{1,13},{2,14},{3,15},{4,8},{5,9},{6,10},{7,11},{8,4},{9,5},... | collective-permute-start | bytes 104456 | tf_op jit(solution)/shard_map/ppermute | solution.py:370
  27.4 3.3 %collective-permute-done.8.refs_2_ = bf16[136,128]{1,0:T(8,128)(2,1)S(1)} collective-permute-done((bf16[136,128]{1,0:T(8,128)(2,1)S(1)}, bf16[136,128]{1,0:T(8,128)(2,1)S(1)}, u32[]{:S(2)}, u32[]{:S(2)}) %collective-permute-start.8) | collective-permute-done | bytes 34848 | tf_op jit(solution)/shard_map/ppermute | solution.py:370
  31.0 0.7 %scales.1 = (f32[128,1536]{1,0:T(8,128)S(1)}, f32[128,1536]{1,0:T(8,128)S(1)}) custom-call(f32[128,1536]{1,0:T(8,128)S(1)} %get-tuple-element.53.forward_ref, f32[128,1536]{1,0:T(8,128)S(1)} %get-tuple-element.54.annuity_ref, s32[12,128]{1,0:T(8,128)S(1)} %get-tuple-element.44.kind_ref, f32[12,128]{1,0:T(8,128)S(1)} %get-tuple-element.45.notional_ref, ...), custom_call_target="tpu_custom_call" | custom-call | flops 400000000 | bytes 4000000 | tf_op jit(solution)/shard_map/scales/pallas_call | solution.py:354
  32.2 1.2 %adjoint.1 = (bf16[512,128]{1,0:T(8,128)(2,1)S(1)}, bf16[128,1536]{1,0:T(8,128)(2,1)S(1)}, bf16[128,1536]{1,0:T(8,128)(2,1)S(1)}) custom-call(bf16[512,128]{1,0:T(8,128)(2,1)S(1)} %collective-permute-done.4.curves.partner, bf16[128,128]{1,0:T(8,128)(2,1)S(1)} %get-tuple-element.52.cots_mine, bf16[128,128]{1,0:T(8,128)(2,1)S(1)} %collective-permute-done.11.cots_partner, ...), custom_call_target="tpu_custom_call" | custom-call | flops 1000000 | bytes 1000000 | tf_op jit(solution)/shard_map/adjoint/pallas_call | solution.py:354
  33.6 1.0 %keep.1.kept = f32[512,128]{1,0:T(8,128)S(1)} custom-call(bf16[512,128]{1,0:T(8,128)(2,1)S(1)} %join.1.curves.mine, bf16[128,1536]{1,0:T(8,128)(2,1)S(1)} %get-tuple-element.57.fwd_cots, bf16[128,1536]{1,0:T(8,128)(2,1)S(1)} %get-tuple-element.58.ann_cots, bf16[1024,1536]{1,0:T(8,128)(2,1)S(1)} %get-tuple-element.38.w_fwd, ...), custom_call_target="tpu_custom_call" | custom-call | flops 200000000 | bytes 4000000 | tf_op jit(solution)/shard_map/keep/pallas_call | solution.py:354
  35.3 1.1 %collective-permute-start.14 = (bf16[128,128]{1,0:T(8,128)(2,1)S(1)}, bf16[128,128]{1,0:T(8,128)(2,1)S(1)}, u32[]{:S(2)}, u32[]{:S(2)}) collective-permute-start(bf16[128,128]{1,0:T(8,128)(2,1)S(1)} %get-tuple-element.62), channel_id=1, source_target_pairs={{0,2},{1,3},{2,0},{3,1},{4,6},{5,7},{6,4},{7,5},{8,10},{9,11},{10,... | collective-permute-start | bytes 98312 | tf_op jit(solution)/shard_map/ppermute | solution.py:370
  36.3 2.0 %collective-permute-start.15 = (bf16[128,128]{1,0:T(8,128)(2,1)S(1)}, bf16[128,128]{1,0:T(8,128)(2,1)S(1)}, u32[]{:S(2)}, u32[]{:S(2)}) collective-permute-start(bf16[128,128]{1,0:T(8,128)(2,1)S(1)} %get-tuple-element.63), channel_id=1, source_target_pairs={{0,4},{1,5},{2,6},{3,7},{4,0},{5,1},{6,2},{7,3},{8,12},{9,13},{10,... | collective-permute-start | bytes 98312 | tf_op jit(solution)/shard_map/ppermute | solution.py:370
  38.3 1.5 %collective-permute-start.10 = (f32[16]{0:T(128)S(1)}, f32[16]{0:T(128)S(1)}, u32[]{:S(2)}, u32[]{:S(2)}) collective-permute-start(f32[16]{0:T(128)S(1)} %bitcast.16), channel_id=1, source_target_pairs={{0,16},{16,0},{1,17},{17,1},{2,18},{18,2},{3,19},{19,3},{4,20},{20... | collective-permute-start | bytes 200 | tf_op jit(solution)/shard_map/ppermute | solution.py:389
  40.3 2.6 %collective-permute-start.16 = (bf16[64,128]{1,0:T(8,128)(2,1)S(1)}, bf16[64,128]{1,0:T(8,128)(2,1)S(1)}, u32[]{:S(2)}, u32[]{:S(2)}) collective-permute-start(bf16[64,128]{1,0:T(8,128)(2,1)S(1)} %get-tuple-element.65), channel_id=1, source_target_pairs={{0,8},{1,9},{2,10},{3,11},{4,12},{5,13},{6,14},{7,15},{8,0},{9,1},... | collective-permute-start | bytes 49160 | tf_op jit(solution)/shard_map/ppermute | solution.py:370
  43.4 1.5 %collective-permute-done.16.arrived = bf16[64,128]{1,0:T(8,128)(2,1)S(1)} collective-permute-done((bf16[64,128]{1,0:T(8,128)(2,1)S(1)}, bf16[64,128]{1,0:T(8,128)(2,1)S(1)}, u32[]{:S(2)}, u32[]{:S(2)}) %collective-permute-start.16) | collective-permute-done | bytes 16416 | tf_op jit(solution)/shard_map/ppermute | solution.py:370
  45.0 0.8 %factors.1 = f32[128,128]{1,0:T(8,128)} custom-call(f32[64,128]{1,0:T(8,128)S(1)} %get-tuple-element.64.kept, bf16[64,128]{1,0:T(8,128)(2,1)S(1)} %collective-permute-done.16.arrived, bf16[128,64]{1,0:T(8,128)(2,1)S(1)} %get-tuple-element.36.basis), custom_call_target="tpu_custom_call" | custom-call | flops 1000000 | bytes 1000000 | tf_op jit(solution)/shard_map/factors/pallas_call | solution.py:354
  (27 shorter events, 5.4 us)
Async XLA Ops:
  0.6 6.6 %collective-permute-start = (bf16[128,128]{1,0:T(8,128)(2,1)}, bf16[128,128]{1,0:T(8,128)(2,1)S(1)}, u32[]{:S(2)}, u32[]{:S(2)}) collective-permute-start(bf16[128,128]{1,0:T(8,128)(2,1)} %bitcast.18), channel_id=1, source_target_pairs={{0,8},{1,9},{2,10},{3,11},{4,12},{5,13},{6,14},{7,15},{8,0},{9,1},... | collective-permute-start | bytes 98312 | tf_op jit(solution)/shard_map/ppermute | solution.py:370
  7.4 6.3 %collective-permute-start.3 = (bf16[128,128]{1,0:T(8,128)(2,1)S(1)}, bf16[128,128]{1,0:T(8,128)(2,1)S(1)}, u32[]{:S(2)}, u32[]{:S(2)}) collective-permute-start(bf16[128,128]{1,0:T(8,128)(2,1)S(1)} %curves2.1.refs_8_.refs_0_), channel_id=1, source_target_pairs={{0,6},{1,7},{2,4},{3,5},{4,2},{5,3},{6,0},{7,1},{8,14},{9,15},{10,... | collective-permute-start | bytes 98312 | tf_op jit(solution)/shard_map/ppermute | solution.py:370
  9.9 3.9 %collective-permute-start.2 = (bf16[128,128]{1,0:T(8,128)(2,1)S(1)}, bf16[128,128]{1,0:T(8,128)(2,1)S(1)}, u32[]{:S(2)}, u32[]{:S(2)}) collective-permute-start(bf16[128,128]{1,0:T(8,128)(2,1)S(1)} %curves2.1.refs_8_.refs_0_), channel_id=1, source_target_pairs={{0,4},{1,5},{2,6},{3,7},{4,0},{5,1},{6,2},{7,3},{8,12},{9,13},{10,... | collective-permute-start | bytes 98312 | tf_op jit(solution)/shard_map/ppermute | solution.py:370
  10.6 3.9 %collective-permute-start.1 = (bf16[128,128]{1,0:T(8,128)(2,1)S(1)}, bf16[128,128]{1,0:T(8,128)(2,1)S(1)}, u32[]{:S(2)}, u32[]{:S(2)}) collective-permute-start(bf16[128,128]{1,0:T(8,128)(2,1)S(1)} %curves2.1.refs_8_.refs_0_), channel_id=1, source_target_pairs={{0,2},{1,3},{2,0},{3,1},{4,6},{5,7},{6,4},{7,5},{8,10},{9,11},{10,... | collective-permute-start | bytes 98312 | tf_op jit(solution)/shard_map/ppermute | solution.py:370
  14.5 1.4 %collective-permute-start.4 = (bf16[512,128]{1,0:T(8,128)(2,1)S(1)}, bf16[512,128]{1,0:T(8,128)(2,1)S(1)}, u32[]{:S(2)}, u32[]{:S(2)}) collective-permute-start(bf16[512,128]{1,0:T(8,128)(2,1)S(1)} %join.1.curves.mine), channel_id=1, source_target_pairs={{0,1},{1,0},{2,3},{3,2},{4,5},{5,4},{6,7},{7,6},{8,9},{9,8},{10,11... | collective-permute-start | bytes 393224 | tf_op jit(solution)/shard_map/ppermute | solution.py:370
  17.2 1.3 %collective-permute-start.5 = (bf16[128,128]{1,0:T(8,128)(2,1)S(1)}, bf16[128,128]{1,0:T(8,128)(2,1)S(1)}, u32[]{:S(2)}, u32[]{:S(2)}) collective-permute-start(bf16[128,128]{1,0:T(8,128)(2,1)S(1)} %get-tuple-element.49), channel_id=1, source_target_pairs={{0,1},{1,0},{2,3},{3,2},{4,5},{5,4},{6,7},{7,6},{8,9},{9,8},{10,11... | collective-permute-start | bytes 98312 | tf_op jit(solution)/shard_map/ppermute | solution.py:370
  18.5 4.0 %collective-permute-start.6 = (bf16[136,128]{1,0:T(8,128)(2,1)S(1)}, bf16[136,128]{1,0:T(8,128)(2,1)S(1)}, u32[]{:S(2)}, u32[]{:S(2)}) collective-permute-start(bf16[136,128]{1,0:T(8,128)(2,1)S(1)} %pair.1), channel_id=1, source_target_pairs={{0,2},{1,3},{2,0},{3,1},{4,6},{5,7},{6,4},{7,5},{8,10},{9,11},{10,... | collective-permute-start | bytes 104456 | tf_op jit(solution)/shard_map/ppermute | solution.py:370
  22.5 4.9 %collective-permute-start.9 = (bf16[136,128]{1,0:T(8,128)(2,1)S(1)}, bf16[136,128]{1,0:T(8,128)(2,1)S(1)}, u32[]{:S(2)}, u32[]{:S(2)}) collective-permute-start(bf16[136,128]{1,0:T(8,128)(2,1)S(1)} %add_convert_fusion.refs_0_), channel_id=1, source_target_pairs={{0,8},{1,9},{2,10},{3,11},{4,12},{5,13},{6,14},{7,15},{8,0},{9,1},... | collective-permute-start | bytes 104456 | tf_op jit(solution)/shard_map/ppermute | solution.py:370
  25.0 5.7 %collective-permute-start.8 = (bf16[136,128]{1,0:T(8,128)(2,1)S(1)}, bf16[136,128]{1,0:T(8,128)(2,1)S(1)}, u32[]{:S(2)}, u32[]{:S(2)}) collective-permute-start(bf16[136,128]{1,0:T(8,128)(2,1)S(1)} %add_convert_fusion.refs_0_), channel_id=1, source_target_pairs={{0,12},{1,13},{2,14},{3,15},{4,8},{5,9},{6,10},{7,11},{8,4},{9,5},... | collective-permute-start | bytes 104456 | tf_op jit(solution)/shard_map/ppermute | solution.py:370
  26.3 4.4 %collective-permute-start.7 = (bf16[136,128]{1,0:T(8,128)(2,1)S(1)}, bf16[136,128]{1,0:T(8,128)(2,1)S(1)}, u32[]{:S(2)}, u32[]{:S(2)}) collective-permute-start(bf16[136,128]{1,0:T(8,128)(2,1)S(1)} %add_convert_fusion.refs_0_), channel_id=1, source_target_pairs={{0,4},{1,5},{2,6},{3,7},{4,0},{5,1},{6,2},{7,3},{8,12},{9,13},{10,... | collective-permute-start | bytes 104456 | tf_op jit(solution)/shard_map/ppermute | solution.py:370
  30.9 1.3 %collective-permute-start.11 = (bf16[128,128]{1,0:T(8,128)(2,1)S(1)}, bf16[128,128]{1,0:T(8,128)(2,1)S(1)}, u32[]{:S(2)}, u32[]{:S(2)}) collective-permute-start(bf16[128,128]{1,0:T(8,128)(2,1)S(1)} %get-tuple-element.52.cots_mine), channel_id=1, source_target_pairs={{0,1},{1,0},{2,3},{3,2},{4,5},{5,4},{6,7},{7,6},{8,9},{9,8},{10,11... | collective-permute-start | bytes 98312 | tf_op jit(solution)/shard_map/ppermute | solution.py:370
  33.4 1.4 %collective-permute-start.12 = (bf16[512,128]{1,0:T(8,128)(2,1)S(1)}, bf16[512,128]{1,0:T(8,128)(2,1)S(1)}, u32[]{:S(2)}, u32[]{:S(2)}) collective-permute-start(bf16[512,128]{1,0:T(8,128)(2,1)S(1)} %get-tuple-element.59), channel_id=1, source_target_pairs={{0,1},{1,0},{2,3},{3,2},{4,5},{5,4},{6,7},{7,6},{8,9},{9,8},{10,11... | collective-permute-start | bytes 393224 | tf_op jit(solution)/shard_map/ppermute | solution.py:370
  34.8 5.1 %collective-permute-start.13 = (bf16[128,128]{1,0:T(8,128)(2,1)S(1)}, bf16[128,128]{1,0:T(8,128)(2,1)S(1)}, u32[]{:S(2)}, u32[]{:S(2)}) collective-permute-start(bf16[128,128]{1,0:T(8,128)(2,1)S(1)} %get-tuple-element.61), channel_id=1, source_target_pairs={{0,6},{1,7},{2,4},{3,5},{4,2},{5,3},{6,0},{7,1},{8,14},{9,15},{10,... | collective-permute-start | bytes 98312 | tf_op jit(solution)/shard_map/ppermute | solution.py:370
  35.3 4.6 %collective-permute-start.14 = (bf16[128,128]{1,0:T(8,128)(2,1)S(1)}, bf16[128,128]{1,0:T(8,128)(2,1)S(1)}, u32[]{:S(2)}, u32[]{:S(2)}) collective-permute-start(bf16[128,128]{1,0:T(8,128)(2,1)S(1)} %get-tuple-element.62), channel_id=1, source_target_pairs={{0,2},{1,3},{2,0},{3,1},{4,6},{5,7},{6,4},{7,5},{8,10},{9,11},{10,... | collective-permute-start | bytes 98312 | tf_op jit(solution)/shard_map/ppermute | solution.py:370
  36.3 3.9 %collective-permute-start.15 = (bf16[128,128]{1,0:T(8,128)(2,1)S(1)}, bf16[128,128]{1,0:T(8,128)(2,1)S(1)}, u32[]{:S(2)}, u32[]{:S(2)}) collective-permute-start(bf16[128,128]{1,0:T(8,128)(2,1)S(1)} %get-tuple-element.63), channel_id=1, source_target_pairs={{0,4},{1,5},{2,6},{3,7},{4,0},{5,1},{6,2},{7,3},{8,12},{9,13},{10,... | collective-permute-start | bytes 98312 | tf_op jit(solution)/shard_map/ppermute | solution.py:370
  38.3 4.6 %collective-permute-start.10 = (f32[16]{0:T(128)S(1)}, f32[16]{0:T(128)S(1)}, u32[]{:S(2)}, u32[]{:S(2)}) collective-permute-start(f32[16]{0:T(128)S(1)} %bitcast.16), channel_id=1, source_target_pairs={{0,16},{16,0},{1,17},{17,1},{2,18},{18,2},{3,19},{19,3},{4,20},{20... | collective-permute-start | bytes 200 | tf_op jit(solution)/shard_map/ppermute | solution.py:389
  40.3 4.7 %collective-permute-start.16 = (bf16[64,128]{1,0:T(8,128)(2,1)S(1)}, bf16[64,128]{1,0:T(8,128)(2,1)S(1)}, u32[]{:S(2)}, u32[]{:S(2)}) collective-permute-start(bf16[64,128]{1,0:T(8,128)(2,1)S(1)} %get-tuple-element.65), channel_id=1, source_target_pairs={{0,8},{1,9},{2,10},{3,11},{4,12},{5,13},{6,14},{7,15},{8,0},{9,1},... | collective-permute-start | bytes 49160 | tf_op jit(solution)/shard_map/ppermute | solution.py:370
